TPU v7x, 512 devices: a whole 4x8x8 slice. The times are simulated.
512 devices in a mesh: gx: 4 (over x), rest: 128 (over y, z, core).
Axes of the slice: x: 4, y: 8, z: 8, core: 2. Of those that a mesh axis runs over, the one named last changes fastest.
Arguments:
- tensor: float32 [512, 672, 672], P('rest', 'gx'), as said below
- basis: float32 [672, 128], P('gx'), may hold values from -0.25 to 0.25
Outputs:
- gram_one: float32 [672, 672], P('gx')
- core: float32 [128, 512, 672], P('gx', 'rest')
- gram_two: float32 [672, 672], replicated
Inputs may be any that keep to these rules, and one draw needn't show every extreme that they name: `tensor`: Real-valued field samples.
All inputs are finite; a program needn't handle non-finite values.
Results may differ from a plain program's by a relative error of at most 0.000073.
Values sent between devices are 32-bit elements; how exact they have to be, the bound alone decides.
No kernel may reach another device: no remote copies, remote signals or barrier semaphores. Data moves between devices by JAX's collectives and lax.ppermute only.
A program may use at most 64 MiB of HBM per device.

v0:
```python
import jax
import jax.numpy as jnp
from jax import lax
from jax.sharding import PartitionSpec as P


def local(tensor, basis):
    highest = lax.Precision.HIGHEST
    slices_here = tensor.shape[0]
    rows_here = tensor.shape[1]
    second_width = tensor.shape[2]
    slices_all = slices_here * lax.axis_size("rest")
    rank_all = basis.shape[1]
    exchanged = lax.all_to_all(tensor, "gx", split_axis=2, concat_axis=1, tiled=True)
    local_gram = jnp.einsum("kic,kjc->ij", exchanged, exchanged, precision=highest)
    summed = lax.psum(local_gram, ("gx", "rest"))
    block_rows = lax.dynamic_slice_in_dim(summed, lax.axis_index("gx") * rows_here, rows_here, 0)
    gram_one = block_rows / (slices_all * second_width)
    core = lax.psum_scatter(
        jnp.einsum("ic,kij->ckj", basis, tensor, precision=highest),
        "gx",
        scatter_dimension=0,
        tiled=True,
    )
    core_flat = core.reshape(-1, second_width)
    local_two = jnp.dot(
        core_flat.T, core_flat, precision=highest, preferred_element_type=jnp.float32
    )
    gram_sum = lax.psum(local_two, ("gx", "rest"))
    gram_two = gram_sum / (slices_all * rank_all)
    return (gram_one, core, gram_two)


def solution(mesh):
    in_specs = (P("rest", "gx", None), P("gx", None))
    out_specs = (P("gx", None), P("gx", "rest", None), P())
    return jax.shard_map(local, mesh=mesh, in_specs=in_specs, out_specs=out_specs, check_vma=False)
```

profile of v0, /device:TPU:1, one launch (start us, length us, event | category | flops | bytes accessed | tf_op | source)
XLA Modules:
  0.0 384.4 jit_solution(14953553316876162083)
XLA Ops:
  7.2 0.0 copy-start
  7.2 0.0 reduce-scatter.2.cloned.1.call-start
  7.2 0.8 copy-done
  8.1 4.3 %fusion = f32[128,4,672]{2,0,1:T(8,128)} fusion(f32[4,168,672]{2,1,0:T(8,128)} %param.2, f32[168,128]{1,0:T(8,128)S(1)} %copy-done), kind=kOutput, calls=%fused_computation.5 | convolution fusion | flops 693633024 | bytes 3268608 | tf_op jit(solution)/shard_map/ic,kij->ckj/dot_general | solution.py:20
  12.3 0.0 reduce-scatter.2.cloned.1.call-update
  12.3 0.0 all-reduce.3.cloned.1.call-start
  12.4 3.2 copy.7
  15.6 45.6 %all_to_all.18 = f32[4,168,672]{1,0,2:T(4,128)S(1)} all-to-all(f32[4,168,672]{1,0,2:T(4,128)S(1)} %copy.7), channel_id=1, replica_groups=mesh['gx'=4,'rest'=128] {'gx'}, dimensions={2} | all-to-all | bytes 3612672 | tf_op jit(solution)/shard_map/all_to_all | solution.py:14
  61.2 1.8 copy.11
  63.0 2.9 all_to_all.16
  65.9 8.9 %convolution_bitcast_fusion.1 = f32[672,672]{1,0:T(8,128)} fusion(f32[4,672,168]{1,2,0:T(8,128)} %all_to_all.16), kind=kOutput, calls=%fused_computation.2 | convolution fusion | flops 3641573376 | bytes 3612672 | tf_op jit(solution)/shard_map/kic,kjc->ij/dot_general | solution.py:15
  74.8 0.0 reduce-scatter.2.cloned.1.call-done
  74.8 4.2 %convolution_bitcast_fusion = f32[672,672]{1,0:T(8,128)} fusion(f32[32,4,672]{2,0,1:T(8,128)} %reduce-scatter.2.cloned.1.call-done), kind=kOutput, calls=%fused_computation.1 | convolution fusion | flops 693633024 | bytes 2150400 | tf_op jit(solution)/shard_map/dot_general | solution.py:26
  79.0 0.0 copy-start.1
  79.0 0.0 all-reduce.3.cloned.1.call-update
  79.0 1.0 copy-done.1
  80.0 1.0 copy.9
  81.0 291.7 %all-reduce.3.cloned.1.call-done = (f32[672,672]{1,0:T(8,128)}, f32[672,672]{1,0:T(8,128)}) async-done(((f32[672,672]{1,0:T(8,128)}, f32[672,672]{1,0:T(8,128)}), (f32[672,672]{1,0:T(8,128)}, f32[672,672]{1,0:T(8,128)})) %all-reduce.3.cloned.1.call-update) | async-done | bytes 3612688 | tf_op jit(solution)/shard_map/psum | solution.py:16
  372.7 3.0 broadcast_multiply_fusion
  375.7 1.9 dynamic-slice_multiply_fusion
Async XLA Ops:
  7.2 0.9 copy-start
  7.2 67.6 %reduce-scatter.2.cloned.1.call-start = ((), (), s32[]{:S(2)}) async-start(), calls=%async_computation.2 | async-start | bytes 1966080 | tf_op jit(solution)/shard_map/reduce_scatter | solution.py:19
  12.3 360.4 %all-reduce.3.cloned.1.call-start = ((), (), s32[]{:S(2)}) async-start(), calls=%async_computation.3 | async-start | bytes 8257536 | tf_op jit(solution)/shard_map/psum | solution.py:16
  79.0 1.0 copy-start.1
Sparse Core Ops, SparseCore 0:
  12.5 54.6 reduce-scatter.1
  79.2 293.5 all-reduce.2
where the time goes:
time: 386 us; the launch traced here: 384 us
  waiting for transfers between devices  292 us (76%)
  blocking collectives  45.6 us (12%)
  matrix products  17.4 us (5%)
  between operations  14.1 us (4%)
  local copies, waits for them, and re-layouts  10.7 us (3%)
  other arithmetic  4.89 us (1%)
    psum x1, waiting for transfers between devices, local(): summed = lax.psum(local_gram, ('gx', 'rest'))  292 us
    all_to_all x1, blocking collectives, local(): lax.all_to_all(tensor, 'gx', split_axis=2, concat_axis=1, tiled=True)  45.6 us
    dot_general x1, matrix products, local(): jnp.einsum('kic,kjc->ij', exchanged, exchanged, precision=highest)  8.86 us
  transfers between devices with their start and end apart: 2, of which 1 were waited for; matrix products, arithmetic and copies ran while one was open for 4% of the time, Pallas kernels for 0%

commit v1 on v0

v1 whole, which is shorter than its diff:
```python
import functools

import jax
import jax.numpy as jnp
from jax import lax
from jax.experimental import pallas as pl
from jax.experimental.pallas import tpu as pltpu
from jax.sharding import Mesh, PartitionSpec as P

LANES = 128


def triangle(width):
    full = width // LANES
    left = width - full * LANES
    offsets, row = [], 0
    for block in range(full):
        offsets.append(row)
        row += (block + 1) * LANES
    tail = row
    row += left * (full + 1)
    return full, left, offsets, tail, row


def halves(value):
    high = value.astype(jnp.bfloat16)
    low = (value - high.astype(jnp.float32)).astype(jnp.bfloat16)
    return high, low


def product(left_high, left_low, right_high, right_low):
    def one(a, b):
        return lax.dot_general(a, b, (((1,), (1,)), ((), ())), preferred_element_type=jnp.float32)

    return one(left_high, right_high) + (one(left_high, right_low) + one(left_low, right_high))


def pack_gram(high_ref, low_ref, out_ref, base, width):
    full, left, offsets, tail, _ = triangle(width)
    for block in range(full):
        rows = (block + 1) * LANES
        mine = pl.ds(block * LANES, LANES)
        out_ref[pl.ds(base + offsets[block], rows), :] = product(
            high_ref[pl.ds(0, rows), :], low_ref[pl.ds(0, rows), :], high_ref[mine, :], low_ref[mine, :]
        )
    last = pl.ds(full * LANES, left)
    strip = product(high_ref[last, :], low_ref[last, :], high_ref[...], low_ref[...])
    for block in range(full):
        out_ref[pl.ds(base + tail + block * left, left), :] = strip[:, block * LANES : (block + 1) * LANES]
    corner = pl.ds(base + tail + full * left, left)
    out_ref[corner, :] = jnp.zeros((left, LANES), jnp.float32)
    out_ref[corner, 0:left] = strip[:, full * LANES :]


def gram_kernel(field_ref, basis_ref, packed_ref, core_ref, field_high, field_low, core_high, core_low):
    first, second = field_ref.shape
    rows_one = triangle(first)[-1]
    rows_two = triangle(second)[-1]
    high, low = halves(field_ref[...])
    field_high[...] = high
    field_low[...] = low
    basis_high, basis_low = halves(basis_ref[...].T)

    def one(a, b):
        return jnp.dot(a, b, preferred_element_type=jnp.float32)

    core = one(basis_high, high) + (one(basis_high, low) + one(basis_low, high))
    core_ref[...] = core
    high, low = halves(core.T)
    core_high[...] = high
    core_low[...] = low
    pack_gram(field_high, field_low, packed_ref, 0, first)
    pack_gram(core_high, core_low, packed_ref, rows_one, second)
    filled = rows_one + rows_two
    spare = packed_ref.shape[0] - filled
    if spare:
        packed_ref[pl.ds(filled, spare), :] = jnp.zeros((spare, LANES), jnp.float32)


def unpack(packed_ref, base, out_ref, width, scale):
    full, left, offsets, tail, _ = triangle(width)
    for block in range(full):
        columns = pl.ds(block * LANES, LANES)
        for row in range(block + 1):
            tile = packed_ref[pl.ds(base + offsets[block] + row * LANES, LANES), :] * scale
            out_ref[pl.ds(row * LANES, LANES), columns] = tile
            if row < block:
                out_ref[columns, pl.ds(row * LANES, LANES)] = tile.T
        tile = packed_ref[pl.ds(base + tail + block * left, left), :] * scale
        out_ref[pl.ds(full * LANES, left), columns] = tile
        out_ref[columns, pl.ds(full * LANES, left)] = tile.T
    corner = packed_ref[pl.ds(base + tail + full * left, left), :] * scale
    out_ref[pl.ds(full * LANES, left), pl.ds(full * LANES, left)] = corner[:, 0:left]


def unpack_kernel(scale_one, scale_two, owner_ref, packed_ref, one_ref, two_ref, whole):
    first = whole.shape[0]
    second = two_ref.shape[0]
    rows = one_ref.shape[0]
    unpack(packed_ref, 0, whole, first, scale_one)
    start = pl.multiple_of(owner_ref[0] * rows, 8)
    one_ref[...] = whole[pl.ds(start, rows), :]
    unpack(packed_ref, triangle(first)[-1], two_ref, second, scale_two)


def scatter_sum(value, axis, count):
    rows = value.shape[0] // count
    parts = lax.all_to_all(value.reshape(count, rows, LANES), axis, 0, 0, tiled=True)
    return jnp.sum(parts, axis=0)


def gather(value, axis, count):
    copies = jnp.broadcast_to(value[None], (count,) + value.shape)
    return lax.all_to_all(copies, axis, 0, 0, tiled=True)


def local(sizes, tensor, basis):
    gx, gy, gz, gc = sizes
    slices_here, rows_here, second = tensor.shape
    first = rows_here * gx
    rank = basis.shape[1]
    slices_all = slices_here * gy * gz * gc
    used = triangle(first)[-1] + triangle(second)[-1]
    unit = 8 * gx * gy * gc
    packed_rows = -(-used // unit) * unit
    vmem = pl.BlockSpec(memory_space=pltpu.VMEM)

    whole_basis = gather(basis, "x", gx).reshape(first, rank)
    field = lax.all_to_all(tensor, "x", 0, 0, tiled=True).reshape(first, second)
    packed, core = pl.pallas_call(
        gram_kernel,
        out_shape=(
            jax.ShapeDtypeStruct((packed_rows, LANES), jnp.float32),
            jax.ShapeDtypeStruct((rank, second), jnp.float32),
        ),
        in_specs=[vmem, vmem],
        out_specs=(vmem, vmem),
        scratch_shapes=[
            pltpu.VMEM((first, second), jnp.bfloat16),
            pltpu.VMEM((first, second), jnp.bfloat16),
            pltpu.VMEM((second, rank), jnp.bfloat16),
            pltpu.VMEM((second, rank), jnp.bfloat16),
        ],
        name="local_grams",
    )(field, whole_basis)
    core_parts = lax.all_to_all(core.reshape(gx, rank // gx, second), "x", 0, 0, tiled=True)
    core_out = jnp.transpose(core_parts, (1, 0, 2))

    part = scatter_sum(packed, "c", gc)
    part = scatter_sum(part, "x", gx)
    part = scatter_sum(part, "y", gy)
    part = jnp.sum(gather(part, "z", gz), axis=0)
    part = gather(part, "y", gy).reshape(-1, LANES)
    part = gather(part, "x", gx).reshape(-1, LANES)
    whole = gather(part, "c", gc).reshape(-1, LANES)

    gram_one, gram_two = pl.pallas_call(
        functools.partial(unpack_kernel, 1.0 / (slices_all * second), 1.0 / (slices_all * rank)),
        out_shape=(
            jax.ShapeDtypeStruct((rows_here, first), jnp.float32),
            jax.ShapeDtypeStruct((second, second), jnp.float32),
        ),
        in_specs=[pl.BlockSpec(memory_space=pltpu.SMEM), vmem],
        out_specs=(vmem, vmem),
        scratch_shapes=[pltpu.VMEM((first, first), jnp.float32)],
        name="mirror",
    )(lax.axis_index("x").astype(jnp.int32).reshape(1), whole)
    return gram_one, core_out, gram_two


def solution(mesh):
    gx, rest = mesh.devices.shape
    sizes = (gx, 8, rest // 16, 2)
    fine = Mesh(mesh.devices.reshape(sizes), ("x", "y", "z", "c"))
    spread = ("y", "z", "c")
    in_specs = (P(spread, "x", None), P("x", None))
    out_specs = (P("x", None), P("x", spread, None), P())
    return jax.shard_map(
        functools.partial(local, sizes), mesh=fine, in_specs=in_specs, out_specs=out_specs, check_vma=False
    )
```

time: 386 us -> 169 us (0.44)
  waiting for transfers between devices: 292 us -> 15.6 us
  blocking collectives: 45.6 us -> 131 us
  matrix products: 17.4 us -> 0 us
  between operations: 14.1 us -> 0.69 us
  Pallas kernels: 0 us -> 11 us
  local copies, waits for them, and re-layouts: 10.7 us -> 3.2 us
  starting transfers between devices: 0.08 us -> 6.99 us
  other arithmetic: 4.89 us -> 0.39 us
    psum x1 -> x0, waiting for transfers between devices: 292 us -> none  [local(): summed = lax.psum(local_gram, ('gx', 'rest'))]
    all_to_all x1 -> x8, blocking collectives: 45.6 us -> 131 us  [the longest x4 56.6 us: gather(): return lax.all_to_all(copies, axis, 0, 0, tiled=True)]
    dot_general x3 -> x0, matrix products: 17.4 us -> none  [the longest x1 8.86 us: local(): jnp.einsum('kic,kjc->ij', exchanged, exchanged, precision=highest)]
    all_to_all x0 -> x2, waiting for transfers between devices: none -> 15.6 us  [the longest x1 9.41 us: gather(): return lax.all_to_all(copies, axis, 0, 0, tiled=True)]
    pallas_call x0 -> x2, Pallas kernels: none -> 11 us  [the longest x1 7.43 us: local(): pl.pallas_call(gram_kernel, out_shape=(jax.ShapeDtypeStruct((packed_rows,...]
    all_to_all x0 -> x2, starting transfers between devices: none -> 6.99 us  [the longest x1 3.53 us: gather(): return lax.all_to_all(copies, axis, 0, 0, tiled=True)]
    unnamed x6 -> x1, local copies, waits for them, and re-layouts: 5.98 us -> 1 us
    div x2 -> x0, other arithmetic: 4.89 us -> none  [the longest x1 3.02 us: local(): gram_two = gram_sum / (slices_all * rank_all)]
  transfers between devices with their start and end apart: 2 -> 2, of which waited for: 1 -> 2; matrix products, arithmetic and copies ran while one was open for 4% -> 1% of each run, Pallas kernels for 0% -> 0%
where the time goes in v1:
time: 169 us
  blocking collectives  131 us (78%)
  waiting for transfers between devices  15.6 us (9%)
  Pallas kernels  11 us (7%)
  starting transfers between devices  6.99 us (4%)
  local copies, waits for them, and re-layouts  3.2 us (2%)
    all_to_all x4, blocking collectives, gather(): return lax.all_to_all(copies, axis, 0, 0, tiled=True)  56.6 us
    all_to_all x3, blocking collectives, scatter_sum(): lax.all_to_all(value.reshape(count, rows, LANES), axis, 0, 0, tiled=True)  50.1 us
    all_to_all x1, blocking collectives, local(): field = lax.all_to_all(tensor, 'x', 0, 0, tiled=True).reshape(first, second)  24.1 us
    all_to_all x1, waiting for transfers between devices, gather(): return lax.all_to_all(copies, axis, 0, 0, tiled=True)  9.41 us
    pallas_call x1, Pallas kernels, local(): pl.pallas_call(gram_kernel, out_shape=(jax.ShapeDtypeStruct((packed_rows,...  7.43 us
    all_to_all x1, waiting for transfers between devices, local(): lax.all_to_all(core.reshape(gx, rank // gx, second), 'x', 0, 0, tiled=True)  6.17 us
    pallas_call x1, Pallas kernels, local(): pl.pallas_call(functools.partial(unpack_kernel, 1.0 / (slices_all * secon...  3.56 us
    all_to_all x1, starting transfers between devices, gather(): return lax.all_to_all(copies, axis, 0, 0, tiled=True)  3.53 us
  transfers between devices with their start and end apart: 2, of which 2 were waited for; matrix products, arithmetic and copies ran while one was open for 1% of the time, Pallas kernels for 0%

profile of v1, /device:TPU:1, one launch (start us, length us, event | category | flops | bytes accessed | tf_op | source)
XLA Modules:
  0.0 168.6 jit_solution(14493765797693561236)
XLA Ops:
  0.6 0.9 broadcast_in_dim.14
  1.5 10.7 %all_to_all.50 = f32[4,168,128]{2,1,0:T(8,128)} all-to-all(f32[4,168,128]{2,1,0:T(8,128)S(1)} %broadcast_in_dim.14), channel_id=1, replica_groups=mesh['x'=4,'y'=8,'z'=8,'c'=2] {'x'}, dimensions={0} | all-to-all | bytes 688128 | tf_op jit(solution)/shard_map/all_to_all | solution.py:114
  12.3 24.1 %all_to_all.51 = f32[4,168,672]{2,1,0:T(8,128)} all-to-all(f32[4,168,672]{2,1,0:T(8,128)} %param.2), channel_id=1, replica_groups=mesh['x'=4,'y'=8,'z'=8,'c'=2] {'x'}, dimensions={0} | all-to-all | bytes 3612672 | tf_op jit(solution)/shard_map/all_to_all | solution.py:129
  36.4 7.4 %local_grams.1 = (f32[4608,128]{1,0:T(8,128)}, f32[128,672]{1,0:T(8,128)}) custom-call(f32[672,672]{1,0:T(8,128)} %bitcast.12, f32[672,128]{1,0:T(8,128)} %bitcast.17), custom_call_target="tpu_custom_call" | custom-call | tf_op jit(solution)/shard_map/local_grams/pallas_call | solution.py:130
  43.8 13.7 %all_to_all.52 = f32[2,2304,128]{2,1,0:T(8,128)S(1)} all-to-all(f32[2,2304,128]{2,1,0:T(8,128)} %bitcast.15), channel_id=1, replica_groups=mesh['x'=4,'y'=8,'z'=8,'c'=2] {'c'}, dimensions={0} | all-to-all | bytes 4718592 | tf_op jit(solution)/shard_map/all_to_all | solution.py:108
  57.6 0.3 reduce_sum.36
  57.8 18.7 %all_to_all.53 = f32[4,576,128]{2,1,0:T(8,128)S(1)} all-to-all(f32[4,576,128]{2,1,0:T(8,128)S(1)} %bitcast.14), channel_id=1, replica_groups=mesh['x'=4,'y'=8,'z'=8,'c'=2] {'x'}, dimensions={0} | all-to-all | bytes 2359296 | tf_op jit(solution)/shard_map/all_to_all | solution.py:108
  76.5 0.1 reduce_sum.37
  76.6 17.7 %all_to_all.54 = f32[8,72,128]{2,1,0:T(8,128)S(1)} all-to-all(f32[8,72,128]{2,1,0:T(8,128)S(1)} %bitcast.18), channel_id=1, replica_groups=mesh['x'=4,'y'=8,'z'=8,'c'=2] {'y'}, dimensions={0} | all-to-all | bytes 589824 | tf_op jit(solution)/shard_map/all_to_all | solution.py:108
  94.3 19.6 %all_to_all.55 = f32[8,72,128]{2,1,0:T(8,128)S(1)} all-to-all(f32[8,72,128]{2,1,0:T(8,128)S(1)} %broadcast_in_dim.15), channel_id=1, replica_groups=mesh['x'=4,'y'=8,'z'=8,'c'=2] {'z'}, dimensions={0} | all-to-all | bytes 589824 | tf_op jit(solution)/shard_map/all_to_all | solution.py:114
  113.9 3.5 %all-to-all-start.9 = ((f32[4,32,672]{2,1,0:T(8,128)}), f32[4,32,672]{2,1,0:T(8,128)S(1)}, u32[]{:S(2)}, u32[]{:S(2)}) async-start(f32[4,32,672]{2,1,0:T(8,128)} %bitcast.9), calls=%async_computation.9 | async-start | bytes 786432 | tf_op jit(solution)/shard_map/all_to_all | solution.py:146
  117.4 6.2 %all-to-all-done.9 = f32[4,32,672]{2,1,0:T(8,128)S(1)} async-done(((f32[4,32,672]{2,1,0:T(8,128)}), f32[4,32,672]{2,1,0:T(8,128)S(1)}, u32[]{:S(2)}, u32[]{:S(2)}) %all-to-all-start.9) | async-done | bytes 344096 | tf_op jit(solution)/shard_map/all_to_all | solution.py:146
  123.6 13.0 %all_to_all.56 = f32[8,72,128]{2,1,0:T(8,128)S(1)} all-to-all(f32[8,72,128]{2,1,0:T(8,128)S(1)} %broadcast_in_dim.16), channel_id=1, replica_groups=mesh['x'=4,'y'=8,'z'=8,'c'=2] {'y'}, dimensions={0} | all-to-all | bytes 589824 | tf_op jit(solution)/shard_map/all_to_all | solution.py:114
  136.6 1.1 broadcast_in_dim.36
  137.6 3.5 %all-to-all-start.7 = ((f32[4,576,128]{2,1,0:T(8,128)}), f32[4,576,128]{2,1,0:T(8,128)S(1)}, u32[]{:S(2)}, u32[]{:S(2)}) async-start(f32[4,576,128]{2,1,0:T(8,128)} %broadcast_in_dim.36), calls=%async_computation.7 | async-start | bytes 2359296 | tf_op jit(solution)/shard_map/all_to_all | solution.py:114
  141.2 1.0 copy.7
  142.2 9.4 %all-to-all-done.7 = f32[4,576,128]{2,1,0:T(8,128)S(1)} async-done(((f32[4,576,128]{2,1,0:T(8,128)}), f32[4,576,128]{2,1,0:T(8,128)S(1)}, u32[]{:S(2)}, u32[]{:S(2)}) %all-to-all-start.7) | async-done | bytes 1179680 | tf_op jit(solution)/shard_map/all_to_all | solution.py:114
  151.6 0.2 broadcast_in_dim.38
  151.8 13.3 %all_to_all.57 = f32[2,2304,128]{2,1,0:T(8,128)} all-to-all(f32[2,2304,128]{2,1,0:T(8,128)S(1)} %broadcast_in_dim.38), channel_id=1, replica_groups=mesh['x'=4,'y'=8,'z'=8,'c'=2] {'c'}, dimensions={0} | all-to-all | bytes 4718592 | tf_op jit(solution)/shard_map/all_to_all | solution.py:114
  165.1 3.6 %mirror.1 = (f32[168,672]{1,0:T(8,128)}, f32[672,672]{1,0:T(8,128)}) custom-call(s32[1]{0:T(128)} %bitcast.owner_ref, f32[4608,128]{1,0:T(8,128)} %bitcast.11), custom_call_target="tpu_custom_call" | custom-call | tf_op jit(solution)/shard_map/mirror/pallas_call | solution.py:157
  (4 shorter events, 0.1 us)
Async XLA Ops:
  113.9 9.7 %all-to-all-start.9 = ((f32[4,32,672]{2,1,0:T(8,128)}), f32[4,32,672]{2,1,0:T(8,128)S(1)}, u32[]{:S(2)}, u32[]{:S(2)}) async-start(f32[4,32,672]{2,1,0:T(8,128)} %bitcast.9), calls=%async_computation.9 | async-start | bytes 786432 | tf_op jit(solution)/shard_map/all_to_all | solution.py:146
  137.6 14.0 %all-to-all-start.7 = ((f32[4,576,128]{2,1,0:T(8,128)}), f32[4,576,128]{2,1,0:T(8,128)S(1)}, u32[]{:S(2)}, u32[]{:S(2)}) async-start(f32[4,576,128]{2,1,0:T(8,128)} %broadcast_in_dim.36), calls=%async_computation.7 | async-start | bytes 2359296 | tf_op jit(solution)/shard_map/all_to_all | solution.py:114

commit v2 on v0

v2 whole, which is shorter than its diff:
```python
import functools

import jax
import jax.numpy as jnp
from jax import lax
from jax.experimental import pallas as pl
from jax.experimental.pallas import tpu as pltpu
from jax.sharding import Mesh, PartitionSpec as P

LANES = 128
FOLD = LANES // 2
VMEM = pl.BlockSpec(memory_space=pltpu.VMEM)
SMEM = pl.BlockSpec(memory_space=pltpu.SMEM)
ROOM = pltpu.CompilerParams(vmem_limit_bytes=24 << 20)


class Layout:
    def __init__(self, width, unit):
        self.width = width
        self.full = width // LANES
        self.left = width - self.full * LANES
        self.above = [0] * self.full
        row = 0
        for block in range(1, self.full):
            self.above[block] = row
            row += block * LANES
        self.strip = row
        row += self.left * (self.full + 1)
        split = -(-self.full // 2)
        self.fold = [(block // split, row + (block % split) * 3 * FOLD) for block in range(self.full)]
        self.used = [row + split * 3 * FOLD, row + (self.full - split) * 3 * FOLD]
        self.rows = -(-self.used[0] // unit) * unit


def halves(value):
    high = value.astype(jnp.bfloat16)
    low = (value - high.astype(jnp.float32)).astype(jnp.bfloat16)
    return high, low


def dot(a, b):
    return jnp.dot(a, b, preferred_element_type=jnp.float32)


def dot_rows(a, b):
    return lax.dot_general(a, b, (((1,), (1,)), ((), ())), preferred_element_type=jnp.float32)


def product(high, low, left, right):
    lh, ll, rh, rl = high[left, :], low[left, :], high[right, :], low[right, :]
    return dot_rows(lh, rh) + (dot_rows(lh, rl) + dot_rows(ll, rh))


def lane_below(rows):
    return lax.broadcasted_iota(jnp.int32, (rows, LANES), 1) < FOLD


def pack_gram(layout, high, low, packed, half):
    full, left = layout.full, layout.left
    for block in range(full):
        mine = pl.ds(block * LANES, LANES)
        tiles = product(high, low, pl.ds(0, (block + 1) * LANES), mine)
        above = block * LANES
        if above:
            packed[half, pl.ds(layout.above[block], above), :] = tiles[:above]
        into, row = layout.fold[block]
        packed[into, pl.ds(row + half * FOLD, FOLD), :] = tiles[above : above + FOLD]
        lower = tiles[above + FOLD :]
        corner = pl.ds(row + 2 * FOLD, FOLD)
        if half == 0:
            packed[into, corner, :] = pltpu.roll(lower, FOLD, 1)
        else:
            packed[into, corner, :] = jnp.where(lane_below(FOLD), packed[into, corner, :], lower)
    last = product(high, low, pl.ds(full * LANES, left), pl.ds(0, layout.width))
    for block in range(full):
        packed[half, pl.ds(layout.strip + block * left, left), :] = last[:, block * LANES : (block + 1) * LANES]
    corner = pl.ds(layout.strip + full * left, left)
    packed[half, corner, :] = jnp.zeros((left, LANES), jnp.float32)
    packed[half, corner, 0:left] = last[:, full * LANES :]
    spare = layout.rows - layout.used[half]
    if spare:
        packed[half, pl.ds(layout.used[half], spare), :] = jnp.zeros((spare, LANES), jnp.float32)


def dense_rows(rows, width):
    full = width // LANES
    left = width - full * LANES
    beside = LANES // left
    group = -(-rows // (8 * beside)) * 8
    return full, left, beside, group, rows * (full + 1) + group


def dense_kernel(field_ref, basis_ref, out_ref):
    _, rows, width = field_ref.shape
    full, left, beside, group, _ = dense_rows(rows, width)
    for block in range(full):
        out_ref[0, pl.ds(block * rows, rows), :] = field_ref[0, :, block * LANES : (block + 1) * LANES]
    out_ref[0, pl.ds(full * rows, rows), :] = basis_ref[...]
    base = (full + 1) * rows
    for part in range(beside):
        some = min(group, rows - part * group)
        piece = field_ref[0, pl.ds(part * group, some), full * LANES : width]
        out_ref[0, pl.ds(base, some), part * left : (part + 1) * left] = piece
        if some < group:
            rest = pl.ds(base + some, group - some)
            out_ref[0, rest, part * left : (part + 1) * left] = jnp.zeros((group - some, left), jnp.float32)


def gram_kernel(
    layout, mine_ref, dense_ref, keep_ref, send_ref, core_ref,
    field, basis, field_high, field_low, core_high, core_low, packed,
):
    blocks = dense_ref.shape[0]
    first, width = field.shape
    rows = first // blocks
    full, left, beside, group, _ = dense_rows(rows, width)
    for owner in range(blocks):
        for block in range(full):
            field[pl.ds(owner * rows, rows), block * LANES : (block + 1) * LANES] = dense_ref[
                owner, pl.ds(block * rows, rows), :
            ]
        basis[pl.ds(owner * rows, rows), :] = dense_ref[owner, pl.ds(full * rows, rows), :]
        base = (full + 1) * rows
        for part in range(beside):
            some = min(group, rows - part * group)
            field[pl.ds(owner * rows + part * group, some), full * LANES : width] = dense_ref[
                owner, pl.ds(base, some), part * left : (part + 1) * left
            ]
    high, low = halves(field[...])
    field_high[...] = high
    field_low[...] = low
    basis_high, basis_low = halves(basis[...].T)
    core = dot(basis_high, high) + (dot(basis_high, low) + dot(basis_low, high))
    core_ref[...] = core
    high, low = halves(core.T)
    core_high[...] = high
    core_low[...] = low
    pack_gram(layout, field_high, field_low, packed, 0)
    pack_gram(layout, core_high, core_low, packed, 1)
    mine = mine_ref[0]
    keep_ref[...] = packed[mine]
    send_ref[...] = packed[1 - mine]


def unpack(layout, packed, half, out_ref, scale):
    full, left = layout.full, layout.left
    for block in range(full):
        columns = pl.ds(block * LANES, LANES)
        for row in range(block):
            there = pl.ds(row * LANES, LANES)
            tile = packed[half, pl.ds(layout.above[block] + row * LANES, LANES), :] * scale
            out_ref[there, columns] = tile
            out_ref[columns, there] = tile.T
        into, row = layout.fold[block]
        upper = packed[into, pl.ds(row + half * FOLD, FOLD), :] * scale
        lower = packed[into, pl.ds(row + 2 * FOLD, FOLD), :] * scale
        if half == 0:
            lower = pltpu.roll(lower, FOLD, 1)
        turned = jnp.concatenate([upper, upper], axis=0).T[FOLD:]
        out_ref[pl.ds(block * LANES, FOLD), columns] = upper
        out_ref[pl.ds(block * LANES + FOLD, FOLD), columns] = jnp.where(lane_below(FOLD), turned, lower)
        tile = packed[half, pl.ds(layout.strip + block * left, left), :] * scale
        out_ref[pl.ds(full * LANES, left), columns] = tile
        out_ref[columns, pl.ds(full * LANES, left)] = tile.T
    corner = packed[half, pl.ds(layout.strip + full * left, left), :] * scale
    out_ref[pl.ds(full * LANES, left), pl.ds(full * LANES, left)] = corner[:, 0:left]


def unpack_kernel(layout, scale_one, scale_two, place_ref, own_ref, other_ref, one_ref, two_ref, packed, whole):
    rows = one_ref.shape[0]
    mine = place_ref[1]
    packed[mine] = own_ref[...]
    packed[1 - mine] = other_ref[...]
    unpack(layout, packed, 0, whole, scale_one)
    one_ref[...] = whole[pl.ds(pl.multiple_of(place_ref[0] * rows, 8), rows), :]
    unpack(layout, packed, 1, two_ref, scale_two)


def exchange(parts, axis):
    return lax.all_to_all(parts, axis, 0, 0, tiled=True)


def copies(value, count):
    return jnp.broadcast_to(value[None], (count,) + value.shape)


def local(sizes, tensor, basis):
    gx, gy, gz, gc = sizes
    slices_here, rows_here, second = tensor.shape
    first = rows_here * gx
    rank = basis.shape[1]
    slices_all = slices_here * gy * gz * gc
    plane = gy * gz
    layout = Layout(first, 8 * gx * plane)
    dense = dense_rows(rows_here, second)[-1]
    swap = [(i, gc - 1 - i) for i in range(gc)]
    place = jnp.stack([lax.axis_index("x"), lax.axis_index("c")]).astype(jnp.int32)

    blocks = pl.pallas_call(
        dense_kernel,
        grid=(slices_here,),
        out_shape=jax.ShapeDtypeStruct((slices_here, dense, LANES), jnp.float32),
        in_specs=[
            pl.BlockSpec((1, rows_here, second), lambda k: (k, 0, 0)),
            pl.BlockSpec((rows_here, rank), lambda k: (0, 0)),
        ],
        out_specs=pl.BlockSpec((1, dense, LANES), lambda k: (k, 0, 0)),
        name="dense_blocks",
    )(tensor, basis)
    blocks = exchange(blocks, "x")
    f32, bf16 = jnp.float32, jnp.bfloat16
    half_shape = jax.ShapeDtypeStruct((layout.rows, LANES), f32)
    keep, send, core = pl.pallas_call(
        functools.partial(gram_kernel, layout),
        out_shape=(half_shape, half_shape, jax.ShapeDtypeStruct((rank, second), f32)),
        in_specs=[SMEM, VMEM],
        out_specs=(VMEM, VMEM, VMEM),
        scratch_shapes=[
            pltpu.VMEM((first, second), f32),
            pltpu.VMEM((first, rank), f32),
            pltpu.VMEM((first, second), bf16),
            pltpu.VMEM((first, second), bf16),
            pltpu.VMEM((second, rank), bf16),
            pltpu.VMEM((second, rank), bf16),
            pltpu.VMEM((2, layout.rows, LANES), f32),
        ],
        compiler_params=ROOM,
        name="local_grams",
    )(place[1:], blocks)

    core_parts = exchange(core.reshape(gx, rank // gx, second), "x")
    came = lax.ppermute(send, "c", swap)
    came, core_parts = lax.optimization_barrier((came, core_parts))
    core_out = jnp.transpose(core_parts, (1, 0, 2))

    part = exchange((keep + came).reshape(gx, -1, LANES), "x")
    part = jnp.sum(part, axis=0)
    part = exchange(part.reshape(plane, -1, LANES), ("y", "z"))
    part = exchange(copies(jnp.sum(part, axis=0), plane), ("y", "z")).reshape(-1, LANES)
    own = exchange(copies(part, gx), "x").reshape(-1, LANES)
    other = lax.ppermute(own, "c", swap)

    gram_one, gram_two = pl.pallas_call(
        functools.partial(unpack_kernel, layout, 1.0 / (slices_all * second), 1.0 / (slices_all * rank)),
        out_shape=(
            jax.ShapeDtypeStruct((rows_here, first), f32),
            jax.ShapeDtypeStruct((second, second), f32),
        ),
        in_specs=[SMEM, VMEM, VMEM],
        out_specs=(VMEM, VMEM),
        scratch_shapes=[pltpu.VMEM((2, layout.rows, LANES), f32), pltpu.VMEM((first, first), f32)],
        compiler_params=ROOM,
        name="mirror",
    )(place, own, other)
    return gram_one, core_out, gram_two


def solution(mesh):
    gx, rest = mesh.devices.shape
    sizes = (gx, 8, rest // 16, 2)
    fine = Mesh(mesh.devices.reshape(sizes), ("x", "y", "z", "c"))
    spread = ("y", "z", "c")
    in_specs = (P(spread, "x", None), P("x", None))
    out_specs = (P("x", None), P("x", spread, None), P())
    return jax.shard_map(
        functools.partial(local, sizes), mesh=fine, in_specs=in_specs, out_specs=out_specs, check_vma=False
    )
```

time: 386 us -> 142 us (0.37)
  waiting for transfers between devices: 292 us -> 22.3 us
  blocking collectives: 45.6 us -> 84.7 us
  starting transfers between devices: 0.08 us -> 21 us
  matrix products: 17.4 us -> 0 us
  between operations: 14.1 us -> 0.68 us
  Pallas kernels: 0 us -> 11.4 us
  local copies, waits for them, and re-layouts: 10.7 us -> 1.09 us
  other arithmetic: 4.89 us -> 0.32 us
    psum x1 -> x0, waiting for transfers between devices: 292 us -> none  [local(): summed = lax.psum(local_gram, ('gx', 'rest'))]
    all_to_all x1 -> x5, blocking collectives: 45.6 us -> 84.7 us  [exchange(): return lax.all_to_all(parts, axis, 0, 0, tiled=True)]
    all_to_all x0 -> x1, waiting for transfers between devices: none -> 21.2 us  [exchange(): return lax.all_to_all(parts, axis, 0, 0, tiled=True)]
    dot_general x3 -> x0, matrix products: 17.4 us -> none  [the longest x1 8.86 us: local(): jnp.einsum('kic,kjc->ij', exchanged, exchanged, precision=highest)]
    ppermute x0 -> x2, starting transfers between devices: none -> 16.2 us  [the longest x1 8.75 us: local(): came = lax.ppermute(send, 'c', swap)]
    pallas_call x0 -> x3, Pallas kernels: none -> 11.4 us  [the longest x1 4.74 us: local(): pl.pallas_call(functools.partial(gram_kernel, layout), out_shape=(half_sh...]
    unnamed x6 -> x1, local copies, waits for them, and re-layouts: 5.98 us -> 1 us
    div x2 -> x0, other arithmetic: 4.89 us -> none  [the longest x1 3.02 us: local(): gram_two = gram_sum / (slices_all * rank_all)]
  transfers between devices with their start and end apart: 2 -> 3, of which waited for: 1 -> 2; matrix products, arithmetic and copies ran while one was open for 4% -> 1% of each run, Pallas kernels for 0% -> 0%
where the time goes in v2:
time: 142 us
  blocking collectives  84.7 us (60%)
  waiting for transfers between devices  22.3 us (16%)
  starting transfers between devices  21 us (15%)
  Pallas kernels  11.4 us (8%)
    all_to_all x5, blocking collectives, exchange(): return lax.all_to_all(parts, axis, 0, 0, tiled=True)  84.7 us
    all_to_all x1, waiting for transfers between devices, exchange(): return lax.all_to_all(parts, axis, 0, 0, tiled=True)  21.2 us
    ppermute x1, starting transfers between devices, local(): came = lax.ppermute(send, 'c', swap)  8.75 us
    ppermute x1, starting transfers between devices, local(): other = lax.ppermute(own, 'c', swap)  7.4 us
    all_to_all x1, starting transfers between devices, exchange(): return lax.all_to_all(parts, axis, 0, 0, tiled=True)  4.84 us
    pallas_call x1, Pallas kernels, local(): pl.pallas_call(functools.partial(gram_kernel, layout), out_shape=(half_sh...  4.74 us
    pallas_call x1, Pallas kernels, local(): pl.pallas_call(dense_kernel, grid=(slices_here,), out_shape=jax.ShapeDtyp...  3.87 us
  transfers between devices with their start and end apart: 3, of which 2 were waited for; matrix products, arithmetic and copies ran while one was open for 1% of the time, Pallas kernels for 0%

profile of v2, /device:TPU:1, one launch (start us, length us, event | category | flops | bytes accessed | tf_op | source)
XLA Modules:
  0.0 141.6 jit_solution(4371986146622342833)
XLA Ops:
  0.6 3.9 %dense_blocks.1 = f32[4,1056,128]{2,1,0:T(8,128)} custom-call(f32[4,168,672]{2,1,0:T(8,128)} %field_ref.1, f32[168,128]{1,0:T(8,128)} %basis_ref.1), custom_call_target="tpu_custom_call" | custom-call | tf_op jit(solution)/shard_map/dense_blocks/pallas_call | solution.py:199
  4.5 4.8 %all-to-all-start = ((f32[4,1056,128]{2,1,0:T(8,128)}), f32[4,1056,128]{2,1,0:T(8,128)S(1)}, u32[]{:S(2)}, u32[]{:S(2)}) async-start(f32[4,1056,128]{2,1,0:T(8,128)} %dense_blocks.1), calls=%async_computation | async-start | bytes 4325376 | tf_op jit(solution)/shard_map/all_to_all | solution.py:180
  9.3 21.2 %all-to-all-done.dense_ref = f32[4,1056,128]{2,1,0:T(8,128)S(1)} async-done(((f32[4,1056,128]{2,1,0:T(8,128)}), f32[4,1056,128]{2,1,0:T(8,128)S(1)}, u32[]{:S(2)}, u32[]{:S(2)}) %all-to-all-start) | async-done | bytes 2162720 | tf_op jit(solution)/shard_map/all_to_all | solution.py:180
  30.5 4.7 %local_grams.1 = (f32[2048,128]{1,0:T(8,128)S(1)}, f32[2048,128]{1,0:T(8,128)S(1)}, f32[128,672]{1,0:T(8,128)S(1)}) custom-call(s32[1]{0:T(128)} %bitcast.1.mine_ref, f32[4,1056,128]{2,1,0:T(8,128)S(1)} %all-to-all-done.dense_ref), custom_call_target="tpu_custom_call" | custom-call | tf_op jit(solution)/shard_map/local_grams/pallas_call | solution.py:213
  35.2 8.7 %collective-permute-start = (f32[2048,128]{1,0:T(8,128)S(1)}, f32[2048,128]{1,0:T(8,128)S(1)}, u32[]{:S(2)}, u32[]{:S(2)}) collective-permute-start(f32[2048,128]{1,0:T(8,128)S(1)} %get-tuple-element.11), channel_id=1, source_target_pairs={{0,1},{1,0},{2,3},{3,2},{4,5},{5,4},{6,7},{7,6},{8,9},{9,8},{10,11... | collective-permute-start | bytes 3145736 | tf_op jit(solution)/shard_map/ppermute | solution.py:232
  44.0 10.3 %all_to_all.30 = f32[4,32,672]{2,1,0:T(8,128)S(1)} all-to-all(f32[4,32,672]{2,1,0:T(8,128)S(1)} %bitcast.10), channel_id=1, replica_groups=mesh['x'=4,'y'=8,'z'=8,'c'=2] {'x'}, dimensions={0} | all-to-all | bytes 688128 | tf_op jit(solution)/shard_map/all_to_all | solution.py:180
  54.3 0.0 collective-permute-done
  54.3 0.1 add.3
  54.4 16.5 %all_to_all.31 = f32[4,512,128]{2,1,0:T(8,128)S(1)} all-to-all(f32[4,512,128]{2,1,0:T(8,128)S(1)} %bitcast.11), channel_id=1, replica_groups=mesh['x'=4,'y'=8,'z'=8,'c'=2] {'x'}, dimensions={0} | all-to-all | bytes 2097152 | tf_op jit(solution)/shard_map/all_to_all | solution.py:180
  70.9 0.1 reduce_sum.18
  71.0 28.6 %all_to_all.32 = f32[64,8,128]{2,1,0:T(8,128)S(1)} all-to-all(f32[64,8,128]{2,1,0:T(8,128)S(1)} %bitcast.13), channel_id=1, replica_groups=mesh['x'=4,'y'=8,'z'=8,'c'=2] {'y','z'}, dimensions={0} | all-to-all | bytes 524288 | tf_op jit(solution)/shard_map/all_to_all | solution.py:180
  99.6 0.1 reduce_sum.19
  99.6 16.4 %all_to_all.33 = f32[64,8,128]{2,1,0:T(8,128)S(1)} all-to-all(f32[64,8,128]{2,1,0:T(8,128)S(1)} %broadcast_in_dim.6), channel_id=1, replica_groups=mesh['x'=4,'y'=8,'z'=8,'c'=2] {'y','z'}, dimensions={0} | all-to-all | bytes 524288 | tf_op jit(solution)/shard_map/all_to_all | solution.py:180
  116.0 0.1 broadcast_in_dim.15
  116.1 13.0 %all_to_all.34 = f32[4,512,128]{2,1,0:T(8,128)S(1)} all-to-all(f32[4,512,128]{2,1,0:T(8,128)S(1)} %broadcast_in_dim.15), channel_id=1, replica_groups=mesh['x'=4,'y'=8,'z'=8,'c'=2] {'x'}, dimensions={0} | all-to-all | bytes 2097152 | tf_op jit(solution)/shard_map/all_to_all | solution.py:180
  129.1 7.4 %collective-permute-start.1 = (f32[2048,128]{1,0:T(8,128)S(1)}, f32[2048,128]{1,0:T(8,128)S(1)}, u32[]{:S(2)}, u32[]{:S(2)}) collective-permute-start(f32[2048,128]{1,0:T(8,128)S(1)} %bitcast.8), channel_id=1, source_target_pairs={{0,1},{1,0},{2,3},{3,2},{4,5},{5,4},{6,7},{7,6},{8,9},{9,8},{10,11... | collective-permute-start | bytes 3145736 | tf_op jit(solution)/shard_map/ppermute | solution.py:241
  136.5 0.1 pad_add_fusion.place_ref
  136.6 1.0 copy.7
  137.6 1.2 collective-permute-done.1.other_ref
  138.7 2.8 %mirror.1 = (f32[168,672]{1,0:T(8,128)}, f32[672,672]{1,0:T(8,128)}) custom-call(s32[2]{0:T(128)S(1)} %pad_add_fusion.place_ref, f32[2048,128]{1,0:T(8,128)S(1)} %bitcast.9, f32[2048,128]{1,0:T(8,128)S(1)} %collective-permute-done.1.other_ref), custom_call_target="tpu_custom_call" | custom-call | tf_op jit(solution)/shard_map/mirror/pallas_call | solution.py:243
  (1 shorter events, 0.0 us)
Async XLA Ops:
  4.5 26.0 %all-to-all-start = ((f32[4,1056,128]{2,1,0:T(8,128)}), f32[4,1056,128]{2,1,0:T(8,128)S(1)}, u32[]{:S(2)}, u32[]{:S(2)}) async-start(f32[4,1056,128]{2,1,0:T(8,128)} %dense_blocks.1), calls=%async_computation | async-start | bytes 4325376 | tf_op jit(solution)/shard_map/all_to_all | solution.py:180
  35.2 19.1 %collective-permute-start = (f32[2048,128]{1,0:T(8,128)S(1)}, f32[2048,128]{1,0:T(8,128)S(1)}, u32[]{:S(2)}, u32[]{:S(2)}) collective-permute-start(f32[2048,128]{1,0:T(8,128)S(1)} %get-tuple-element.11), channel_id=1, source_target_pairs={{0,1},{1,0},{2,3},{3,2},{4,5},{5,4},{6,7},{7,6},{8,9},{9,8},{10,11... | collective-permute-start | bytes 3145736 | tf_op jit(solution)/shard_map/ppermute | solution.py:232
  129.1 9.7 %collective-permute-start.1 = (f32[2048,128]{1,0:T(8,128)S(1)}, f32[2048,128]{1,0:T(8,128)S(1)}, u32[]{:S(2)}, u32[]{:S(2)}) collective-permute-start(f32[2048,128]{1,0:T(8,128)S(1)} %bitcast.8), channel_id=1, source_target_pairs={{0,1},{1,0},{2,3},{3,2},{4,5},{5,4},{6,7},{7,6},{8,9},{9,8},{10,11... | collective-permute-start | bytes 3145736 | tf_op jit(solution)/shard_map/ppermute | solution.py:241

commit v3 on v2

--- a/solution.py
+++ b/solution.py
@@ -90,24 +90,40 @@
     return full, left, beside, group, rows * (full + 1) + group
 
 
-def dense_kernel(field_ref, basis_ref, out_ref):
-    _, rows, width = field_ref.shape
+def dense_kernel(field_ref, basis_ref, out_ref, dense, tail, arrived, left_for):
+    blocks, rows, width = field_ref.shape
     full, left, beside, group, _ = dense_rows(rows, width)
-    for block in range(full):
-        out_ref[0, pl.ds(block * rows, rows), :] = field_ref[0, :, block * LANES : (block + 1) * LANES]
-    out_ref[0, pl.ds(full * rows, rows), :] = basis_ref[...]
+    moves = []
+    for block in range(blocks):
+        last = field_ref.at[block, :, pl.ds(full * LANES, left)]
+        mine = [pltpu.make_async_copy(last, tail.at[block], arrived.at[block, full + 1])]
+        for part in range(full + 1):
+            source = basis_ref if part == full else field_ref.at[block, :, pl.ds(part * LANES, LANES)]
+            into = dense.at[block, pl.ds(part * rows, rows), :]
+            mine.append(pltpu.make_async_copy(source, into, arrived.at[block, part]))
+        for move in mine:
+            move.start()
+        moves.append(mine)
     base = (full + 1) * rows
-    for part in range(beside):
-        some = min(group, rows - part * group)
-        piece = field_ref[0, pl.ds(part * group, some), full * LANES : width]
-        out_ref[0, pl.ds(base, some), part * left : (part + 1) * left] = piece
-        if some < group:
-            rest = pl.ds(base + some, group - some)
-            out_ref[0, rest, part * left : (part + 1) * left] = jnp.zeros((group - some, left), jnp.float32)
+    done = []
+    for block in range(blocks):
+        for move in moves[block]:
+            move.wait()
+        for part in range(beside):
+            some = min(group, rows - part * group)
+            lanes = slice(part * left, (part + 1) * left)
+            dense[block, pl.ds(base, some), lanes] = tail[block, pl.ds(part * group, some), :]
+            if some < group:
+                dense[block, pl.ds(base + some, group - some), lanes] = jnp.zeros((group - some, left), jnp.float32)
+        move = pltpu.make_async_copy(dense.at[block], out_ref.at[block], left_for.at[block])
+        move.start()
+        done.append(move)
+    for move in done:
+        move.wait()
 
 
 def gram_kernel(
-    layout, mine_ref, dense_ref, keep_ref, send_ref, core_ref,
+    layout, place_ref, dense_ref, keep_ref, send_ref, core_ref,
     field, basis, field_high, field_low, core_high, core_low, packed,
 ):
     blocks = dense_ref.shape[0]
@@ -131,13 +147,20 @@
     field_low[...] = low
     basis_high, basis_low = halves(basis[...].T)
     core = dot(basis_high, high) + (dot(basis_high, low) + dot(basis_low, high))
-    core_ref[...] = core
+    owners, tiles, owned, _ = core_ref.shape
+    for owner in range(owners):
+        for tile in range(tiles):
+            lanes = min(LANES, width - tile * LANES)
+            piece = core[owner * owned : (owner + 1) * owned, tile * LANES : tile * LANES + lanes]
+            if lanes < LANES:
+                core_ref[owner, tile] = jnp.zeros((owned, LANES), jnp.float32)
+            core_ref[owner, tile, :, 0:lanes] = piece
     high, low = halves(core.T)
     core_high[...] = high
     core_low[...] = low
     pack_gram(layout, field_high, field_low, packed, 0)
     pack_gram(layout, core_high, core_low, packed, 1)
-    mine = mine_ref[0]
+    mine = place_ref[1]
     keep_ref[...] = packed[mine]
     send_ref[...] = packed[1 - mine]
 
@@ -196,23 +219,28 @@
     swap = [(i, gc - 1 - i) for i in range(gc)]
     place = jnp.stack([lax.axis_index("x"), lax.axis_index("c")]).astype(jnp.int32)
 
+    outside = pl.BlockSpec(memory_space=pl.ANY)
+    full, left = dense_rows(rows_here, second)[:2]
     blocks = pl.pallas_call(
         dense_kernel,
-        grid=(slices_here,),
         out_shape=jax.ShapeDtypeStruct((slices_here, dense, LANES), jnp.float32),
-        in_specs=[
-            pl.BlockSpec((1, rows_here, second), lambda k: (k, 0, 0)),
-            pl.BlockSpec((rows_here, rank), lambda k: (0, 0)),
+        in_specs=[outside, outside],
+        out_specs=outside,
+        scratch_shapes=[
+            pltpu.VMEM((slices_here, dense, LANES), jnp.float32),
+            pltpu.VMEM((slices_here, rows_here, left), jnp.float32),
+            pltpu.SemaphoreType.DMA((slices_here, full + 2)),
+            pltpu.SemaphoreType.DMA((slices_here,)),
         ],
-        out_specs=pl.BlockSpec((1, dense, LANES), lambda k: (k, 0, 0)),
         name="dense_blocks",
     )(tensor, basis)
+    blocks, place = lax.optimization_barrier((blocks, place))
     blocks = exchange(blocks, "x")
     f32, bf16 = jnp.float32, jnp.bfloat16
     half_shape = jax.ShapeDtypeStruct((layout.rows, LANES), f32)
     keep, send, core = pl.pallas_call(
         functools.partial(gram_kernel, layout),
-        out_shape=(half_shape, half_shape, jax.ShapeDtypeStruct((rank, second), f32)),
+        out_shape=(half_shape, half_shape, jax.ShapeDtypeStruct((gx, full + 1, rank // gx, LANES), f32)),
         in_specs=[SMEM, VMEM],
         out_specs=(VMEM, VMEM, VMEM),
         scratch_shapes=[
@@ -226,15 +254,15 @@
         ],
         compiler_params=ROOM,
         name="local_grams",
-    )(place[1:], blocks)
-
-    core_parts = exchange(core.reshape(gx, rank // gx, second), "x")
+    )(place, blocks)
+
     came = lax.ppermute(send, "c", swap)
-    came, core_parts = lax.optimization_barrier((came, core_parts))
-    core_out = jnp.transpose(core_parts, (1, 0, 2))
-
-    part = exchange((keep + came).reshape(gx, -1, LANES), "x")
-    part = jnp.sum(part, axis=0)
+    sums = (keep + came).reshape(gx, -1, LANES)
+    some = sums.shape[1]
+    parts = exchange(jnp.concatenate([sums, core.reshape(gx, -1, LANES)], axis=1), "x")
+    part = jnp.sum(parts[:, :some], axis=0)
+    core_out = parts[:, some:].reshape(gx, full + 1, rank // gx, LANES)
+    core_out = jnp.transpose(core_out, (2, 0, 1, 3)).reshape(rank // gx, gx, -1)[:, :, :second]
     part = exchange(part.reshape(plane, -1, LANES), ("y", "z"))
     part = exchange(copies(jnp.sum(part, axis=0), plane), ("y", "z")).reshape(-1, LANES)
     own = exchange(copies(part, gx), "x").reshape(-1, LANES)

time: 142 us -> 141 us (level)
  blocking collectives: 84.7 us -> 109 us
  waiting for transfers between devices: 22.3 us -> 3.46 us
  starting transfers between devices: 21 us -> 15.1 us
    all_to_all x5, blocking collectives: 84.7 us -> 109 us  [exchange(): return lax.all_to_all(parts, axis, 0, 0, tiled=True)]
    all_to_all x1 -> x0, waiting for transfers between devices: 21.2 us -> none  [exchange(): return lax.all_to_all(parts, axis, 0, 0, tiled=True)]
    all_to_all x1 -> x0, starting transfers between devices: 4.84 us -> none  [exchange(): return lax.all_to_all(parts, axis, 0, 0, tiled=True)]
    ppermute x1, waiting for transfers between devices: 0.01 us -> 2.26 us  [local(): came = lax.ppermute(send, 'c', swap)]
  transfers between devices with their start and end apart: 3 -> 2, of which waited for: 2 -> 2; matrix products, arithmetic and copies ran while one was open for 1% -> 1% of each run, Pallas kernels for 0% -> 0%
where the time goes in v3:
time: 141 us
  blocking collectives  109 us (77%)
  starting transfers between devices  15.1 us (11%)
  Pallas kernels  11.4 us (8%)
  waiting for transfers between devices  3.46 us (2%)
    all_to_all x5, blocking collectives, exchange(): return lax.all_to_all(parts, axis, 0, 0, tiled=True)  109 us
    ppermute x1, starting transfers between devices, local(): came = lax.ppermute(send, 'c', swap)  8.44 us
    ppermute x1, starting transfers between devices, local(): other = lax.ppermute(own, 'c', swap)  6.63 us
    pallas_call x1, Pallas kernels, local(): pl.pallas_call(functools.partial(gram_kernel, layout), out_shape=(half_sh...  5.3 us
    pallas_call x1, Pallas kernels, local(): pl.pallas_call(dense_kernel, out_shape=jax.ShapeDtypeStruct((slices_here,...  3.24 us
  transfers between devices with their start and end apart: 2, of which 2 were waited for; matrix products, arithmetic and copies ran while one was open for 1% of the time, Pallas kernels for 0%

profile of v3, /device:TPU:1, one launch (start us, length us, event | category | flops | bytes accessed | tf_op | source)
XLA Modules:
  0.0 140.6 jit_solution(8970188974792286344)
XLA Ops:
  0.6 0.1 pad_add_fusion.place_ref
  0.7 3.2 %dense_blocks.1 = f32[4,1056,128]{2,1,0:T(8,128)} custom-call(f32[4,168,672]{2,1,0:T(8,128)} %field_ref.1, f32[168,128]{1,0:T(8,128)} %basis_ref.1), custom_call_target="tpu_custom_call" | custom-call | tf_op jit(solution)/shard_map/dense_blocks/pallas_call | solution.py:224
  4.0 26.3 %all_to_all.25.dense_ref = f32[4,1056,128]{2,1,0:T(8,128)S(1)} all-to-all(f32[4,1056,128]{2,1,0:T(8,128)} %dense_blocks.1), channel_id=1, replica_groups=mesh['x'=4,'y'=8,'z'=8,'c'=2] {'x'}, dimensions={0} | all-to-all | bytes 4325376 | tf_op jit(solution)/shard_map/all_to_all | solution.py:203
  30.3 5.3 %local_grams.1 = (f32[2048,128]{1,0:T(8,128)S(1)}, f32[2048,128]{1,0:T(8,128)S(1)}, f32[4,6,32,128]{3,2,1,0:T(8,128)S(1)}) custom-call(s32[2]{0:T(128)S(1)} %pad_add_fusion.place_ref, f32[4,1056,128]{2,1,0:T(8,128)S(1)} %all_to_all.25.dense_ref), custom_call_target="tpu_custom_call" | custom-call | tf_op jit(solution)/shard_map/local_grams/pallas_call | solution.py:241
  35.6 8.4 %collective-permute-start = (f32[2048,128]{1,0:T(8,128)S(1)}, f32[2048,128]{1,0:T(8,128)S(1)}, u32[]{:S(2)}, u32[]{:S(2)}) collective-permute-start(f32[2048,128]{1,0:T(8,128)S(1)} %get-tuple-element.13), channel_id=1, source_target_pairs={{0,1},{1,0},{2,3},{3,2},{4,5},{5,4},{6,7},{7,6},{8,9},{9,8},{10,11... | collective-permute-start | bytes 3145736 | tf_op jit(solution)/shard_map/ppermute | solution.py:259
  44.0 2.3 %collective-permute-done = f32[2048,128]{1,0:T(8,128)S(1)} collective-permute-done((f32[2048,128]{1,0:T(8,128)S(1)}, f32[2048,128]{1,0:T(8,128)S(1)}, u32[]{:S(2)}, u32[]{:S(2)}) %collective-permute-start) | collective-permute-done | bytes 1048608 | tf_op jit(solution)/shard_map/ppermute | solution.py:259
  46.3 0.1 add.3
  46.4 0.1 pad_maximum_fusion
  46.5 21.5 %all_to_all.26 = f32[4,704,128]{2,1,0:T(8,128)S(1)} all-to-all(f32[4,704,128]{2,1,0:T(8,128)S(1)} %pad_maximum_fusion), channel_id=1, replica_groups=mesh['x'=4,'y'=8,'z'=8,'c'=2] {'x'}, dimensions={0} | all-to-all | bytes 2883584 | tf_op jit(solution)/shard_map/all_to_all | solution.py:203
  68.1 28.6 %all_to_all.27 = f32[64,8,128]{2,1,0:T(8,128)S(1)} all-to-all(f32[64,8,128]{2,1,0:T(8,128)S(1)} %bitcast.22), channel_id=1, replica_groups=mesh['x'=4,'y'=8,'z'=8,'c'=2] {'y','z'}, dimensions={0} | all-to-all | bytes 524288 | tf_op jit(solution)/shard_map/all_to_all | solution.py:203
  96.6 0.1 reduce_sum.19
  96.7 18.4 %all_to_all.28 = f32[64,8,128]{2,1,0:T(8,128)S(1)} all-to-all(f32[64,8,128]{2,1,0:T(8,128)S(1)} %broadcast_in_dim.6), channel_id=1, replica_groups=mesh['x'=4,'y'=8,'z'=8,'c'=2] {'y','z'}, dimensions={0} | all-to-all | bytes 524288 | tf_op jit(solution)/shard_map/all_to_all | solution.py:203
  115.1 0.1 broadcast_in_dim.15
  115.2 13.7 %all_to_all.29 = f32[4,512,128]{2,1,0:T(8,128)S(1)} all-to-all(f32[4,512,128]{2,1,0:T(8,128)S(1)} %broadcast_in_dim.15), channel_id=1, replica_groups=mesh['x'=4,'y'=8,'z'=8,'c'=2] {'x'}, dimensions={0} | all-to-all | bytes 2097152 | tf_op jit(solution)/shard_map/all_to_all | solution.py:203
  128.9 6.6 %collective-permute-start.1 = (f32[2048,128]{1,0:T(8,128)S(1)}, f32[2048,128]{1,0:T(8,128)S(1)}, u32[]{:S(2)}, u32[]{:S(2)}) collective-permute-start(f32[2048,128]{1,0:T(8,128)S(1)} %bitcast.15), channel_id=1, source_target_pairs={{0,1},{1,0},{2,3},{3,2},{4,5},{5,4},{6,7},{7,6},{8,9},{9,8},{10,11... | collective-permute-start | bytes 3145736 | tf_op jit(solution)/shard_map/ppermute | solution.py:269
  135.6 1.0 copy.10
  136.6 1.2 collective-permute-done.1.other_ref
  137.8 2.8 %mirror.1 = (f32[168,672]{1,0:T(8,128)}, f32[672,672]{1,0:T(8,128)}) custom-call(s32[2]{0:T(128)S(1)} %pad_add_fusion.place_ref, f32[2048,128]{1,0:T(8,128)S(1)} %bitcast.16, f32[2048,128]{1,0:T(8,128)S(1)} %collective-permute-done.1.other_ref), custom_call_target="tpu_custom_call" | custom-call | tf_op jit(solution)/shard_map/mirror/pallas_call | solution.py:271
  (4 shorter events, 0.1 us)
Async XLA Ops:
  35.6 10.7 %collective-permute-start = (f32[2048,128]{1,0:T(8,128)S(1)}, f32[2048,128]{1,0:T(8,128)S(1)}, u32[]{:S(2)}, u32[]{:S(2)}) collective-permute-start(f32[2048,128]{1,0:T(8,128)S(1)} %get-tuple-element.13), channel_id=1, source_target_pairs={{0,1},{1,0},{2,3},{3,2},{4,5},{5,4},{6,7},{7,6},{8,9},{9,8},{10,11... | collective-permute-start | bytes 3145736 | tf_op jit(solution)/shard_map/ppermute | solution.py:259
  128.9 8.9 %collective-permute-start.1 = (f32[2048,128]{1,0:T(8,128)S(1)}, f32[2048,128]{1,0:T(8,128)S(1)}, u32[]{:S(2)}, u32[]{:S(2)}) collective-permute-start(f32[2048,128]{1,0:T(8,128)S(1)} %bitcast.15), channel_id=1, source_target_pairs={{0,1},{1,0},{2,3},{3,2},{4,5},{5,4},{6,7},{7,6},{8,9},{9,8},{10,11... | collective-permute-start | bytes 3145736 | tf_op jit(solution)/shard_map/ppermute | solution.py:269

commit v4 on v2

v4 whole, which is shorter than its diff:
```python
import functools

import jax
import jax.numpy as jnp
from jax import lax
from jax.experimental import pallas as pl
from jax.experimental.pallas import tpu as pltpu
from jax.sharding import Mesh, PartitionSpec as P

LANES = 128
FOLD = LANES // 2
VMEM = pl.BlockSpec(memory_space=pltpu.VMEM)
SMEM = pl.BlockSpec(memory_space=pltpu.SMEM)
ROOM = pltpu.CompilerParams(vmem_limit_bytes=24 << 20)


class Layout:
    def __init__(self, width, unit):
        self.width = width
        self.full = width // LANES
        self.left = width - self.full * LANES
        self.above = [0] * self.full
        row = 0
        for block in range(1, self.full):
            self.above[block] = row
            row += block * LANES
        self.strip = row
        row += self.left * (self.full + 1)
        split = -(-self.full // 2)
        self.fold = [(block // split, row + (block % split) * 3 * FOLD) for block in range(self.full)]
        self.used = [row + split * 3 * FOLD, row + (self.full - split) * 3 * FOLD]
        self.rows = -(-self.used[0] // unit) * unit


def halves(value):
    high = value.astype(jnp.bfloat16)
    low = (value - high.astype(jnp.float32)).astype(jnp.bfloat16)
    return high, low


def dot(a, b):
    return jnp.dot(a, b, preferred_element_type=jnp.float32)


def dot_rows(a, b):
    return lax.dot_general(a, b, (((1,), (1,)), ((), ())), preferred_element_type=jnp.float32)


def lane_below(rows):
    return lax.broadcasted_iota(jnp.int32, (rows, LANES), 1) < FOLD


def pack_gram(layout, product, packed, half):
    full, left, width = layout.full, layout.left, layout.width
    for start in range(0, width, 2 * LANES):
        columns = min(2 * LANES, width - start)
        last = start + columns == width
        group = product(width if last else start + columns, start, columns)
        for block in range(start // LANES, min(full, (start + columns) // LANES)):
            inside = slice(block * LANES - start, (block + 1) * LANES - start)
            above = block * LANES
            if above:
                packed[half, pl.ds(layout.above[block], above), :] = group[:above, inside]
            into, row = layout.fold[block]
            packed[into, pl.ds(row + half * FOLD, FOLD), :] = group[above : above + FOLD, inside]
            lower = group[above + FOLD : above + LANES, inside]
            corner = pl.ds(row + 2 * FOLD, FOLD)
            if half == 0:
                packed[into, corner, :] = pltpu.roll(lower, FOLD, 1)
            else:
                packed[into, corner, :] = jnp.where(lane_below(FOLD), packed[into, corner, :], lower)
        if last:
            strip = group[:, full * LANES - start :]
            for block in range(full):
                piece = strip[block * LANES : (block + 1) * LANES].T
                packed[half, pl.ds(layout.strip + block * left, left), :] = piece
            corner = pl.ds(layout.strip + full * left, left)
            packed[half, corner, :] = jnp.zeros((left, LANES), jnp.float32)
            packed[half, corner, 0:left] = strip[full * LANES :]
    spare = layout.rows - layout.used[half]
    if spare:
        packed[half, pl.ds(layout.used[half], spare), :] = jnp.zeros((spare, LANES), jnp.float32)


def dense_rows(rows, width):
    full = width // LANES
    left = width - full * LANES
    beside = LANES // left
    group = -(-rows // (8 * beside)) * 8
    return full, left, beside, group, rows * (full + 1) + group


def dense_kernel(field_ref, basis_ref, out_ref):
    blocks, rows, width = field_ref.shape
    full, left, beside, group, _ = dense_rows(rows, width)
    base = (full + 1) * rows
    for block in range(blocks):
        for part in range(full):
            out_ref[block, pl.ds(part * rows, rows), :] = field_ref[block, :, part * LANES : (part + 1) * LANES]
        out_ref[block, pl.ds(full * rows, rows), :] = basis_ref[...]
        for part in range(beside):
            some = min(group, rows - part * group)
            lanes = slice(part * left, (part + 1) * left)
            piece = field_ref[block, pl.ds(part * group, some), full * LANES : width]
            out_ref[block, pl.ds(base, some), lanes] = piece
            if some < group:
                out_ref[block, pl.ds(base + some, group - some), lanes] = jnp.zeros((group - some, left), jnp.float32)


def core_kernel(dense_ref, high_ref, low_ref, core_ref, field, basis):
    blocks = dense_ref.shape[0]
    first, width = field.shape
    rows = first // blocks
    full, left, beside, group, _ = dense_rows(rows, width)
    base = (full + 1) * rows
    for owner in range(blocks):
        own = owner * rows
        for part in range(full):
            field[pl.ds(own, rows), part * LANES : (part + 1) * LANES] = dense_ref[owner, pl.ds(part * rows, rows), :]
        basis[pl.ds(own, rows), :] = dense_ref[owner, pl.ds(full * rows, rows), :]
        for part in range(beside):
            some = min(group, rows - part * group)
            piece = dense_ref[owner, pl.ds(base, some), part * left : (part + 1) * left]
            field[pl.ds(own + part * group, some), full * LANES : width] = piece
    high, low = halves(field[...])
    high_ref[...] = high
    low_ref[...] = low
    basis_high, basis_low = halves(basis[...].T)
    core_ref[...] = dot(basis_high, high) + (dot(basis_high, low) + dot(basis_low, high))


def gram_kernel(layout, place_ref, high_ref, low_ref, core_ref, keep_ref, send_ref, left_side, right_side, packed):
    rank = core_ref.shape[0]
    high, low = halves(core_ref[...].T)
    left_side[:, 0:rank] = high
    left_side[:, rank : 2 * rank] = low
    right_side[:, 0:rank] = high
    right_side[:, rank : 2 * rank] = high

    def field_product(rows, start, columns):
        lh, ll = high_ref[pl.ds(0, rows), :], low_ref[pl.ds(0, rows), :]
        rh, rl = high_ref[pl.ds(start, columns), :], low_ref[pl.ds(start, columns), :]
        return dot_rows(lh, rh) + (dot_rows(lh, rl) + dot_rows(ll, rh))

    def core_product(rows, start, columns):
        here, there = pl.ds(0, rows), pl.ds(start, columns)
        both = dot_rows(left_side[here, :], right_side[there, :])
        return both + dot_rows(left_side[here, 0:rank], left_side[there, rank : 2 * rank])

    pack_gram(layout, field_product, packed, 0)
    pack_gram(layout, core_product, packed, 1)
    mine = place_ref[1]
    keep_ref[...] = packed[mine]
    send_ref[...] = packed[1 - mine]


def unpack(layout, packed, half, out_ref, scale):
    full, left = layout.full, layout.left
    for block in range(full):
        columns = pl.ds(block * LANES, LANES)
        for row in range(block):
            there = pl.ds(row * LANES, LANES)
            tile = packed[half, pl.ds(layout.above[block] + row * LANES, LANES), :] * scale
            out_ref[there, columns] = tile
            out_ref[columns, there] = tile.T
        into, row = layout.fold[block]
        upper = packed[into, pl.ds(row + half * FOLD, FOLD), :] * scale
        lower = packed[into, pl.ds(row + 2 * FOLD, FOLD), :] * scale
        if half == 0:
            lower = pltpu.roll(lower, FOLD, 1)
        turned = jnp.concatenate([upper, upper], axis=0).T[FOLD:]
        out_ref[pl.ds(block * LANES, FOLD), columns] = upper
        out_ref[pl.ds(block * LANES + FOLD, FOLD), columns] = jnp.where(lane_below(FOLD), turned, lower)
        tile = packed[half, pl.ds(layout.strip + block * left, left), :] * scale
        out_ref[pl.ds(full * LANES, left), columns] = tile
        out_ref[columns, pl.ds(full * LANES, left)] = tile.T
    corner = packed[half, pl.ds(layout.strip + full * left, left), :] * scale
    out_ref[pl.ds(full * LANES, left), pl.ds(full * LANES, left)] = corner[:, 0:left]


def unpack_kernel(layout, scale_one, scale_two, place_ref, own_ref, other_ref, one_ref, two_ref, packed, whole):
    rows = one_ref.shape[0]
    mine = place_ref[1]
    packed[mine] = own_ref[...]
    packed[1 - mine] = other_ref[...]
    unpack(layout, packed, 0, whole, scale_one)
    one_ref[...] = whole[pl.ds(pl.multiple_of(place_ref[0] * rows, 8), rows), :]
    unpack(layout, packed, 1, two_ref, scale_two)


def exchange(parts, axis):
    return lax.all_to_all(parts, axis, 0, 0, tiled=True)


def copies(value, count):
    return jnp.broadcast_to(value[None], (count,) + value.shape)


def cost(flops, moved):
    return pl.CostEstimate(flops=flops, transcendentals=0, bytes_accessed=moved)


def scatter_sum(value, axes, count):
    return jnp.sum(exchange(value.reshape(count, -1, LANES), axes), axis=0)


def gather(value, axes, count):
    return exchange(copies(value, count), axes).reshape(-1, LANES)


def local(sizes, tensor, basis):
    gx = sizes["x"]
    slices_here, rows_here, second = tensor.shape
    first = rows_here * gx
    rank = basis.shape[1]
    near, far = ("x", "zl"), ("y", "zh")
    near_count, far_count = gx * sizes["zl"], sizes["y"] * sizes["zh"]
    slices_all = slices_here * sizes["y"] * sizes["zh"] * sizes["zl"] * sizes["c"]
    layout = Layout(first, 8 * near_count * far_count)
    dense = dense_rows(rows_here, second)[-1]
    swap = [(i, sizes["c"] - 1 - i) for i in range(sizes["c"])]
    place = jnp.stack([lax.axis_index("x"), lax.axis_index("c")]).astype(jnp.int32)
    f32, bf16 = jnp.float32, jnp.bfloat16

    blocks = pl.pallas_call(
        dense_kernel,
        out_shape=jax.ShapeDtypeStruct((slices_here, dense, LANES), f32),
        in_specs=[VMEM, VMEM],
        out_specs=VMEM,
        compiler_params=ROOM,
        name="dense_blocks",
    )(tensor, basis)
    blocks, place = lax.optimization_barrier((blocks, place))
    blocks = exchange(blocks, "x")
    high, low, core = pl.pallas_call(
        core_kernel,
        out_shape=(
            jax.ShapeDtypeStruct((first, second), bf16),
            jax.ShapeDtypeStruct((first, second), bf16),
            jax.ShapeDtypeStruct((rank, second), f32),
        ),
        in_specs=[VMEM],
        out_specs=(VMEM, VMEM, VMEM),
        scratch_shapes=[pltpu.VMEM((first, second), f32), pltpu.VMEM((first, rank), f32)],
        compiler_params=ROOM,
        cost_estimate=cost(6 * rank * first * second, 8 * first * second),
        name="core_of_slice",
    )(blocks)
    core_parts = exchange(core.reshape(gx, rank // gx, second), "x")
    half_shape = jax.ShapeDtypeStruct((layout.rows, LANES), f32)
    keep, send = pl.pallas_call(
        functools.partial(gram_kernel, layout),
        out_shape=(half_shape, half_shape),
        in_specs=[SMEM, VMEM, VMEM, VMEM],
        out_specs=(VMEM, VMEM),
        scratch_shapes=[
            pltpu.VMEM((second, 2 * rank), bf16),
            pltpu.VMEM((second, 2 * rank), bf16),
            pltpu.VMEM((2, layout.rows, LANES), f32),
        ],
        compiler_params=ROOM,
        cost_estimate=cost(4 * first * first * second, 12 * first * second),
        name="local_grams",
    )(place, high, low, core)

    send, core_parts = lax.optimization_barrier((send, core_parts))
    came = lax.ppermute(send, "c", swap)
    core_out = jnp.transpose(core_parts, (1, 0, 2))
    part = scatter_sum(scatter_sum(keep + came, near, near_count), far, far_count)
    own = gather(gather(part, far, far_count), near, near_count)
    other = lax.ppermute(own, "c", swap)

    gram_one, gram_two = pl.pallas_call(
        functools.partial(unpack_kernel, layout, 1.0 / (slices_all * second), 1.0 / (slices_all * rank)),
        out_shape=(
            jax.ShapeDtypeStruct((rows_here, first), f32),
            jax.ShapeDtypeStruct((second, second), f32),
        ),
        in_specs=[SMEM, VMEM, VMEM],
        out_specs=(VMEM, VMEM),
        scratch_shapes=[pltpu.VMEM((2, layout.rows, LANES), f32), pltpu.VMEM((first, first), f32)],
        compiler_params=ROOM,
        name="mirror",
    )(place, own, other)
    return gram_one, core_out, gram_two


def solution(mesh):
    gx, rest = mesh.devices.shape
    sizes = {"x": gx, "y": 8, "zh": rest // 32, "zl": 2, "c": 2}
    fine = Mesh(mesh.devices.reshape(tuple(sizes.values())), tuple(sizes))
    spread = ("y", "zh", "zl", "c")
    in_specs = (P(spread, "x", None), P("x", None))
    out_specs = (P("x", None), P("x", spread, None), P())
    return jax.shard_map(
        functools.partial(local, sizes), mesh=fine, in_specs=in_specs, out_specs=out_specs, check_vma=False
    )
```

time: 142 us -> 140 us (0.986)
  waiting for transfers between devices: 22.3 us -> 4.94 us
  blocking collectives: 84.7 us -> 101 us
  local copies, waits for them, and re-layouts: 1.09 us -> 5.72 us
  Pallas kernels: 11.4 us -> 8.21 us
  starting transfers between devices: 21 us -> 19.1 us
    all_to_all x1, waiting for transfers between devices: 21.2 us -> 1.41 us  [exchange(): return lax.all_to_all(parts, axis, 0, 0, tiled=True)]
    all_to_all x5, blocking collectives: 84.7 us -> 101 us  [exchange(): return lax.all_to_all(parts, axis, 0, 0, tiled=True)]
    unnamed x1 -> x9, local copies, waits for them, and re-layouts: 1 us -> 5.64 us
    ppermute x1, waiting for transfers between devices: 0.01 us -> 2.26 us  [local(): came = lax.ppermute(send, 'c', swap)]
    pallas_call x1 -> x2, Pallas kernels: 3.87 us -> 1.85 us  [the longest x1 1.67 us: local(): pl.pallas_call(core_kernel, out_shape=(jax.ShapeDtypeStruct((first, secon...]
  transfers between devices with their start and end apart: 3 -> 3, of which waited for: 2 -> 3; matrix products, arithmetic and copies ran while one was open for 1% -> 1% of each run, Pallas kernels for 0% -> 3%
where the time goes in v4:
time: 140 us; the launch traced here: 139 us
  blocking collectives  101 us (72%)
  starting transfers between devices  19.1 us (14%)
  Pallas kernels  8.21 us (6%)
  local copies, waits for them, and re-layouts  5.72 us (4%)
  waiting for transfers between devices  4.94 us (4%)
    all_to_all x5, blocking collectives, exchange(): return lax.all_to_all(parts, axis, 0, 0, tiled=True)  101 us
    ppermute x1, starting transfers between devices, local(): came = lax.ppermute(send, 'c', swap)  8.76 us
    ppermute x1, starting transfers between devices, local(): other = lax.ppermute(own, 'c', swap)  6.83 us
    unnamed x9, local copies, waits for them, and re-layouts  5.64 us
    pallas_call x1, Pallas kernels, local(): pl.pallas_call(functools.partial(gram_kernel, layout), out_shape=(half_sh...  3.55 us
    all_to_all x1, starting transfers between devices, exchange(): return lax.all_to_all(parts, axis, 0, 0, tiled=True)  3.46 us
    pallas_call x1, Pallas kernels, local(): pl.pallas_call(functools.partial(unpack_kernel, layout, 1.0 / (slices_all...  2.81 us
  transfers between devices with their start and end apart: 3, of which 3 were waited for; matrix products, arithmetic and copies ran while one was open for 1% of the time, Pallas kernels for 3%

profile of v4, /device:TPU:1, one launch (start us, length us, event | category | flops | bytes accessed | tf_op | source)
XLA Modules:
  0.0 139.4 jit_solution(15707959098828632168)
XLA Ops:
  0.6 0.1 pad_add_fusion.place_ref
  0.7 0.0 copy-start
  0.7 1.6 %copy-done = f32[4,168,672]{2,1,0:T(8,128)S(1)} copy-done((f32[4,168,672]{2,1,0:T(8,128)S(1)}, f32[4,168,672]{2,1,0:T(8,128)}, u32[]{:S(2)}) %copy-start) | copy-done | bytes 1806360
  2.3 0.0 copy-start.1
  2.3 0.9 copy-done.1
  3.2 0.2 dense_blocks.1
  3.4 26.9 %all_to_all.30.dense_ref = f32[4,1056,128]{2,1,0:T(8,128)S(1)} all-to-all(f32[4,1056,128]{2,1,0:T(8,128)S(1)} %dense_blocks.1), channel_id=1, replica_groups=mesh['x'=4,'y'=8,'zh'=4,'zl'=2,'c'=2] {'x'}, dimensions={0} | all-to-all | bytes 4325376 | tf_op jit(solution)/shard_map/all_to_all | solution.py:192
  30.3 1.7 %core_of_slice.1 = (bf16[672,672]{1,0:T(8,128)(2,1)S(1)}, bf16[672,672]{1,0:T(8,128)(2,1)S(1)}, f32[128,672]{1,0:T(8,128)}) custom-call(f32[4,1056,128]{2,1,0:T(8,128)S(1)} %all_to_all.30.dense_ref), custom_call_target="tpu_custom_call" | custom-call | flops 346816512 | bytes 3612672 | tf_op jit(solution)/shard_map/core_of_slice/pallas_call | solution.py:235
  31.9 0.0 copy-start.2
  31.9 1.0 copy-done.2
  32.9 3.5 %all-to-all-start.1 = ((f32[4,32,672]{2,1,0:T(8,128)}), f32[4,32,672]{2,1,0:T(8,128)S(1)}, u32[]{:S(2)}, u32[]{:S(2)}) async-start(f32[4,32,672]{2,1,0:T(8,128)} %bitcast.2), calls=%async_computation.1 | async-start | bytes 786432 | tf_op jit(solution)/shard_map/all_to_all | solution.py:192
  36.4 0.0 copy-start.3
  36.4 1.2 copy-done.3
  37.6 3.6 %local_grams.1 = (f32[2048,128]{1,0:T(8,128)S(1)}, f32[2048,128]{1,0:T(8,128)S(1)}) custom-call(s32[2]{0:T(128)S(1)} %pad_add_fusion.place_ref, bf16[672,672]{1,0:T(8,128)(2,1)S(1)} %get-tuple-element.16.high_ref, bf16[672,672]{1,0:T(8,128)(2,1)S(1)} %copy-done.3, f32[128,672]{1,0:T(8,128)} %get-tuple-element.18.core_ref), custom_call_target="tpu_custom_call" | custom-call | flops 1213857792 | bytes 5419008 | tf_op jit(solution)/shard_map/local_grams/pallas_call | solution.py:251
  41.2 1.4 %all-to-all-done.1 = f32[4,32,672]{2,1,0:T(8,128)S(1)} async-done(((f32[4,32,672]{2,1,0:T(8,128)}), f32[4,32,672]{2,1,0:T(8,128)S(1)}, u32[]{:S(2)}, u32[]{:S(2)}) %all-to-all-start.1) | async-done | bytes 344096 | tf_op jit(solution)/shard_map/all_to_all | solution.py:192
  42.6 8.8 %collective-permute-start = (f32[2048,128]{1,0:T(8,128)S(1)}, f32[2048,128]{1,0:T(8,128)S(1)}, u32[]{:S(2)}, u32[]{:S(2)}) collective-permute-start(f32[2048,128]{1,0:T(8,128)S(1)} %get-tuple-element.21), channel_id=1, source_target_pairs={{0,1},{1,0},{2,3},{3,2},{4,5},{5,4},{6,7},{7,6},{8,9},{9,8},{10,11... | collective-permute-start | bytes 3145736 | tf_op jit(solution)/shard_map/ppermute | solution.py:267
  51.3 2.3 %collective-permute-done = f32[2048,128]{1,0:T(8,128)S(1)} collective-permute-done((f32[2048,128]{1,0:T(8,128)S(1)}, f32[2048,128]{1,0:T(8,128)S(1)}, u32[]{:S(2)}, u32[]{:S(2)}) %collective-permute-start) | collective-permute-done | bytes 1048608 | tf_op jit(solution)/shard_map/ppermute | solution.py:267
  53.6 0.1 add.3
  53.7 18.6 %all_to_all.31 = f32[8,256,128]{2,1,0:T(8,128)S(1)} all-to-all(f32[8,256,128]{2,1,0:T(8,128)S(1)} %bitcast.10), channel_id=1, replica_groups=mesh['x'=4,'y'=8,'zh'=4,'zl'=2,'c'=2] {'x','zl'}, dimensions={0} | all-to-all | bytes 2097152 | tf_op jit(solution)/shard_map/all_to_all | solution.py:192
  72.3 0.1 reduce_sum.18
  72.4 26.0 %all_to_all.32 = f32[32,8,128]{2,1,0:T(8,128)S(1)} all-to-all(f32[32,8,128]{2,1,0:T(8,128)S(1)} %bitcast.12), channel_id=1, replica_groups=mesh['x'=4,'y'=8,'zh'=4,'zl'=2,'c'=2] {'y','zh'}, dimensions={0} | all-to-all | bytes 262144 | tf_op jit(solution)/shard_map/all_to_all | solution.py:192
  98.4 14.4 %all_to_all.33 = f32[32,8,128]{2,1,0:T(8,128)S(1)} all-to-all(f32[32,8,128]{2,1,0:T(8,128)S(1)} %broadcast_in_dim.6), channel_id=1, replica_groups=mesh['x'=4,'y'=8,'zh'=4,'zl'=2,'c'=2] {'y','zh'}, dimensions={0} | all-to-all | bytes 262144 | tf_op jit(solution)/shard_map/all_to_all | solution.py:192
  112.8 0.1 broadcast_in_dim.15
  112.9 14.6 %all_to_all.34 = f32[8,256,128]{2,1,0:T(8,128)S(1)} all-to-all(f32[8,256,128]{2,1,0:T(8,128)S(1)} %broadcast_in_dim.15), channel_id=1, replica_groups=mesh['x'=4,'y'=8,'zh'=4,'zl'=2,'c'=2] {'x','zl'}, dimensions={0} | all-to-all | bytes 2097152 | tf_op jit(solution)/shard_map/all_to_all | solution.py:192
  127.5 6.8 %collective-permute-start.1 = (f32[2048,128]{1,0:T(8,128)S(1)}, f32[2048,128]{1,0:T(8,128)S(1)}, u32[]{:S(2)}, u32[]{:S(2)}) collective-permute-start(f32[2048,128]{1,0:T(8,128)S(1)} %bitcast.8), channel_id=1, source_target_pairs={{0,1},{1,0},{2,3},{3,2},{4,5},{5,4},{6,7},{7,6},{8,9},{9,8},{10,11... | collective-permute-start | bytes 3145736 | tf_op jit(solution)/shard_map/ppermute | solution.py:271
  134.4 1.0 copy.7
  135.4 1.3 collective-permute-done.1.other_ref
  136.6 2.8 %mirror.1 = (f32[168,672]{1,0:T(8,128)}, f32[672,672]{1,0:T(8,128)}) custom-call(s32[2]{0:T(128)S(1)} %pad_add_fusion.place_ref, f32[2048,128]{1,0:T(8,128)S(1)} %bitcast.9, f32[2048,128]{1,0:T(8,128)S(1)} %collective-permute-done.1.other_ref), custom_call_target="tpu_custom_call" | custom-call | tf_op jit(solution)/shard_map/mirror/pallas_call | solution.py:273
  (2 shorter events, 0.0 us)
Async XLA Ops:
  0.7 1.6 %copy-start = (f32[4,168,672]{2,1,0:T(8,128)S(1)}, f32[4,168,672]{2,1,0:T(8,128)}, u32[]{:S(2)}) copy-start(f32[4,168,672]{2,1,0:T(8,128)} %field_ref.1) | copy-start | bytes 5419012
  2.3 0.9 copy-start.1
  31.9 1.0 copy-start.2
  32.9 9.7 %all-to-all-start.1 = ((f32[4,32,672]{2,1,0:T(8,128)}), f32[4,32,672]{2,1,0:T(8,128)S(1)}, u32[]{:S(2)}, u32[]{:S(2)}) async-start(f32[4,32,672]{2,1,0:T(8,128)} %bitcast.2), calls=%async_computation.1 | async-start | bytes 786432 | tf_op jit(solution)/shard_map/all_to_all | solution.py:192
  36.4 1.2 copy-start.3
  42.6 11.0 %collective-permute-start = (f32[2048,128]{1,0:T(8,128)S(1)}, f32[2048,128]{1,0:T(8,128)S(1)}, u32[]{:S(2)}, u32[]{:S(2)}) collective-permute-start(f32[2048,128]{1,0:T(8,128)S(1)} %get-tuple-element.21), channel_id=1, source_target_pairs={{0,1},{1,0},{2,3},{3,2},{4,5},{5,4},{6,7},{7,6},{8,9},{9,8},{10,11... | collective-permute-start | bytes 3145736 | tf_op jit(solution)/shard_map/ppermute | solution.py:267
  127.5 9.1 %collective-permute-start.1 = (f32[2048,128]{1,0:T(8,128)S(1)}, f32[2048,128]{1,0:T(8,128)S(1)}, u32[]{:S(2)}, u32[]{:S(2)}) collective-permute-start(f32[2048,128]{1,0:T(8,128)S(1)} %bitcast.8), channel_id=1, source_target_pairs={{0,1},{1,0},{2,3},{3,2},{4,5},{5,4},{6,7},{7,6},{8,9},{9,8},{10,11... | collective-permute-start | bytes 3145736 | tf_op jit(solution)/shard_map/ppermute | solution.py:271

commit v5 on v4

--- a/solution.py
+++ b/solution.py
@@ -107,9 +107,13 @@
                 out_ref[block, pl.ds(base + some, group - some), lanes] = jnp.zeros((group - some, left), jnp.float32)
 
 
-def core_kernel(dense_ref, high_ref, low_ref, core_ref, field, basis):
+def gram_kernel(
+    layout, place_ref, dense_ref, keep_ref, send_ref, core_ref,
+    field, basis, field_high, field_low, left_side, right_side, packed,
+):
     blocks = dense_ref.shape[0]
     first, width = field.shape
+    rank = basis.shape[1]
     rows = first // blocks
     full, left, beside, group, _ = dense_rows(rows, width)
     base = (full + 1) * rows
@@ -123,23 +127,20 @@
             piece = dense_ref[owner, pl.ds(base, some), part * left : (part + 1) * left]
             field[pl.ds(own + part * group, some), full * LANES : width] = piece
     high, low = halves(field[...])
-    high_ref[...] = high
-    low_ref[...] = low
+    field_high[...] = high
+    field_low[...] = low
     basis_high, basis_low = halves(basis[...].T)
-    core_ref[...] = dot(basis_high, high) + (dot(basis_high, low) + dot(basis_low, high))
-
-
-def gram_kernel(layout, place_ref, high_ref, low_ref, core_ref, keep_ref, send_ref, left_side, right_side, packed):
-    rank = core_ref.shape[0]
-    high, low = halves(core_ref[...].T)
+    core = dot(basis_high, high) + (dot(basis_high, low) + dot(basis_low, high))
+    core_ref[...] = core
+    high, low = halves(core.T)
     left_side[:, 0:rank] = high
     left_side[:, rank : 2 * rank] = low
     right_side[:, 0:rank] = high
     right_side[:, rank : 2 * rank] = high
 
     def field_product(rows, start, columns):
-        lh, ll = high_ref[pl.ds(0, rows), :], low_ref[pl.ds(0, rows), :]
-        rh, rl = high_ref[pl.ds(start, columns), :], low_ref[pl.ds(start, columns), :]
+        lh, ll = field_high[pl.ds(0, rows), :], field_low[pl.ds(0, rows), :]
+        rh, rl = field_high[pl.ds(start, columns), :], field_low[pl.ds(start, columns), :]
         return dot_rows(lh, rh) + (dot_rows(lh, rl) + dot_rows(ll, rh))
 
     def core_product(rows, start, columns):
@@ -152,6 +153,22 @@
     mine = place_ref[1]
     keep_ref[...] = packed[mine]
     send_ref[...] = packed[1 - mine]
+
+
+def parts_kernel(place_ref, core_ref, after_ref, *out_refs):
+    owned = out_refs[0].shape[0]
+    for step, out_ref in enumerate(out_refs):
+        owner = lax.rem(place_ref[0] + step, len(out_refs))
+        out_ref[...] = core_ref[pl.ds(pl.multiple_of(owner * owned, 8), owned), :]
+
+
+def rows_kernel(place_ref, *refs):
+    came, (out_ref, ordered) = refs[:-2], refs[-2:]
+    count = len(came)
+    for step, ref in enumerate(came):
+        ordered[lax.rem(place_ref[0] + count - step, count)] = ref[...]
+    for owner in range(count):
+        out_ref[:, owner, :] = ordered[owner]
 
 
 def unpack(layout, packed, half, out_ref, scale):
@@ -232,41 +249,54 @@
     )(tensor, basis)
     blocks, place = lax.optimization_barrier((blocks, place))
     blocks = exchange(blocks, "x")
-    high, low, core = pl.pallas_call(
-        core_kernel,
-        out_shape=(
-            jax.ShapeDtypeStruct((first, second), bf16),
-            jax.ShapeDtypeStruct((first, second), bf16),
-            jax.ShapeDtypeStruct((rank, second), f32),
-        ),
-        in_specs=[VMEM],
+    half_shape = jax.ShapeDtypeStruct((layout.rows, LANES), f32)
+    keep, send, core = pl.pallas_call(
+        functools.partial(gram_kernel, layout),
+        out_shape=(half_shape, half_shape, jax.ShapeDtypeStruct((rank, second), f32)),
+        in_specs=[SMEM, VMEM],
         out_specs=(VMEM, VMEM, VMEM),
-        scratch_shapes=[pltpu.VMEM((first, second), f32), pltpu.VMEM((first, rank), f32)],
-        compiler_params=ROOM,
-        cost_estimate=cost(6 * rank * first * second, 8 * first * second),
-        name="core_of_slice",
-    )(blocks)
-    core_parts = exchange(core.reshape(gx, rank // gx, second), "x")
-    half_shape = jax.ShapeDtypeStruct((layout.rows, LANES), f32)
-    keep, send = pl.pallas_call(
-        functools.partial(gram_kernel, layout),
-        out_shape=(half_shape, half_shape),
-        in_specs=[SMEM, VMEM, VMEM, VMEM],
-        out_specs=(VMEM, VMEM),
         scratch_shapes=[
+            pltpu.VMEM((first, second), f32),
+            pltpu.VMEM((first, rank), f32),
+            pltpu.VMEM((first, second), bf16),
+            pltpu.VMEM((first, second), bf16),
             pltpu.VMEM((second, 2 * rank), bf16),
             pltpu.VMEM((second, 2 * rank), bf16),
             pltpu.VMEM((2, layout.rows, LANES), f32),
         ],
         compiler_params=ROOM,
-        cost_estimate=cost(4 * first * first * second, 12 * first * second),
+        cost_estimate=cost(5 * first * first * second, 12 * first * second),
         name="local_grams",
-    )(place, high, low, core)
-
-    send, core_parts = lax.optimization_barrier((send, core_parts))
+    )(place, blocks)
+
     came = lax.ppermute(send, "c", swap)
-    core_out = jnp.transpose(core_parts, (1, 0, 2))
-    part = scatter_sum(scatter_sum(keep + came, near, near_count), far, far_count)
+    part = scatter_sum(keep + came, near, near_count)
+    owned = rank // gx
+    core_parts = pl.pallas_call(
+        parts_kernel,
+        out_shape=[jax.ShapeDtypeStruct((owned, second), f32)] * gx,
+        in_specs=[SMEM, VMEM, VMEM],
+        out_specs=[VMEM] * gx,
+        compiler_params=ROOM,
+        cost_estimate=cost(rank * second, 8 * rank * second),
+        name="core_parts",
+    )(place, core, part[:8])
+    came_core = [core_parts[0]]
+    for step in range(1, gx):
+        shift = [(i, (i + step) % gx) for i in range(gx)]
+        came_core.append(lax.ppermute(core_parts[step], "x", shift))
+    part = scatter_sum(part, far, far_count)
+    part, *came_core = lax.optimization_barrier((part, *came_core))
+    core_out = pl.pallas_call(
+        rows_kernel,
+        out_shape=jax.ShapeDtypeStruct((owned, gx, second), f32),
+        in_specs=[SMEM] + [VMEM] * gx,
+        out_specs=VMEM,
+        scratch_shapes=[pltpu.VMEM((gx, owned, second), f32)],
+        compiler_params=ROOM,
+        cost_estimate=cost(rank * second, 8 * rank * second),
+        name="core_rows",
+    )(place, *came_core)
     own = gather(gather(part, far, far_count), near, near_count)
     other = lax.ppermute(own, "c", swap)
 

time: 140 us -> 142 us (1.014)
  starting transfers between devices: 19.1 us -> 38.4 us
  blocking collectives: 101 us -> 83.2 us
  local copies, waits for them, and re-layouts: 5.72 us -> 3.24 us
  waiting for transfers between devices: 4.94 us -> 6.38 us
    all_to_all x5 -> x4, blocking collectives: 101 us -> 83.2 us  [exchange(): return lax.all_to_all(parts, axis, 0, 0, tiled=True)]
    all_to_all x1, starting transfers between devices: 3.46 us -> 14.8 us  [exchange(): return lax.all_to_all(parts, axis, 0, 0, tiled=True)]
    ppermute x0 -> x3, starting transfers between devices: none -> 8.67 us  [local(): came_core.append(lax.ppermute(core_parts[step], 'x', shift))]
    unnamed x9 -> x4, local copies, waits for them, and re-layouts: 5.64 us -> 2.47 us
    ppermute x0 -> x3, waiting for transfers between devices: none -> 1.81 us  [local(): came_core.append(lax.ppermute(core_parts[step], 'x', shift))]
  transfers between devices with their start and end apart: 3 -> 6, of which waited for: 3 -> 4; matrix products, arithmetic and copies ran while one was open for 1% -> 1% of each run, Pallas kernels for 3% -> 1%
where the time goes in v5:
time: 142 us
  blocking collectives  83.2 us (59%)
  starting transfers between devices  38.4 us (27%)
  Pallas kernels  8.76 us (6%)
  waiting for transfers between devices  6.38 us (4%)
  local copies, waits for them, and re-layouts  3.24 us (2%)
    all_to_all x4, blocking collectives, exchange(): return lax.all_to_all(parts, axis, 0, 0, tiled=True)  83.2 us
    all_to_all x1, starting transfers between devices, exchange(): return lax.all_to_all(parts, axis, 0, 0, tiled=True)  14.8 us
    ppermute x3, starting transfers between devices, local(): came_core.append(lax.ppermute(core_parts[step], 'x', shift))  8.67 us
    ppermute x1, starting transfers between devices, local(): came = lax.ppermute(send, 'c', swap)  7.63 us
    ppermute x1, starting transfers between devices, local(): other = lax.ppermute(own, 'c', swap)  7.31 us
    pallas_call x1, Pallas kernels, local(): pl.pallas_call(functools.partial(gram_kernel, layout), out_shape=(half_sh...  3.8 us
  transfers between devices with their start and end apart: 6, of which 4 were waited for; matrix products, arithmetic and copies ran while one was open for 1% of the time, Pallas kernels for 1%

profile of v5, /device:TPU:1, one launch (start us, length us, event | category | flops | bytes accessed | tf_op | source)
XLA Modules:
  0.0 141.6 jit_solution(9093982703045753630)
XLA Ops:
  0.6 0.1 pad_add_fusion.place_ref
  0.7 0.0 copy-start
  0.7 1.6 %copy-done = f32[4,168,672]{2,1,0:T(8,128)S(1)} copy-done((f32[4,168,672]{2,1,0:T(8,128)S(1)}, f32[4,168,672]{2,1,0:T(8,128)}, u32[]{:S(2)}) %copy-start) | copy-done | bytes 1806360
  2.3 0.0 copy-start.1
  2.3 0.9 copy-done.1
  3.2 0.2 dense_blocks.1
  3.4 26.9 %all_to_all.25.dense_ref = f32[4,1056,128]{2,1,0:T(8,128)S(1)} all-to-all(f32[4,1056,128]{2,1,0:T(8,128)S(1)} %dense_blocks.1), channel_id=1, replica_groups=mesh['x'=4,'y'=8,'zh'=4,'zl'=2,'c'=2] {'x'}, dimensions={0} | all-to-all | bytes 4325376 | tf_op jit(solution)/shard_map/all_to_all | solution.py:209
  30.3 3.8 %local_grams.1 = (f32[2048,128]{1,0:T(8,128)S(1)}, f32[2048,128]{1,0:T(8,128)S(1)}, f32[128,672]{1,0:T(8,128)S(1)}) custom-call(s32[2]{0:T(128)S(1)} %pad_add_fusion.place_ref, f32[4,1056,128]{2,1,0:T(8,128)S(1)} %all_to_all.25.dense_ref), custom_call_target="tpu_custom_call" | custom-call | flops 1517322240 | bytes 5419008 | tf_op jit(solution)/shard_map/local_grams/pallas_call | solution.py:253
  34.1 7.6 %collective-permute-start = (f32[2048,128]{1,0:T(8,128)S(1)}, f32[2048,128]{1,0:T(8,128)S(1)}, u32[]{:S(2)}, u32[]{:S(2)}) collective-permute-start(f32[2048,128]{1,0:T(8,128)S(1)} %get-tuple-element.22), channel_id=1, source_target_pairs={{0,1},{1,0},{2,3},{3,2},{4,5},{5,4},{6,7},{7,6},{8,9},{9,8},{10,11... | collective-permute-start | bytes 3145736 | tf_op jit(solution)/shard_map/ppermute | solution.py:272
  41.7 2.3 %collective-permute-done = f32[2048,128]{1,0:T(8,128)S(1)} collective-permute-done((f32[2048,128]{1,0:T(8,128)S(1)}, f32[2048,128]{1,0:T(8,128)S(1)}, u32[]{:S(2)}, u32[]{:S(2)}) %collective-permute-start) | collective-permute-done | bytes 1048608 | tf_op jit(solution)/shard_map/ppermute | solution.py:272
  44.0 0.1 add.3
  44.1 18.6 %all_to_all.26 = f32[8,256,128]{2,1,0:T(8,128)S(1)} all-to-all(f32[8,256,128]{2,1,0:T(8,128)S(1)} %bitcast.8), channel_id=1, replica_groups=mesh['x'=4,'y'=8,'zh'=4,'zl'=2,'c'=2] {'x','zl'}, dimensions={0} | all-to-all | bytes 2097152 | tf_op jit(solution)/shard_map/all_to_all | solution.py:209
  62.7 0.7 reduce_sum.18
  63.4 14.8 %all-to-all-start.2 = ((f32[32,8,128]{2,1,0:T(8,128)}), f32[32,8,128]{2,1,0:T(8,128)S(1)}, u32[]{:S(2)}, u32[]{:S(2)}) async-start(f32[32,8,128]{2,1,0:T(8,128)} %bitcast.3), calls=%async_computation.2 | async-start | bytes 262144 | tf_op jit(solution)/shard_map/all_to_all | solution.py:209
  78.2 0.7 slice.4.after_ref
  78.9 0.6 core_parts.1
  79.5 1.9 %collective-permute-start.1 = (f32[32,672]{1,0:T(8,128)S(1)}, f32[32,672]{1,0:T(8,128)S(1)}, u32[]{:S(2)}, u32[]{:S(2)}) collective-permute-start(f32[32,672]{1,0:T(8,128)S(1)} %get-tuple-element.25), channel_id=1, source_target_pairs={{0,128},{128,256},{256,384},{384,0},{1,129},{129,257},{257,385},{3... | collective-permute-start | bytes 258056 | tf_op jit(solution)/shard_map/ppermute | solution.py:287
  81.4 4.0 %collective-permute-start.2 = (f32[32,672]{1,0:T(8,128)S(1)}, f32[32,672]{1,0:T(8,128)S(1)}, u32[]{:S(2)}, u32[]{:S(2)}) collective-permute-start(f32[32,672]{1,0:T(8,128)S(1)} %get-tuple-element.26), channel_id=1, source_target_pairs={{0,256},{128,384},{256,0},{384,128},{1,257},{129,385},{257,1},{385... | collective-permute-start | bytes 258056 | tf_op jit(solution)/shard_map/ppermute | solution.py:287
  85.4 2.8 %collective-permute-start.3 = (f32[32,672]{1,0:T(8,128)S(1)}, f32[32,672]{1,0:T(8,128)S(1)}, u32[]{:S(2)}, u32[]{:S(2)}) collective-permute-start(f32[32,672]{1,0:T(8,128)S(1)} %get-tuple-element.27), channel_id=1, source_target_pairs={{0,384},{128,0},{256,128},{384,256},{1,385},{129,1},{257,129},{385... | collective-permute-start | bytes 258056 | tf_op jit(solution)/shard_map/ppermute | solution.py:287
  88.2 1.4 %all-to-all-done.2 = f32[32,8,128]{2,1,0:T(8,128)S(1)} async-done(((f32[32,8,128]{2,1,0:T(8,128)}), f32[32,8,128]{2,1,0:T(8,128)S(1)}, u32[]{:S(2)}, u32[]{:S(2)}) %all-to-all-start.2) | async-done | bytes 131104 | tf_op jit(solution)/shard_map/all_to_all | solution.py:209
  89.6 0.0 collective-permute-done.1.refs_1_
  89.6 0.0 collective-permute-done.2.refs_2_
  89.6 1.8 %collective-permute-done.3.refs_3_ = f32[32,672]{1,0:T(8,128)S(1)} collective-permute-done((f32[32,672]{1,0:T(8,128)S(1)}, f32[32,672]{1,0:T(8,128)S(1)}, u32[]{:S(2)}, u32[]{:S(2)}) %collective-permute-start.3) | collective-permute-done | bytes 86048 | tf_op jit(solution)/shard_map/ppermute | solution.py:287
  91.5 22.4 %all_to_all.27 = f32[32,8,128]{2,1,0:T(8,128)S(1)} all-to-all(f32[32,8,128]{2,1,0:T(8,128)S(1)} %broadcast_in_dim.6), channel_id=1, replica_groups=mesh['x'=4,'y'=8,'zh'=4,'zl'=2,'c'=2] {'y','zh'}, dimensions={0} | all-to-all | bytes 262144 | tf_op jit(solution)/shard_map/all_to_all | solution.py:209
  113.9 0.1 broadcast_in_dim.15
  113.9 15.3 %all_to_all.28 = f32[8,256,128]{2,1,0:T(8,128)S(1)} all-to-all(f32[8,256,128]{2,1,0:T(8,128)S(1)} %broadcast_in_dim.15), channel_id=1, replica_groups=mesh['x'=4,'y'=8,'zh'=4,'zl'=2,'c'=2] {'x','zl'}, dimensions={0} | all-to-all | bytes 2097152 | tf_op jit(solution)/shard_map/all_to_all | solution.py:209
  129.2 7.3 %collective-permute-start.4 = (f32[2048,128]{1,0:T(8,128)S(1)}, f32[2048,128]{1,0:T(8,128)S(1)}, u32[]{:S(2)}, u32[]{:S(2)}) collective-permute-start(f32[2048,128]{1,0:T(8,128)S(1)} %bitcast.6), channel_id=1, source_target_pairs={{0,1},{1,0},{2,3},{3,2},{4,5},{5,4},{6,7},{7,6},{8,9},{9,8},{10,11... | collective-permute-start | bytes 3145736 | tf_op jit(solution)/shard_map/ppermute | solution.py:301
  136.5 1.4 core_rows.1
  137.9 0.9 collective-permute-done.4.other_ref
  138.8 2.8 %mirror.1 = (f32[168,672]{1,0:T(8,128)}, f32[672,672]{1,0:T(8,128)}) custom-call(s32[2]{0:T(128)S(1)} %pad_add_fusion.place_ref, f32[2048,128]{1,0:T(8,128)S(1)} %bitcast.7, f32[2048,128]{1,0:T(8,128)S(1)} %collective-permute-done.4.other_ref), custom_call_target="tpu_custom_call" | custom-call | tf_op jit(solution)/shard_map/mirror/pallas_call | solution.py:303
  (2 shorter events, 0.0 us)
Async XLA Ops:
  0.7 1.6 %copy-start = (f32[4,168,672]{2,1,0:T(8,128)S(1)}, f32[4,168,672]{2,1,0:T(8,128)}, u32[]{:S(2)}) copy-start(f32[4,168,672]{2,1,0:T(8,128)} %field_ref.1) | copy-start | bytes 5419012
  2.3 0.9 copy-start.1
  34.1 9.9 %collective-permute-start = (f32[2048,128]{1,0:T(8,128)S(1)}, f32[2048,128]{1,0:T(8,128)S(1)}, u32[]{:S(2)}, u32[]{:S(2)}) collective-permute-start(f32[2048,128]{1,0:T(8,128)S(1)} %get-tuple-element.22), channel_id=1, source_target_pairs={{0,1},{1,0},{2,3},{3,2},{4,5},{5,4},{6,7},{7,6},{8,9},{9,8},{10,11... | collective-permute-start | bytes 3145736 | tf_op jit(solution)/shard_map/ppermute | solution.py:272
  63.4 26.2 %all-to-all-start.2 = ((f32[32,8,128]{2,1,0:T(8,128)}), f32[32,8,128]{2,1,0:T(8,128)S(1)}, u32[]{:S(2)}, u32[]{:S(2)}) async-start(f32[32,8,128]{2,1,0:T(8,128)} %bitcast.3), calls=%async_computation.2 | async-start | bytes 262144 | tf_op jit(solution)/shard_map/all_to_all | solution.py:209
  79.5 10.2 %collective-permute-start.1 = (f32[32,672]{1,0:T(8,128)S(1)}, f32[32,672]{1,0:T(8,128)S(1)}, u32[]{:S(2)}, u32[]{:S(2)}) collective-permute-start(f32[32,672]{1,0:T(8,128)S(1)} %get-tuple-element.25), channel_id=1, source_target_pairs={{0,128},{128,256},{256,384},{384,0},{1,129},{129,257},{257,385},{3... | collective-permute-start | bytes 258056 | tf_op jit(solution)/shard_map/ppermute | solution.py:287
  81.4 8.2 %collective-permute-start.2 = (f32[32,672]{1,0:T(8,128)S(1)}, f32[32,672]{1,0:T(8,128)S(1)}, u32[]{:S(2)}, u32[]{:S(2)}) collective-permute-start(f32[32,672]{1,0:T(8,128)S(1)} %get-tuple-element.26), channel_id=1, source_target_pairs={{0,256},{128,384},{256,0},{384,128},{1,257},{129,385},{257,1},{385... | collective-permute-start | bytes 258056 | tf_op jit(solution)/shard_map/ppermute | solution.py:287
  85.4 6.1 %collective-permute-start.3 = (f32[32,672]{1,0:T(8,128)S(1)}, f32[32,672]{1,0:T(8,128)S(1)}, u32[]{:S(2)}, u32[]{:S(2)}) collective-permute-start(f32[32,672]{1,0:T(8,128)S(1)} %get-tuple-element.27), channel_id=1, source_target_pairs={{0,384},{128,0},{256,128},{384,256},{1,385},{129,1},{257,129},{385... | collective-permute-start | bytes 258056 | tf_op jit(solution)/shard_map/ppermute | solution.py:287
  129.2 9.6 %collective-permute-start.4 = (f32[2048,128]{1,0:T(8,128)S(1)}, f32[2048,128]{1,0:T(8,128)S(1)}, u32[]{:S(2)}, u32[]{:S(2)}) collective-permute-start(f32[2048,128]{1,0:T(8,128)S(1)} %bitcast.6), channel_id=1, source_target_pairs={{0,1},{1,0},{2,3},{3,2},{4,5},{5,4},{6,7},{7,6},{8,9},{9,8},{10,11... | collective-permute-start | bytes 3145736 | tf_op jit(solution)/shard_map/ppermute | solution.py:301

commit v6 on v5

--- a/solution.py
+++ b/solution.py
@@ -270,23 +270,24 @@
     )(place, blocks)
 
     came = lax.ppermute(send, "c", swap)
-    part = scatter_sum(keep + came, near, near_count)
+    sums = keep + came
     owned = rank // gx
     core_parts = pl.pallas_call(
         parts_kernel,
         out_shape=[jax.ShapeDtypeStruct((owned, second), f32)] * gx,
-        in_specs=[SMEM, VMEM, VMEM],
+        in_specs=[SMEM, VMEM, pl.BlockSpec(memory_space=pl.ANY)],
         out_specs=[VMEM] * gx,
         compiler_params=ROOM,
         cost_estimate=cost(rank * second, 8 * rank * second),
         name="core_parts",
-    )(place, core, part[:8])
+    )(place, core, came)
     came_core = [core_parts[0]]
     for step in range(1, gx):
         shift = [(i, (i + step) % gx) for i in range(gx)]
         came_core.append(lax.ppermute(core_parts[step], "x", shift))
-    part = scatter_sum(part, far, far_count)
+    part = exchange(sums.reshape(near_count, -1, LANES), near)
     part, *came_core = lax.optimization_barrier((part, *came_core))
+    part = scatter_sum(jnp.sum(part, axis=0), far, far_count)
     core_out = pl.pallas_call(
         rows_kernel,
         out_shape=jax.ShapeDtypeStruct((owned, gx, second), f32),

time: 142 us -> 138 us (0.972)
  starting transfers between devices: 38.4 us -> 27.7 us
  waiting for transfers between devices: 6.38 us -> 10.2 us
  blocking collectives: 83.2 us -> 86 us
    all_to_all x1, starting transfers between devices: 14.8 us -> 3.97 us  [exchange(): return lax.all_to_all(parts, axis, 0, 0, tiled=True)]
    ppermute x3, waiting for transfers between devices: 1.81 us -> 7.08 us  [local(): came_core.append(lax.ppermute(core_parts[step], 'x', shift))]
    all_to_all x4, blocking collectives: 83.2 us -> 86 us  [exchange(): return lax.all_to_all(parts, axis, 0, 0, tiled=True)]
    ppermute x3, starting transfers between devices: 8.67 us -> 10.8 us  [local(): came_core.append(lax.ppermute(core_parts[step], 'x', shift))]
    ppermute x1, starting transfers between devices: 7.31 us -> 5.35 us  [local(): other = lax.ppermute(own, 'c', swap)]
    all_to_all x1, waiting for transfers between devices: 1.44 us -> 0.01 us  [exchange(): return lax.all_to_all(parts, axis, 0, 0, tiled=True)]
  transfers between devices with their start and end apart: 6 -> 6, of which waited for: 4 -> 4; matrix products, arithmetic and copies ran while one was open for 1% -> 0% of each run, Pallas kernels for 1% -> 1%
where the time goes in v6:
time: 138 us; the launch traced here: 137 us
  blocking collectives  86 us (62%)
  starting transfers between devices  27.7 us (20%)
  waiting for transfers between devices  10.2 us (7%)
  Pallas kernels  8.76 us (6%)
  local copies, waits for them, and re-layouts  2.55 us (2%)
    all_to_all x4, blocking collectives, exchange(): return lax.all_to_all(parts, axis, 0, 0, tiled=True)  86 us
    ppermute x3, starting transfers between devices, local(): came_core.append(lax.ppermute(core_parts[step], 'x', shift))  10.8 us
    ppermute x1, starting transfers between devices, local(): came = lax.ppermute(send, 'c', swap)  7.63 us
    ppermute x3, waiting for transfers between devices, local(): came_core.append(lax.ppermute(core_parts[step], 'x', shift))  7.08 us
    ppermute x1, starting transfers between devices, local(): other = lax.ppermute(own, 'c', swap)  5.35 us
    all_to_all x1, starting transfers between devices, exchange(): return lax.all_to_all(parts, axis, 0, 0, tiled=True)  3.97 us
    pallas_call x1, Pallas kernels, local(): pl.pallas_call(functools.partial(gram_kernel, layout), out_shape=(half_sh...  3.8 us
    pallas_call x1, Pallas kernels, local(): pl.pallas_call(functools.partial(unpack_kernel, layout, 1.0 / (slices_all...  2.81 us
  transfers between devices with their start and end apart: 6, of which 4 were waited for; matrix products, arithmetic and copies ran while one was open for 0% of the time, Pallas kernels for 1%

profile of v6, /device:TPU:1, one launch (start us, length us, event | category | flops | bytes accessed | tf_op | source)
XLA Modules:
  0.0 137.2 jit_solution(14147441949670897735)
XLA Ops:
  0.6 0.1 pad_add_fusion.place_ref
  0.7 0.0 copy-start
  0.7 1.6 %copy-done = f32[4,168,672]{2,1,0:T(8,128)S(1)} copy-done((f32[4,168,672]{2,1,0:T(8,128)S(1)}, f32[4,168,672]{2,1,0:T(8,128)}, u32[]{:S(2)}) %copy-start) | copy-done | bytes 1806360
  2.3 0.0 copy-start.1
  2.3 0.9 copy-done.1
  3.2 0.2 dense_blocks.1
  3.4 26.9 %all_to_all.25.dense_ref = f32[4,1056,128]{2,1,0:T(8,128)S(1)} all-to-all(f32[4,1056,128]{2,1,0:T(8,128)S(1)} %dense_blocks.1), channel_id=1, replica_groups=mesh['x'=4,'y'=8,'zh'=4,'zl'=2,'c'=2] {'x'}, dimensions={0} | all-to-all | bytes 4325376 | tf_op jit(solution)/shard_map/all_to_all | solution.py:209
  30.3 3.8 %local_grams.1 = (f32[2048,128]{1,0:T(8,128)S(1)}, f32[2048,128]{1,0:T(8,128)S(1)}, f32[128,672]{1,0:T(8,128)S(1)}) custom-call(s32[2]{0:T(128)S(1)} %pad_add_fusion.place_ref, f32[4,1056,128]{2,1,0:T(8,128)S(1)} %all_to_all.25.dense_ref), custom_call_target="tpu_custom_call" | custom-call | flops 1517322240 | bytes 5419008 | tf_op jit(solution)/shard_map/local_grams/pallas_call | solution.py:253
  34.1 7.6 %collective-permute-start = (f32[2048,128]{1,0:T(8,128)S(1)}, f32[2048,128]{1,0:T(8,128)S(1)}, u32[]{:S(2)}, u32[]{:S(2)}) collective-permute-start(f32[2048,128]{1,0:T(8,128)S(1)} %get-tuple-element.22), channel_id=1, source_target_pairs={{0,1},{1,0},{2,3},{3,2},{4,5},{5,4},{6,7},{7,6},{8,9},{9,8},{10,11... | collective-permute-start | bytes 3145736 | tf_op jit(solution)/shard_map/ppermute | solution.py:272
  41.7 2.3 %collective-permute-done.after_ref = f32[2048,128]{1,0:T(8,128)S(1)} collective-permute-done((f32[2048,128]{1,0:T(8,128)S(1)}, f32[2048,128]{1,0:T(8,128)S(1)}, u32[]{:S(2)}, u32[]{:S(2)}) %collective-permute-start) | collective-permute-done | bytes 1048608 | tf_op jit(solution)/shard_map/ppermute | solution.py:272
  44.0 1.1 add.3
  45.1 4.0 %all-to-all-start.1 = ((f32[8,256,128]{2,1,0:T(8,128)}), f32[8,256,128]{2,1,0:T(8,128)S(1)}, u32[]{:S(2)}, u32[]{:S(2)}) async-start(f32[8,256,128]{2,1,0:T(8,128)} %bitcast.2), calls=%async_computation.1 | async-start | bytes 2097152 | tf_op jit(solution)/shard_map/all_to_all | solution.py:209
  49.0 0.6 core_parts.1
  49.6 3.4 %collective-permute-start.1 = (f32[32,672]{1,0:T(8,128)S(1)}, f32[32,672]{1,0:T(8,128)S(1)}, u32[]{:S(2)}, u32[]{:S(2)}) collective-permute-start(f32[32,672]{1,0:T(8,128)S(1)} %get-tuple-element.25), channel_id=1, source_target_pairs={{0,128},{128,256},{256,384},{384,0},{1,129},{129,257},{257,385},{3... | collective-permute-start | bytes 258056 | tf_op jit(solution)/shard_map/ppermute | solution.py:287
  53.0 4.3 %collective-permute-start.2 = (f32[32,672]{1,0:T(8,128)S(1)}, f32[32,672]{1,0:T(8,128)S(1)}, u32[]{:S(2)}, u32[]{:S(2)}) collective-permute-start(f32[32,672]{1,0:T(8,128)S(1)} %get-tuple-element.26), channel_id=1, source_target_pairs={{0,256},{128,384},{256,0},{384,128},{1,257},{129,385},{257,1},{385... | collective-permute-start | bytes 258056 | tf_op jit(solution)/shard_map/ppermute | solution.py:287
  57.3 3.1 %collective-permute-start.3 = (f32[32,672]{1,0:T(8,128)S(1)}, f32[32,672]{1,0:T(8,128)S(1)}, u32[]{:S(2)}, u32[]{:S(2)}) collective-permute-start(f32[32,672]{1,0:T(8,128)S(1)} %get-tuple-element.27), channel_id=1, source_target_pairs={{0,384},{128,0},{256,128},{384,256},{1,385},{129,1},{257,129},{385... | collective-permute-start | bytes 258056 | tf_op jit(solution)/shard_map/ppermute | solution.py:287
  60.4 5.6 %collective-permute-done.1.refs_1_ = f32[32,672]{1,0:T(8,128)S(1)} collective-permute-done((f32[32,672]{1,0:T(8,128)S(1)}, f32[32,672]{1,0:T(8,128)S(1)}, u32[]{:S(2)}, u32[]{:S(2)}) %collective-permute-start.1) | collective-permute-done | bytes 86048 | tf_op jit(solution)/shard_map/ppermute | solution.py:287
  66.0 1.5 %collective-permute-done.2.refs_2_ = f32[32,672]{1,0:T(8,128)S(1)} collective-permute-done((f32[32,672]{1,0:T(8,128)S(1)}, f32[32,672]{1,0:T(8,128)S(1)}, u32[]{:S(2)}, u32[]{:S(2)}) %collective-permute-start.2) | collective-permute-done | bytes 86048 | tf_op jit(solution)/shard_map/ppermute | solution.py:287
  67.5 0.0 collective-permute-done.3.refs_3_
  67.5 0.0 all-to-all-done.1
  67.5 0.1 reduce_sum.18
  67.5 26.9 %all_to_all.26 = f32[32,8,128]{2,1,0:T(8,128)S(1)} all-to-all(f32[32,8,128]{2,1,0:T(8,128)S(1)} %bitcast.8), channel_id=1, replica_groups=mesh['x'=4,'y'=8,'zh'=4,'zl'=2,'c'=2] {'y','zh'}, dimensions={0} | all-to-all | bytes 262144 | tf_op jit(solution)/shard_map/all_to_all | solution.py:209
  94.5 14.5 %all_to_all.27 = f32[32,8,128]{2,1,0:T(8,128)S(1)} all-to-all(f32[32,8,128]{2,1,0:T(8,128)S(1)} %broadcast_in_dim.6), channel_id=1, replica_groups=mesh['x'=4,'y'=8,'zh'=4,'zl'=2,'c'=2] {'y','zh'}, dimensions={0} | all-to-all | bytes 262144 | tf_op jit(solution)/shard_map/all_to_all | solution.py:209
  109.0 0.1 broadcast_in_dim.15
  109.0 17.7 %all_to_all.28 = f32[8,256,128]{2,1,0:T(8,128)S(1)} all-to-all(f32[8,256,128]{2,1,0:T(8,128)S(1)} %broadcast_in_dim.15), channel_id=1, replica_groups=mesh['x'=4,'y'=8,'zh'=4,'zl'=2,'c'=2] {'x','zl'}, dimensions={0} | all-to-all | bytes 2097152 | tf_op jit(solution)/shard_map/all_to_all | solution.py:209
  126.8 5.3 %collective-permute-start.4 = (f32[2048,128]{1,0:T(8,128)S(1)}, f32[2048,128]{1,0:T(8,128)S(1)}, u32[]{:S(2)}, u32[]{:S(2)}) collective-permute-start(f32[2048,128]{1,0:T(8,128)S(1)} %bitcast.6), channel_id=1, source_target_pairs={{0,1},{1,0},{2,3},{3,2},{4,5},{5,4},{6,7},{7,6},{8,9},{9,8},{10,11... | collective-permute-start | bytes 3145736 | tf_op jit(solution)/shard_map/ppermute | solution.py:302
  132.1 1.4 %core_rows.1 = f32[32,4,672]{2,1,0:T(4,128)} custom-call(s32[2]{0:T(128)S(1)} %pad_add_fusion.place_ref, f32[32,672]{1,0:T(8,128)S(1)} %get-tuple-element.30.refs_0_, f32[32,672]{1,0:T(8,128)S(1)} %collective-permute-done.1.refs_1_, f32[32,672]{1,0:T(8,128)S(1)} %collective-permute-done.2.refs_2_, f32[32,672]{1,0:T(8,128)S(1)} %collective-permute-done.3.refs_3_), custom_call_target="tpu_custom_call" | custom-call | flops 86016 | bytes 688128 | tf_op jit(solution)/shard_map/core_rows/pallas_call | solution.py:291
  133.5 0.9 collective-permute-done.4.other_ref
  134.4 2.8 %mirror.1 = (f32[168,672]{1,0:T(8,128)}, f32[672,672]{1,0:T(8,128)}) custom-call(s32[2]{0:T(128)S(1)} %pad_add_fusion.place_ref, f32[2048,128]{1,0:T(8,128)S(1)} %bitcast.7, f32[2048,128]{1,0:T(8,128)S(1)} %collective-permute-done.4.other_ref), custom_call_target="tpu_custom_call" | custom-call | tf_op jit(solution)/shard_map/mirror/pallas_call | solution.py:304
  (2 shorter events, 0.0 us)
Async XLA Ops:
  0.7 1.6 %copy-start = (f32[4,168,672]{2,1,0:T(8,128)S(1)}, f32[4,168,672]{2,1,0:T(8,128)}, u32[]{:S(2)}) copy-start(f32[4,168,672]{2,1,0:T(8,128)} %field_ref.1) | copy-start | bytes 5419012
  2.3 0.9 copy-start.1
  34.1 9.9 %collective-permute-start = (f32[2048,128]{1,0:T(8,128)S(1)}, f32[2048,128]{1,0:T(8,128)S(1)}, u32[]{:S(2)}, u32[]{:S(2)}) collective-permute-start(f32[2048,128]{1,0:T(8,128)S(1)} %get-tuple-element.22), channel_id=1, source_target_pairs={{0,1},{1,0},{2,3},{3,2},{4,5},{5,4},{6,7},{7,6},{8,9},{9,8},{10,11... | collective-permute-start | bytes 3145736 | tf_op jit(solution)/shard_map/ppermute | solution.py:272
  45.1 22.4 %all-to-all-start.1 = ((f32[8,256,128]{2,1,0:T(8,128)}), f32[8,256,128]{2,1,0:T(8,128)S(1)}, u32[]{:S(2)}, u32[]{:S(2)}) async-start(f32[8,256,128]{2,1,0:T(8,128)} %bitcast.2), calls=%async_computation.1 | async-start | bytes 2097152 | tf_op jit(solution)/shard_map/all_to_all | solution.py:209
  49.6 16.4 %collective-permute-start.1 = (f32[32,672]{1,0:T(8,128)S(1)}, f32[32,672]{1,0:T(8,128)S(1)}, u32[]{:S(2)}, u32[]{:S(2)}) collective-permute-start(f32[32,672]{1,0:T(8,128)S(1)} %get-tuple-element.25), channel_id=1, source_target_pairs={{0,128},{128,256},{256,384},{384,0},{1,129},{129,257},{257,385},{3... | collective-permute-start | bytes 258056 | tf_op jit(solution)/shard_map/ppermute | solution.py:287
  53.0 14.5 %collective-permute-start.2 = (f32[32,672]{1,0:T(8,128)S(1)}, f32[32,672]{1,0:T(8,128)S(1)}, u32[]{:S(2)}, u32[]{:S(2)}) collective-permute-start(f32[32,672]{1,0:T(8,128)S(1)} %get-tuple-element.26), channel_id=1, source_target_pairs={{0,256},{128,384},{256,0},{384,128},{1,257},{129,385},{257,1},{385... | collective-permute-start | bytes 258056 | tf_op jit(solution)/shard_map/ppermute | solution.py:287
  57.3 10.2 %collective-permute-start.3 = (f32[32,672]{1,0:T(8,128)S(1)}, f32[32,672]{1,0:T(8,128)S(1)}, u32[]{:S(2)}, u32[]{:S(2)}) collective-permute-start(f32[32,672]{1,0:T(8,128)S(1)} %get-tuple-element.27), channel_id=1, source_target_pairs={{0,384},{128,0},{256,128},{384,256},{1,385},{129,1},{257,129},{385... | collective-permute-start | bytes 258056 | tf_op jit(solution)/shard_map/ppermute | solution.py:287
  126.8 7.6 %collective-permute-start.4 = (f32[2048,128]{1,0:T(8,128)S(1)}, f32[2048,128]{1,0:T(8,128)S(1)}, u32[]{:S(2)}, u32[]{:S(2)}) collective-permute-start(f32[2048,128]{1,0:T(8,128)S(1)} %bitcast.6), channel_id=1, source_target_pairs={{0,1},{1,0},{2,3},{3,2},{4,5},{5,4},{6,7},{7,6},{8,9},{9,8},{10,11... | collective-permute-start | bytes 3145736 | tf_op jit(solution)/shard_map/ppermute | solution.py:302

commit v7 on v6

--- a/solution.py
+++ b/solution.py
@@ -2,6 +2,7 @@
 
 import jax
 import jax.numpy as jnp
+import numpy as np
 from jax import lax
 from jax.experimental import pallas as pl
 from jax.experimental.pallas import tpu as pltpu
@@ -205,8 +206,8 @@
     unpack(layout, packed, 1, two_ref, scale_two)
 
 
-def exchange(parts, axis):
-    return lax.all_to_all(parts, axis, 0, 0, tiled=True)
+def exchange(parts, axes, groups=None):
+    return lax.all_to_all(parts, axes, 0, 0, axis_index_groups=groups, tiled=True)
 
 
 def copies(value, count):
@@ -217,12 +218,14 @@
     return pl.CostEstimate(flops=flops, transcendentals=0, bytes_accessed=moved)
 
 
-def scatter_sum(value, axes, count):
-    return jnp.sum(exchange(value.reshape(count, -1, LANES), axes), axis=0)
-
-
-def gather(value, axes, count):
-    return exchange(copies(value, count), axes).reshape(-1, LANES)
+def both_groups(sizes):
+    shape = tuple(sizes.values())
+    index = np.arange(np.prod(shape)).reshape(shape)
+    near = [index[:, a, b, d, e, 0] for a, b, d, e in np.ndindex(shape[1:5])]
+    near += [index[a, b, :, d, :, 1] for a, b, d in np.ndindex(shape[0], shape[1], shape[3])]
+    far = [index[a, ..., 0] for a in range(shape[0])]
+    far += [index[:, :, b, :, e, 1] for b, e in np.ndindex(shape[2], shape[4])]
+    return [[group.reshape(-1).tolist() for group in groups] for groups in (near, far)]
 
 
 def local(sizes, tensor, basis):
@@ -230,9 +233,10 @@
     slices_here, rows_here, second = tensor.shape
     first = rows_here * gx
     rank = basis.shape[1]
-    near, far = ("x", "zl"), ("y", "zh")
-    near_count, far_count = gx * sizes["zl"], sizes["y"] * sizes["zh"]
-    slices_all = slices_here * sizes["y"] * sizes["zh"] * sizes["zl"] * sizes["c"]
+    axes = tuple(sizes)
+    near, far = both_groups(sizes)
+    near_count, far_count = len(near[0]), len(far[0])
+    slices_all = slices_here * near_count * far_count // gx * sizes["c"]
     layout = Layout(first, 8 * near_count * far_count)
     dense = dense_rows(rows_here, second)[-1]
     swap = [(i, sizes["c"] - 1 - i) for i in range(sizes["c"])]
@@ -285,9 +289,9 @@
     for step in range(1, gx):
         shift = [(i, (i + step) % gx) for i in range(gx)]
         came_core.append(lax.ppermute(core_parts[step], "x", shift))
-    part = exchange(sums.reshape(near_count, -1, LANES), near)
+    part = exchange(sums.reshape(near_count, -1, LANES), axes, near)
     part, *came_core = lax.optimization_barrier((part, *came_core))
-    part = scatter_sum(jnp.sum(part, axis=0), far, far_count)
+    part = exchange(jnp.sum(part, axis=0).reshape(far_count, -1, LANES), axes, far)
     core_out = pl.pallas_call(
         rows_kernel,
         out_shape=jax.ShapeDtypeStruct((owned, gx, second), f32),
@@ -298,7 +302,8 @@
         cost_estimate=cost(rank * second, 8 * rank * second),
         name="core_rows",
     )(place, *came_core)
-    own = gather(gather(part, far, far_count), near, near_count)
+    part = exchange(copies(jnp.sum(part, axis=0), far_count), axes, far).reshape(-1, LANES)
+    own = exchange(copies(part, near_count), axes, near).reshape(-1, LANES)
     other = lax.ppermute(own, "c", swap)
 
     gram_one, gram_two = pl.pallas_call(
@@ -318,9 +323,9 @@
 
 def solution(mesh):
     gx, rest = mesh.devices.shape
-    sizes = {"x": gx, "y": 8, "zh": rest // 32, "zl": 2, "c": 2}
+    sizes = {"x": gx, "yh": 4, "yl": 2, "zh": rest // 32, "zl": 2, "c": 2}
     fine = Mesh(mesh.devices.reshape(tuple(sizes.values())), tuple(sizes))
-    spread = ("y", "zh", "zl", "c")
+    spread = ("yh", "yl", "zh", "zl", "c")
     in_specs = (P(spread, "x", None), P("x", None))
     out_specs = (P("x", None), P("x", spread, None), P())
     return jax.shard_map(

time: 138 us -> 138 us (level)
  blocking collectives: 86 us -> 94.8 us
  starting transfers between devices: 27.7 us -> 22.5 us
  waiting for transfers between devices: 10.2 us -> 6.69 us
    all_to_all x4, blocking collectives: 86 us -> 94.8 us  [exchange(): lax.all_to_all(parts, axes, 0, 0, axis_index_groups=groups, tiled=True)]
    ppermute x3, waiting for transfers between devices: 7.08 us -> 3.31 us  [local(): came_core.append(lax.ppermute(core_parts[step], 'x', shift))]
    ppermute x1, starting transfers between devices: 5.35 us -> 2.02 us  [local(): other = lax.ppermute(own, 'c', swap)]
    ppermute x3, starting transfers between devices: 10.8 us -> 8.51 us  [local(): came_core.append(lax.ppermute(core_parts[step], 'x', shift))]
  transfers between devices with their start and end apart: 6 -> 6, of which waited for: 4 -> 3; matrix products, arithmetic and copies ran while one was open for 0% -> 0% of each run, Pallas kernels for 1% -> 1%
where the time goes in v7:
time: 138 us; the launch traced here: 137 us
  blocking collectives  94.8 us (69%)
  starting transfers between devices  22.5 us (16%)
  Pallas kernels  8.76 us (6%)
  waiting for transfers between devices  6.69 us (5%)
  local copies, waits for them, and re-layouts  2.56 us (2%)
    all_to_all x4, blocking collectives, exchange(): lax.all_to_all(parts, axes, 0, 0, axis_index_groups=groups, tiled=True)  94.8 us
    ppermute x3, starting transfers between devices, local(): came_core.append(lax.ppermute(core_parts[step], 'x', shift))  8.51 us
    ppermute x1, starting transfers between devices, local(): came = lax.ppermute(send, 'c', swap)  7.63 us
    all_to_all x1, starting transfers between devices, exchange(): lax.all_to_all(parts, axes, 0, 0, axis_index_groups=groups, tiled=True)  4.37 us
    pallas_call x1, Pallas kernels, local(): pl.pallas_call(functools.partial(gram_kernel, layout), out_shape=(half_sh...  3.8 us
    ppermute x3, waiting for transfers between devices, local(): came_core.append(lax.ppermute(core_parts[step], 'x', shift))  3.31 us
    pallas_call x1, Pallas kernels, local(): pl.pallas_call(functools.partial(unpack_kernel, layout, 1.0 / (slices_all...  2.81 us
  transfers between devices with their start and end apart: 6, of which 3 were waited for; matrix products, arithmetic and copies ran while one was open for 0% of the time, Pallas kernels for 1%

profile of v7, /device:TPU:1, one launch (start us, length us, event | category | flops | bytes accessed | tf_op | source)
XLA Modules:
  0.0 137.4 jit_solution(7511092043497883875)
XLA Ops:
  0.6 0.1 pad_add_fusion.place_ref
  0.7 0.0 copy-start
  0.7 1.6 %copy-done = f32[4,168,672]{2,1,0:T(8,128)S(1)} copy-done((f32[4,168,672]{2,1,0:T(8,128)S(1)}, f32[4,168,672]{2,1,0:T(8,128)}, u32[]{:S(2)}) %copy-start) | copy-done | bytes 1806360
  2.3 0.0 copy-start.1
  2.3 0.9 copy-done.1
  3.2 0.2 dense_blocks.1
  3.4 26.9 %all_to_all.25.dense_ref = f32[4,1056,128]{2,1,0:T(8,128)S(1)} all-to-all(f32[4,1056,128]{2,1,0:T(8,128)S(1)} %dense_blocks.1), channel_id=1, replica_groups=mesh['x'=4,'yh'=4,'yl'=2,'zh'=4,'zl'=2,'c'=2] {'x'}, dimensions={0} | all-to-all | bytes 4325376 | tf_op jit(solution)/shard_map/all_to_all | solution.py:210
  30.3 3.8 %local_grams.1 = (f32[2048,128]{1,0:T(8,128)S(1)}, f32[2048,128]{1,0:T(8,128)S(1)}, f32[128,672]{1,0:T(8,128)S(1)}) custom-call(s32[2]{0:T(128)S(1)} %pad_add_fusion.place_ref, f32[4,1056,128]{2,1,0:T(8,128)S(1)} %all_to_all.25.dense_ref), custom_call_target="tpu_custom_call" | custom-call | flops 1517322240 | bytes 5419008 | tf_op jit(solution)/shard_map/local_grams/pallas_call | solution.py:257
  34.1 7.6 %collective-permute-start = (f32[2048,128]{1,0:T(8,128)S(1)}, f32[2048,128]{1,0:T(8,128)S(1)}, u32[]{:S(2)}, u32[]{:S(2)}) collective-permute-start(f32[2048,128]{1,0:T(8,128)S(1)} %get-tuple-element.22), channel_id=1, source_target_pairs={{0,1},{1,0},{2,3},{3,2},{4,5},{5,4},{6,7},{7,6},{8,9},{9,8},{10,11... | collective-permute-start | bytes 3145736 | tf_op jit(solution)/shard_map/ppermute | solution.py:276
  41.7 2.3 %collective-permute-done.after_ref = f32[2048,128]{1,0:T(8,128)S(1)} collective-permute-done((f32[2048,128]{1,0:T(8,128)S(1)}, f32[2048,128]{1,0:T(8,128)S(1)}, u32[]{:S(2)}, u32[]{:S(2)}) %collective-permute-start) | collective-permute-done | bytes 1048608 | tf_op jit(solution)/shard_map/ppermute | solution.py:276
  44.0 1.1 add.3
  45.1 4.4 %all-to-all-start.1 = ((f32[4,512,128]{2,1,0:T(8,128)}), f32[4,512,128]{2,1,0:T(8,128)S(1)}, u32[]{:S(2)}, u32[]{:S(2)}) async-start(f32[4,512,128]{2,1,0:T(8,128)} %bitcast.2), calls=%async_computation.1 | async-start | bytes 2097152 | tf_op jit(solution)/shard_map/all_to_all | solution.py:210
  49.4 0.6 core_parts.1
  50.0 2.2 %collective-permute-start.1 = (f32[32,672]{1,0:T(8,128)S(1)}, f32[32,672]{1,0:T(8,128)S(1)}, u32[]{:S(2)}, u32[]{:S(2)}) collective-permute-start(f32[32,672]{1,0:T(8,128)S(1)} %get-tuple-element.25), channel_id=1, source_target_pairs={{0,128},{128,256},{256,384},{384,0},{1,129},{129,257},{257,385},{3... | collective-permute-start | bytes 258056 | tf_op jit(solution)/shard_map/ppermute | solution.py:291
  52.2 3.7 %collective-permute-start.2 = (f32[32,672]{1,0:T(8,128)S(1)}, f32[32,672]{1,0:T(8,128)S(1)}, u32[]{:S(2)}, u32[]{:S(2)}) collective-permute-start(f32[32,672]{1,0:T(8,128)S(1)} %get-tuple-element.26), channel_id=1, source_target_pairs={{0,256},{128,384},{256,0},{384,128},{1,257},{129,385},{257,1},{385... | collective-permute-start | bytes 258056 | tf_op jit(solution)/shard_map/ppermute | solution.py:291
  55.9 2.6 %collective-permute-start.3 = (f32[32,672]{1,0:T(8,128)S(1)}, f32[32,672]{1,0:T(8,128)S(1)}, u32[]{:S(2)}, u32[]{:S(2)}) collective-permute-start(f32[32,672]{1,0:T(8,128)S(1)} %get-tuple-element.27), channel_id=1, source_target_pairs={{0,384},{128,0},{256,128},{384,256},{1,385},{129,1},{257,129},{385... | collective-permute-start | bytes 258056 | tf_op jit(solution)/shard_map/ppermute | solution.py:291
  58.6 3.3 %collective-permute-done.1.refs_1_ = f32[32,672]{1,0:T(8,128)S(1)} collective-permute-done((f32[32,672]{1,0:T(8,128)S(1)}, f32[32,672]{1,0:T(8,128)S(1)}, u32[]{:S(2)}, u32[]{:S(2)}) %collective-permute-start.1) | collective-permute-done | bytes 86048 | tf_op jit(solution)/shard_map/ppermute | solution.py:291
  61.9 0.0 collective-permute-done.2.refs_2_
  61.9 0.0 collective-permute-done.3.refs_3_
  61.9 0.0 all-to-all-done.1
  61.9 0.1 reduce_sum.18
  62.0 33.2 %all_to_all.26 = f32[64,8,128]{2,1,0:T(8,128)S(1)} all-to-all(f32[64,8,128]{2,1,0:T(8,128)S(1)} %bitcast.8), channel_id=1, replica_groups={{0,2,4,6,8,10,12,14,16,18,20,22,24,26,28,30,32,34,36,38,40,42,44,46,48,..., dimensions={0} | all-to-all | bytes 524288 | tf_op jit(solution)/shard_map/all_to_all | solution.py:210
  95.2 0.1 reduce_sum.19
  95.3 23.5 %all_to_all.27 = f32[64,8,128]{2,1,0:T(8,128)S(1)} all-to-all(f32[64,8,128]{2,1,0:T(8,128)S(1)} %broadcast_in_dim.6), channel_id=1, replica_groups={{0,2,4,6,8,10,12,14,16,18,20,22,24,26,28,30,32,34,36,38,40,42,44,46,48,..., dimensions={0} | all-to-all | bytes 524288 | tf_op jit(solution)/shard_map/all_to_all | solution.py:210
  118.8 0.1 broadcast_in_dim.15
  118.8 11.2 %all_to_all.28 = f32[4,512,128]{2,1,0:T(8,128)S(1)} all-to-all(f32[4,512,128]{2,1,0:T(8,128)S(1)} %broadcast_in_dim.15), channel_id=1, replica_groups={{0,128,256,384},{2,130,258,386},{4,132,260,388},{6,134,262,390},{8,136,..., dimensions={0} | all-to-all | bytes 2097152 | tf_op jit(solution)/shard_map/all_to_all | solution.py:210
  130.1 2.0 %collective-permute-start.4 = (f32[2048,128]{1,0:T(8,128)S(1)}, f32[2048,128]{1,0:T(8,128)S(1)}, u32[]{:S(2)}, u32[]{:S(2)}) collective-permute-start(f32[2048,128]{1,0:T(8,128)S(1)} %bitcast.6), channel_id=1, source_target_pairs={{0,1},{1,0},{2,3},{3,2},{4,5},{5,4},{6,7},{7,6},{8,9},{9,8},{10,11... | collective-permute-start | bytes 3145736 | tf_op jit(solution)/shard_map/ppermute | solution.py:307
  132.1 1.4 %core_rows.1 = f32[32,4,672]{2,1,0:T(4,128)} custom-call(s32[2]{0:T(128)S(1)} %pad_add_fusion.place_ref, f32[32,672]{1,0:T(8,128)S(1)} %get-tuple-element.30.refs_0_, f32[32,672]{1,0:T(8,128)S(1)} %collective-permute-done.1.refs_1_, f32[32,672]{1,0:T(8,128)S(1)} %collective-permute-done.2.refs_2_, f32[32,672]{1,0:T(8,128)S(1)} %collective-permute-done.3.refs_3_), custom_call_target="tpu_custom_call" | custom-call | flops 86016 | bytes 688128 | tf_op jit(solution)/shard_map/core_rows/pallas_call | solution.py:295
  133.5 1.1 collective-permute-done.4.other_ref
  134.6 2.8 %mirror.1 = (f32[168,672]{1,0:T(8,128)}, f32[672,672]{1,0:T(8,128)}) custom-call(s32[2]{0:T(128)S(1)} %pad_add_fusion.place_ref, f32[2048,128]{1,0:T(8,128)S(1)} %bitcast.7, f32[2048,128]{1,0:T(8,128)S(1)} %collective-permute-done.4.other_ref), custom_call_target="tpu_custom_call" | custom-call | tf_op jit(solution)/shard_map/mirror/pallas_call | solution.py:309
  (1 shorter events, 0.0 us)
Async XLA Ops:
  0.7 1.6 %copy-start = (f32[4,168,672]{2,1,0:T(8,128)S(1)}, f32[4,168,672]{2,1,0:T(8,128)}, u32[]{:S(2)}) copy-start(f32[4,168,672]{2,1,0:T(8,128)} %field_ref.1) | copy-start | bytes 5419012
  2.3 0.9 copy-start.1
  34.1 9.9 %collective-permute-start = (f32[2048,128]{1,0:T(8,128)S(1)}, f32[2048,128]{1,0:T(8,128)S(1)}, u32[]{:S(2)}, u32[]{:S(2)}) collective-permute-start(f32[2048,128]{1,0:T(8,128)S(1)} %get-tuple-element.22), channel_id=1, source_target_pairs={{0,1},{1,0},{2,3},{3,2},{4,5},{5,4},{6,7},{7,6},{8,9},{9,8},{10,11... | collective-permute-start | bytes 3145736 | tf_op jit(solution)/shard_map/ppermute | solution.py:276
  45.1 16.8 %all-to-all-start.1 = ((f32[4,512,128]{2,1,0:T(8,128)}), f32[4,512,128]{2,1,0:T(8,128)S(1)}, u32[]{:S(2)}, u32[]{:S(2)}) async-start(f32[4,512,128]{2,1,0:T(8,128)} %bitcast.2), calls=%async_computation.1 | async-start | bytes 2097152 | tf_op jit(solution)/shard_map/all_to_all | solution.py:210
  50.0 11.8 %collective-permute-start.1 = (f32[32,672]{1,0:T(8,128)S(1)}, f32[32,672]{1,0:T(8,128)S(1)}, u32[]{:S(2)}, u32[]{:S(2)}) collective-permute-start(f32[32,672]{1,0:T(8,128)S(1)} %get-tuple-element.25), channel_id=1, source_target_pairs={{0,128},{128,256},{256,384},{384,0},{1,129},{129,257},{257,385},{3... | collective-permute-start | bytes 258056 | tf_op jit(solution)/shard_map/ppermute | solution.py:291
  52.2 9.6 %collective-permute-start.2 = (f32[32,672]{1,0:T(8,128)S(1)}, f32[32,672]{1,0:T(8,128)S(1)}, u32[]{:S(2)}, u32[]{:S(2)}) collective-permute-start(f32[32,672]{1,0:T(8,128)S(1)} %get-tuple-element.26), channel_id=1, source_target_pairs={{0,256},{128,384},{256,0},{384,128},{1,257},{129,385},{257,1},{385... | collective-permute-start | bytes 258056 | tf_op jit(solution)/shard_map/ppermute | solution.py:291
  55.9 5.9 %collective-permute-start.3 = (f32[32,672]{1,0:T(8,128)S(1)}, f32[32,672]{1,0:T(8,128)S(1)}, u32[]{:S(2)}, u32[]{:S(2)}) collective-permute-start(f32[32,672]{1,0:T(8,128)S(1)} %get-tuple-element.27), channel_id=1, source_target_pairs={{0,384},{128,0},{256,128},{384,256},{1,385},{129,1},{257,129},{385... | collective-permute-start | bytes 258056 | tf_op jit(solution)/shard_map/ppermute | solution.py:291
  130.1 4.5 %collective-permute-start.4 = (f32[2048,128]{1,0:T(8,128)S(1)}, f32[2048,128]{1,0:T(8,128)S(1)}, u32[]{:S(2)}, u32[]{:S(2)}) collective-permute-start(f32[2048,128]{1,0:T(8,128)S(1)} %bitcast.6), channel_id=1, source_target_pairs={{0,1},{1,0},{2,3},{3,2},{4,5},{5,4},{6,7},{7,6},{8,9},{9,8},{10,11... | collective-permute-start | bytes 3145736 | tf_op jit(solution)/shard_map/ppermute | solution.py:307

commit v8 on v7

--- a/solution.py
+++ b/solution.py
@@ -221,10 +221,10 @@
 def both_groups(sizes):
     shape = tuple(sizes.values())
     index = np.arange(np.prod(shape)).reshape(shape)
-    near = [index[:, a, b, d, e, 0] for a, b, d, e in np.ndindex(shape[1:5])]
-    near += [index[a, b, :, d, :, 1] for a, b, d in np.ndindex(shape[0], shape[1], shape[3])]
-    far = [index[a, ..., 0] for a in range(shape[0])]
-    far += [index[:, :, b, :, e, 1] for b, e in np.ndindex(shape[2], shape[4])]
+    near = [index[:, b, d, :, 0] for b, d in np.ndindex(shape[1], shape[2])]
+    near += [index[a, :, d, e, 1] for a, d, e in np.ndindex(shape[0], shape[2], shape[3])]
+    far = [index[a, :, :, e, 0] for a, e in np.ndindex(shape[0], shape[3])]
+    far += [index[:, b, :, :, 1] for b in range(shape[1])]
     return [[group.reshape(-1).tolist() for group in groups] for groups in (near, far)]
 
 
@@ -323,9 +323,9 @@
 
 def solution(mesh):
     gx, rest = mesh.devices.shape
-    sizes = {"x": gx, "yh": 4, "yl": 2, "zh": rest // 32, "zl": 2, "c": 2}
+    sizes = {"x": gx, "y": 8, "zh": rest // 32, "zl": 2, "c": 2}
     fine = Mesh(mesh.devices.reshape(tuple(sizes.values())), tuple(sizes))
-    spread = ("yh", "yl", "zh", "zl", "c")
+    spread = ("y", "zh", "zl", "c")
     in_specs = (P(spread, "x", None), P("x", None))
     out_specs = (P("x", None), P("x", spread, None), P())
     return jax.shard_map(

time: 138 us -> 132 us (0.957)
  blocking collectives: 94.8 us -> 80.1 us
  waiting for transfers between devices: 6.69 us -> 11.8 us
  starting transfers between devices: 22.5 us -> 26.8 us
    all_to_all x4, blocking collectives: 94.8 us -> 80.1 us  [exchange(): lax.all_to_all(parts, axes, 0, 0, axis_index_groups=groups, tiled=True)]
    all_to_all x1, waiting for transfers between devices: 0.01 us -> 5.5 us  [exchange(): lax.all_to_all(parts, axes, 0, 0, axis_index_groups=groups, tiled=True)]
    all_to_all x1, starting transfers between devices: 4.37 us -> 6.82 us  [exchange(): lax.all_to_all(parts, axes, 0, 0, axis_index_groups=groups, tiled=True)]
    ppermute x1, starting transfers between devices: 2.02 us -> 3.82 us  [local(): other = lax.ppermute(own, 'c', swap)]
  transfers between devices with their start and end apart: 6 -> 6, of which waited for: 3 -> 6; matrix products, arithmetic and copies ran while one was open for 0% -> 0% of each run, Pallas kernels for 1% -> 1%
where the time goes in v8:
time: 132 us
  blocking collectives  80.1 us (61%)
  starting transfers between devices  26.8 us (20%)
  waiting for transfers between devices  11.8 us (9%)
  Pallas kernels  8.76 us (7%)
  local copies, waits for them, and re-layouts  2.55 us (2%)
    all_to_all x4, blocking collectives, exchange(): lax.all_to_all(parts, axes, 0, 0, axis_index_groups=groups, tiled=True)  80.1 us
    ppermute x3, starting transfers between devices, local(): came_core.append(lax.ppermute(core_parts[step], 'x', shift))  8.51 us
    ppermute x1, starting transfers between devices, local(): came = lax.ppermute(send, 'c', swap)  7.63 us
    all_to_all x1, starting transfers between devices, exchange(): lax.all_to_all(parts, axes, 0, 0, axis_index_groups=groups, tiled=True)  6.82 us
    all_to_all x1, waiting for transfers between devices, exchange(): lax.all_to_all(parts, axes, 0, 0, axis_index_groups=groups, tiled=True)  5.5 us
    ppermute x1, starting transfers between devices, local(): other = lax.ppermute(own, 'c', swap)  3.82 us
    pallas_call x1, Pallas kernels, local(): pl.pallas_call(functools.partial(gram_kernel, layout), out_shape=(half_sh...  3.8 us
    ppermute x3, waiting for transfers between devices, local(): came_core.append(lax.ppermute(core_parts[step], 'x', shift))  3.18 us
  transfers between devices with their start and end apart: 6, of which 6 were waited for; matrix products, arithmetic and copies ran while one was open for 0% of the time, Pallas kernels for 1%

profile of v8, /device:TPU:1, one launch (start us, length us, event | category | flops | bytes accessed | tf_op | source)
XLA Modules:
  0.0 132.0 jit_solution(17828188386016882268)
XLA Ops:
  0.6 0.1 pad_add_fusion.place_ref
  0.7 0.0 copy-start
  0.7 1.6 %copy-done = f32[4,168,672]{2,1,0:T(8,128)S(1)} copy-done((f32[4,168,672]{2,1,0:T(8,128)S(1)}, f32[4,168,672]{2,1,0:T(8,128)}, u32[]{:S(2)}) %copy-start) | copy-done | bytes 1806360
  2.3 0.0 copy-start.1
  2.3 0.9 copy-done.1
  3.2 0.2 dense_blocks.1
  3.4 26.9 %all_to_all.25.dense_ref = f32[4,1056,128]{2,1,0:T(8,128)S(1)} all-to-all(f32[4,1056,128]{2,1,0:T(8,128)S(1)} %dense_blocks.1), channel_id=1, replica_groups=mesh['x'=4,'y'=8,'zh'=4,'zl'=2,'c'=2] {'x'}, dimensions={0} | all-to-all | bytes 4325376 | tf_op jit(solution)/shard_map/all_to_all | solution.py:210
  30.3 3.8 %local_grams.1 = (f32[2048,128]{1,0:T(8,128)S(1)}, f32[2048,128]{1,0:T(8,128)S(1)}, f32[128,672]{1,0:T(8,128)S(1)}) custom-call(s32[2]{0:T(128)S(1)} %pad_add_fusion.place_ref, f32[4,1056,128]{2,1,0:T(8,128)S(1)} %all_to_all.25.dense_ref), custom_call_target="tpu_custom_call" | custom-call | flops 1517322240 | bytes 5419008 | tf_op jit(solution)/shard_map/local_grams/pallas_call | solution.py:257
  34.1 7.6 %collective-permute-start = (f32[2048,128]{1,0:T(8,128)S(1)}, f32[2048,128]{1,0:T(8,128)S(1)}, u32[]{:S(2)}, u32[]{:S(2)}) collective-permute-start(f32[2048,128]{1,0:T(8,128)S(1)} %get-tuple-element.22), channel_id=1, source_target_pairs={{0,1},{1,0},{2,3},{3,2},{4,5},{5,4},{6,7},{7,6},{8,9},{9,8},{10,11... | collective-permute-start | bytes 3145736 | tf_op jit(solution)/shard_map/ppermute | solution.py:276
  41.7 2.3 %collective-permute-done.after_ref = f32[2048,128]{1,0:T(8,128)S(1)} collective-permute-done((f32[2048,128]{1,0:T(8,128)S(1)}, f32[2048,128]{1,0:T(8,128)S(1)}, u32[]{:S(2)}, u32[]{:S(2)}) %collective-permute-start) | collective-permute-done | bytes 1048608 | tf_op jit(solution)/shard_map/ppermute | solution.py:276
  44.0 1.1 add.3
  45.1 6.8 %all-to-all-start.1 = ((f32[8,256,128]{2,1,0:T(8,128)}), f32[8,256,128]{2,1,0:T(8,128)S(1)}, u32[]{:S(2)}, u32[]{:S(2)}) async-start(f32[8,256,128]{2,1,0:T(8,128)} %bitcast.2), calls=%async_computation.1 | async-start | bytes 2097152 | tf_op jit(solution)/shard_map/all_to_all | solution.py:210
  51.9 0.6 core_parts.1
  52.5 2.2 %collective-permute-start.1 = (f32[32,672]{1,0:T(8,128)S(1)}, f32[32,672]{1,0:T(8,128)S(1)}, u32[]{:S(2)}, u32[]{:S(2)}) collective-permute-start(f32[32,672]{1,0:T(8,128)S(1)} %get-tuple-element.25), channel_id=1, source_target_pairs={{0,128},{128,256},{256,384},{384,0},{1,129},{129,257},{257,385},{3... | collective-permute-start | bytes 258056 | tf_op jit(solution)/shard_map/ppermute | solution.py:291
  54.7 3.7 %collective-permute-start.2 = (f32[32,672]{1,0:T(8,128)S(1)}, f32[32,672]{1,0:T(8,128)S(1)}, u32[]{:S(2)}, u32[]{:S(2)}) collective-permute-start(f32[32,672]{1,0:T(8,128)S(1)} %get-tuple-element.26), channel_id=1, source_target_pairs={{0,256},{128,384},{256,0},{384,128},{1,257},{129,385},{257,1},{385... | collective-permute-start | bytes 258056 | tf_op jit(solution)/shard_map/ppermute | solution.py:291
  58.4 2.6 %collective-permute-start.3 = (f32[32,672]{1,0:T(8,128)S(1)}, f32[32,672]{1,0:T(8,128)S(1)}, u32[]{:S(2)}, u32[]{:S(2)}) collective-permute-start(f32[32,672]{1,0:T(8,128)S(1)} %get-tuple-element.27), channel_id=1, source_target_pairs={{0,384},{128,0},{256,128},{384,256},{1,385},{129,1},{257,129},{385... | collective-permute-start | bytes 258056 | tf_op jit(solution)/shard_map/ppermute | solution.py:291
  61.0 1.4 %collective-permute-done.1.refs_1_ = f32[32,672]{1,0:T(8,128)S(1)} collective-permute-done((f32[32,672]{1,0:T(8,128)S(1)}, f32[32,672]{1,0:T(8,128)S(1)}, u32[]{:S(2)}, u32[]{:S(2)}) %collective-permute-start.1) | collective-permute-done | bytes 86048 | tf_op jit(solution)/shard_map/ppermute | solution.py:291
  62.4 1.7 %collective-permute-done.2.refs_2_ = f32[32,672]{1,0:T(8,128)S(1)} collective-permute-done((f32[32,672]{1,0:T(8,128)S(1)}, f32[32,672]{1,0:T(8,128)S(1)}, u32[]{:S(2)}, u32[]{:S(2)}) %collective-permute-start.2) | collective-permute-done | bytes 86048 | tf_op jit(solution)/shard_map/ppermute | solution.py:291
  64.1 0.1 collective-permute-done.3.refs_3_
  64.2 5.5 %all-to-all-done.1 = f32[8,256,128]{2,1,0:T(8,128)S(1)} async-done(((f32[8,256,128]{2,1,0:T(8,128)}), f32[8,256,128]{2,1,0:T(8,128)S(1)}, u32[]{:S(2)}, u32[]{:S(2)}) %all-to-all-start.1) | async-done | bytes 1048608 | tf_op jit(solution)/shard_map/all_to_all | solution.py:210
  69.7 0.1 reduce_sum.18
  69.8 20.0 %all_to_all.26 = f32[32,8,128]{2,1,0:T(8,128)S(1)} all-to-all(f32[32,8,128]{2,1,0:T(8,128)S(1)} %bitcast.8), channel_id=1, replica_groups={{0,4,8,12,16,20,24,28,32,36,40,44,48,52,56,60,64,68,72,76,80,84,88,92,9..., dimensions={0} | all-to-all | bytes 262144 | tf_op jit(solution)/shard_map/all_to_all | solution.py:210
  89.8 13.0 %all_to_all.27 = f32[32,8,128]{2,1,0:T(8,128)S(1)} all-to-all(f32[32,8,128]{2,1,0:T(8,128)S(1)} %broadcast_in_dim.6), channel_id=1, replica_groups={{0,4,8,12,16,20,24,28,32,36,40,44,48,52,56,60,64,68,72,76,80,84,88,92,9..., dimensions={0} | all-to-all | bytes 262144 | tf_op jit(solution)/shard_map/all_to_all | solution.py:210
  102.8 0.1 broadcast_in_dim.15
  102.9 20.2 %all_to_all.28 = f32[8,256,128]{2,1,0:T(8,128)S(1)} all-to-all(f32[8,256,128]{2,1,0:T(8,128)S(1)} %broadcast_in_dim.15), channel_id=1, replica_groups={{0,2,128,130,256,258,384,386},{4,6,132,134,260,262,388,390},{8,10,136,1..., dimensions={0} | all-to-all | bytes 2097152 | tf_op jit(solution)/shard_map/all_to_all | solution.py:210
  123.1 3.8 %collective-permute-start.4 = (f32[2048,128]{1,0:T(8,128)S(1)}, f32[2048,128]{1,0:T(8,128)S(1)}, u32[]{:S(2)}, u32[]{:S(2)}) collective-permute-start(f32[2048,128]{1,0:T(8,128)S(1)} %bitcast.6), channel_id=1, source_target_pairs={{0,1},{1,0},{2,3},{3,2},{4,5},{5,4},{6,7},{7,6},{8,9},{9,8},{10,11... | collective-permute-start | bytes 3145736 | tf_op jit(solution)/shard_map/ppermute | solution.py:307
  126.9 1.4 %core_rows.1 = f32[32,4,672]{2,1,0:T(4,128)} custom-call(s32[2]{0:T(128)S(1)} %pad_add_fusion.place_ref, f32[32,672]{1,0:T(8,128)S(1)} %get-tuple-element.30.refs_0_, f32[32,672]{1,0:T(8,128)S(1)} %collective-permute-done.1.refs_1_, f32[32,672]{1,0:T(8,128)S(1)} %collective-permute-done.2.refs_2_, f32[32,672]{1,0:T(8,128)S(1)} %collective-permute-done.3.refs_3_), custom_call_target="tpu_custom_call" | custom-call | flops 86016 | bytes 688128 | tf_op jit(solution)/shard_map/core_rows/pallas_call | solution.py:295
  128.3 0.9 collective-permute-done.4.other_ref
  129.2 2.8 %mirror.1 = (f32[168,672]{1,0:T(8,128)}, f32[672,672]{1,0:T(8,128)}) custom-call(s32[2]{0:T(128)S(1)} %pad_add_fusion.place_ref, f32[2048,128]{1,0:T(8,128)S(1)} %bitcast.7, f32[2048,128]{1,0:T(8,128)S(1)} %collective-permute-done.4.other_ref), custom_call_target="tpu_custom_call" | custom-call | tf_op jit(solution)/shard_map/mirror/pallas_call | solution.py:309
  (2 shorter events, 0.0 us)
Async XLA Ops:
  0.7 1.6 %copy-start = (f32[4,168,672]{2,1,0:T(8,128)S(1)}, f32[4,168,672]{2,1,0:T(8,128)}, u32[]{:S(2)}) copy-start(f32[4,168,672]{2,1,0:T(8,128)} %field_ref.1) | copy-start | bytes 5419012
  2.3 0.9 copy-start.1
  34.1 9.9 %collective-permute-start = (f32[2048,128]{1,0:T(8,128)S(1)}, f32[2048,128]{1,0:T(8,128)S(1)}, u32[]{:S(2)}, u32[]{:S(2)}) collective-permute-start(f32[2048,128]{1,0:T(8,128)S(1)} %get-tuple-element.22), channel_id=1, source_target_pairs={{0,1},{1,0},{2,3},{3,2},{4,5},{5,4},{6,7},{7,6},{8,9},{9,8},{10,11... | collective-permute-start | bytes 3145736 | tf_op jit(solution)/shard_map/ppermute | solution.py:276
  45.1 24.6 %all-to-all-start.1 = ((f32[8,256,128]{2,1,0:T(8,128)}), f32[8,256,128]{2,1,0:T(8,128)S(1)}, u32[]{:S(2)}, u32[]{:S(2)}) async-start(f32[8,256,128]{2,1,0:T(8,128)} %bitcast.2), calls=%async_computation.1 | async-start | bytes 2097152 | tf_op jit(solution)/shard_map/all_to_all | solution.py:210
  52.5 9.9 %collective-permute-start.1 = (f32[32,672]{1,0:T(8,128)S(1)}, f32[32,672]{1,0:T(8,128)S(1)}, u32[]{:S(2)}, u32[]{:S(2)}) collective-permute-start(f32[32,672]{1,0:T(8,128)S(1)} %get-tuple-element.25), channel_id=1, source_target_pairs={{0,128},{128,256},{256,384},{384,0},{1,129},{129,257},{257,385},{3... | collective-permute-start | bytes 258056 | tf_op jit(solution)/shard_map/ppermute | solution.py:291
  54.7 9.4 %collective-permute-start.2 = (f32[32,672]{1,0:T(8,128)S(1)}, f32[32,672]{1,0:T(8,128)S(1)}, u32[]{:S(2)}, u32[]{:S(2)}) collective-permute-start(f32[32,672]{1,0:T(8,128)S(1)} %get-tuple-element.26), channel_id=1, source_target_pairs={{0,256},{128,384},{256,0},{384,128},{1,257},{129,385},{257,1},{385... | collective-permute-start | bytes 258056 | tf_op jit(solution)/shard_map/ppermute | solution.py:291
  58.4 5.8 %collective-permute-start.3 = (f32[32,672]{1,0:T(8,128)S(1)}, f32[32,672]{1,0:T(8,128)S(1)}, u32[]{:S(2)}, u32[]{:S(2)}) collective-permute-start(f32[32,672]{1,0:T(8,128)S(1)} %get-tuple-element.27), channel_id=1, source_target_pairs={{0,384},{128,0},{256,128},{384,256},{1,385},{129,1},{257,129},{385... | collective-permute-start | bytes 258056 | tf_op jit(solution)/shard_map/ppermute | solution.py:291
  123.1 6.1 %collective-permute-start.4 = (f32[2048,128]{1,0:T(8,128)S(1)}, f32[2048,128]{1,0:T(8,128)S(1)}, u32[]{:S(2)}, u32[]{:S(2)}) collective-permute-start(f32[2048,128]{1,0:T(8,128)S(1)} %bitcast.6), channel_id=1, source_target_pairs={{0,1},{1,0},{2,3},{3,2},{4,5},{5,4},{6,7},{7,6},{8,9},{9,8},{10,11... | collective-permute-start | bytes 3145736 | tf_op jit(solution)/shard_map/ppermute | solution.py:307

commit v9 on v8

--- a/solution.py
+++ b/solution.py
@@ -221,10 +221,12 @@
 def both_groups(sizes):
     shape = tuple(sizes.values())
     index = np.arange(np.prod(shape)).reshape(shape)
-    near = [index[:, b, d, :, 0] for b, d in np.ndindex(shape[1], shape[2])]
-    near += [index[a, :, d, e, 1] for a, d, e in np.ndindex(shape[0], shape[2], shape[3])]
-    far = [index[a, :, :, e, 0] for a, e in np.ndindex(shape[0], shape[3])]
-    far += [index[:, b, :, :, 1] for b in range(shape[1])]
+    near, far = [], []
+    for core in range(shape[3]):
+        places = np.roll(index[..., core], core - 1, axis=(0, 1, 2))
+        places = places.reshape(shape[0] // 2, 2, shape[1] // 2, 2, shape[2] // 2, 2)
+        near += [places[a, :, b, :, d, :] for a, b, d in np.ndindex(places.shape[::2])]
+        far += [places[:, a, :, b, :, d] for a, b, d in np.ndindex(2, 2, 2)]
     return [[group.reshape(-1).tolist() for group in groups] for groups in (near, far)]
 
 
@@ -323,9 +325,9 @@
 
 def solution(mesh):
     gx, rest = mesh.devices.shape
-    sizes = {"x": gx, "y": 8, "zh": rest // 32, "zl": 2, "c": 2}
+    sizes = {"x": gx, "y": 8, "z": rest // 16, "c": 2}
     fine = Mesh(mesh.devices.reshape(tuple(sizes.values())), tuple(sizes))
-    spread = ("y", "zh", "zl", "c")
+    spread = ("y", "z", "c")
     in_specs = (P(spread, "x", None), P("x", None))
     out_specs = (P("x", None), P("x", spread, None), P())
     return jax.shard_map(

time: 132 us -> 138 us (1.045)
  blocking collectives: 80.1 us -> 91.1 us
  waiting for transfers between devices: 11.8 us -> 6.25 us
    all_to_all x4, blocking collectives: 80.1 us -> 91.1 us  [exchange(): lax.all_to_all(parts, axes, 0, 0, axis_index_groups=groups, tiled=True)]
    all_to_all x1, waiting for transfers between devices: 5.5 us -> 0.01 us  [exchange(): lax.all_to_all(parts, axes, 0, 0, axis_index_groups=groups, tiled=True)]
    all_to_all x1, starting transfers between devices: 6.82 us -> 4.38 us  [exchange(): lax.all_to_all(parts, axes, 0, 0, axis_index_groups=groups, tiled=True)]
    ppermute x1, starting transfers between devices: 3.82 us -> 5.27 us  [local(): other = lax.ppermute(own, 'c', swap)]
  transfers between devices with their start and end apart: 6 -> 6, of which waited for: 6 -> 4; matrix products, arithmetic and copies ran while one was open for 0% -> 0% of each run, Pallas kernels for 1% -> 1%
where the time goes in v9:
time: 138 us
  blocking collectives  91.1 us (66%)
  starting transfers between devices  26.9 us (19%)
  Pallas kernels  8.76 us (6%)
  waiting for transfers between devices  6.25 us (5%)
  local copies, waits for them, and re-layouts  2.55 us (2%)
    all_to_all x4, blocking collectives, exchange(): lax.all_to_all(parts, axes, 0, 0, axis_index_groups=groups, tiled=True)  91.1 us
    ppermute x3, starting transfers between devices, local(): came_core.append(lax.ppermute(core_parts[step], 'x', shift))  9.59 us
    ppermute x1, starting transfers between devices, local(): came = lax.ppermute(send, 'c', swap)  7.63 us
    ppermute x1, starting transfers between devices, local(): other = lax.ppermute(own, 'c', swap)  5.27 us
    all_to_all x1, starting transfers between devices, exchange(): lax.all_to_all(parts, axes, 0, 0, axis_index_groups=groups, tiled=True)  4.38 us
    pallas_call x1, Pallas kernels, local(): pl.pallas_call(functools.partial(gram_kernel, layout), out_shape=(half_sh...  3.8 us
    ppermute x3, waiting for transfers between devices, local(): came_core.append(lax.ppermute(core_parts[step], 'x', shift))  3.11 us
    pallas_call x1, Pallas kernels, local(): pl.pallas_call(functools.partial(unpack_kernel, layout, 1.0 / (slices_all...  2.81 us
  transfers between devices with their start and end apart: 6, of which 4 were waited for; matrix products, arithmetic and copies ran while one was open for 0% of the time, Pallas kernels for 1%

profile of v9, /device:TPU:1, one launch (start us, length us, event | category | flops | bytes accessed | tf_op | source)
XLA Modules:
  0.0 137.5 jit_solution(12766920455991674813)
XLA Ops:
  0.6 0.1 pad_add_fusion.place_ref
  0.7 0.0 copy-start
  0.7 1.6 %copy-done = f32[4,168,672]{2,1,0:T(8,128)S(1)} copy-done((f32[4,168,672]{2,1,0:T(8,128)S(1)}, f32[4,168,672]{2,1,0:T(8,128)}, u32[]{:S(2)}) %copy-start) | copy-done | bytes 1806360
  2.3 0.0 copy-start.1
  2.3 0.9 copy-done.1
  3.2 0.2 dense_blocks.1
  3.4 26.9 %all_to_all.25.dense_ref = f32[4,1056,128]{2,1,0:T(8,128)S(1)} all-to-all(f32[4,1056,128]{2,1,0:T(8,128)S(1)} %dense_blocks.1), channel_id=1, replica_groups=mesh['x'=4,'y'=8,'z'=8,'c'=2] {'x'}, dimensions={0} | all-to-all | bytes 4325376 | tf_op jit(solution)/shard_map/all_to_all | solution.py:210
  30.3 3.8 %local_grams.1 = (f32[2048,128]{1,0:T(8,128)S(1)}, f32[2048,128]{1,0:T(8,128)S(1)}, f32[128,672]{1,0:T(8,128)S(1)}) custom-call(s32[2]{0:T(128)S(1)} %pad_add_fusion.place_ref, f32[4,1056,128]{2,1,0:T(8,128)S(1)} %all_to_all.25.dense_ref), custom_call_target="tpu_custom_call" | custom-call | flops 1517322240 | bytes 5419008 | tf_op jit(solution)/shard_map/local_grams/pallas_call | solution.py:259
  34.1 7.6 %collective-permute-start = (f32[2048,128]{1,0:T(8,128)S(1)}, f32[2048,128]{1,0:T(8,128)S(1)}, u32[]{:S(2)}, u32[]{:S(2)}) collective-permute-start(f32[2048,128]{1,0:T(8,128)S(1)} %get-tuple-element.22), channel_id=1, source_target_pairs={{0,1},{1,0},{2,3},{3,2},{4,5},{5,4},{6,7},{7,6},{8,9},{9,8},{10,11... | collective-permute-start | bytes 3145736 | tf_op jit(solution)/shard_map/ppermute | solution.py:278
  41.7 2.3 %collective-permute-done.after_ref = f32[2048,128]{1,0:T(8,128)S(1)} collective-permute-done((f32[2048,128]{1,0:T(8,128)S(1)}, f32[2048,128]{1,0:T(8,128)S(1)}, u32[]{:S(2)}, u32[]{:S(2)}) %collective-permute-start) | collective-permute-done | bytes 1048608 | tf_op jit(solution)/shard_map/ppermute | solution.py:278
  44.0 1.1 add.3
  45.1 4.4 %all-to-all-start.1 = ((f32[8,256,128]{2,1,0:T(8,128)}), f32[8,256,128]{2,1,0:T(8,128)S(1)}, u32[]{:S(2)}, u32[]{:S(2)}) async-start(f32[8,256,128]{2,1,0:T(8,128)} %bitcast.2), calls=%async_computation.1 | async-start | bytes 2097152 | tf_op jit(solution)/shard_map/all_to_all | solution.py:210
  49.4 0.6 core_parts.1
  50.0 3.4 %collective-permute-start.1 = (f32[32,672]{1,0:T(8,128)S(1)}, f32[32,672]{1,0:T(8,128)S(1)}, u32[]{:S(2)}, u32[]{:S(2)}) collective-permute-start(f32[32,672]{1,0:T(8,128)S(1)} %get-tuple-element.25), channel_id=1, source_target_pairs={{0,128},{128,256},{256,384},{384,0},{1,129},{129,257},{257,385},{3... | collective-permute-start | bytes 258056 | tf_op jit(solution)/shard_map/ppermute | solution.py:293
  53.4 3.7 %collective-permute-start.2 = (f32[32,672]{1,0:T(8,128)S(1)}, f32[32,672]{1,0:T(8,128)S(1)}, u32[]{:S(2)}, u32[]{:S(2)}) collective-permute-start(f32[32,672]{1,0:T(8,128)S(1)} %get-tuple-element.26), channel_id=1, source_target_pairs={{0,256},{128,384},{256,0},{384,128},{1,257},{129,385},{257,1},{385... | collective-permute-start | bytes 258056 | tf_op jit(solution)/shard_map/ppermute | solution.py:293
  57.1 2.5 %collective-permute-start.3 = (f32[32,672]{1,0:T(8,128)S(1)}, f32[32,672]{1,0:T(8,128)S(1)}, u32[]{:S(2)}, u32[]{:S(2)}) collective-permute-start(f32[32,672]{1,0:T(8,128)S(1)} %get-tuple-element.27), channel_id=1, source_target_pairs={{0,384},{128,0},{256,128},{384,256},{1,385},{129,1},{257,129},{385... | collective-permute-start | bytes 258056 | tf_op jit(solution)/shard_map/ppermute | solution.py:293
  59.6 0.0 collective-permute-done.1.refs_1_
  59.7 2.0 %collective-permute-done.2.refs_2_ = f32[32,672]{1,0:T(8,128)S(1)} collective-permute-done((f32[32,672]{1,0:T(8,128)S(1)}, f32[32,672]{1,0:T(8,128)S(1)}, u32[]{:S(2)}, u32[]{:S(2)}) %collective-permute-start.2) | collective-permute-done | bytes 86048 | tf_op jit(solution)/shard_map/ppermute | solution.py:293
  61.7 1.1 collective-permute-done.3.refs_3_
  62.8 0.0 all-to-all-done.1
  62.8 0.1 reduce_sum.18
  62.8 29.1 %all_to_all.26 = f32[32,8,128]{2,1,0:T(8,128)S(1)} all-to-all(f32[32,8,128]{2,1,0:T(8,128)S(1)} %bitcast.8), channel_id=1, replica_groups={{146,150,154,158,178,182,186,190,210,214,218,222,242,246,250,254,402,40..., dimensions={0} | all-to-all | bytes 262144 | tf_op jit(solution)/shard_map/all_to_all | solution.py:210
  92.0 17.4 %all_to_all.27 = f32[32,8,128]{2,1,0:T(8,128)S(1)} all-to-all(f32[32,8,128]{2,1,0:T(8,128)S(1)} %broadcast_in_dim.6), channel_id=1, replica_groups={{146,150,154,158,178,182,186,190,210,214,218,222,242,246,250,254,402,40..., dimensions={0} | all-to-all | bytes 262144 | tf_op jit(solution)/shard_map/all_to_all | solution.py:210
  109.3 0.1 broadcast_in_dim.15
  109.4 17.7 %all_to_all.28 = f32[8,256,128]{2,1,0:T(8,128)S(1)} all-to-all(f32[8,256,128]{2,1,0:T(8,128)S(1)} %broadcast_in_dim.15), channel_id=1, replica_groups={{146,148,162,164,274,276,290,292},{150,152,166,168,278,280,294,296},{15..., dimensions={0} | all-to-all | bytes 2097152 | tf_op jit(solution)/shard_map/all_to_all | solution.py:210
  127.2 5.3 %collective-permute-start.4 = (f32[2048,128]{1,0:T(8,128)S(1)}, f32[2048,128]{1,0:T(8,128)S(1)}, u32[]{:S(2)}, u32[]{:S(2)}) collective-permute-start(f32[2048,128]{1,0:T(8,128)S(1)} %bitcast.6), channel_id=1, source_target_pairs={{0,1},{1,0},{2,3},{3,2},{4,5},{5,4},{6,7},{7,6},{8,9},{9,8},{10,11... | collective-permute-start | bytes 3145736 | tf_op jit(solution)/shard_map/ppermute | solution.py:309
  132.4 1.4 %core_rows.1 = f32[32,4,672]{2,1,0:T(4,128)} custom-call(s32[2]{0:T(128)S(1)} %pad_add_fusion.place_ref, f32[32,672]{1,0:T(8,128)S(1)} %get-tuple-element.30.refs_0_, f32[32,672]{1,0:T(8,128)S(1)} %collective-permute-done.1.refs_1_, f32[32,672]{1,0:T(8,128)S(1)} %collective-permute-done.2.refs_2_, f32[32,672]{1,0:T(8,128)S(1)} %collective-permute-done.3.refs_3_), custom_call_target="tpu_custom_call" | custom-call | flops 86016 | bytes 688128 | tf_op jit(solution)/shard_map/core_rows/pallas_call | solution.py:297
  133.8 0.9 collective-permute-done.4.other_ref
  134.7 2.8 %mirror.1 = (f32[168,672]{1,0:T(8,128)}, f32[672,672]{1,0:T(8,128)}) custom-call(s32[2]{0:T(128)S(1)} %pad_add_fusion.place_ref, f32[2048,128]{1,0:T(8,128)S(1)} %bitcast.7, f32[2048,128]{1,0:T(8,128)S(1)} %collective-permute-done.4.other_ref), custom_call_target="tpu_custom_call" | custom-call | tf_op jit(solution)/shard_map/mirror/pallas_call | solution.py:311
  (2 shorter events, 0.0 us)
Async XLA Ops:
  0.7 1.6 %copy-start = (f32[4,168,672]{2,1,0:T(8,128)S(1)}, f32[4,168,672]{2,1,0:T(8,128)}, u32[]{:S(2)}) copy-start(f32[4,168,672]{2,1,0:T(8,128)} %field_ref.1) | copy-start | bytes 5419012
  2.3 0.9 copy-start.1
  34.1 9.9 %collective-permute-start = (f32[2048,128]{1,0:T(8,128)S(1)}, f32[2048,128]{1,0:T(8,128)S(1)}, u32[]{:S(2)}, u32[]{:S(2)}) collective-permute-start(f32[2048,128]{1,0:T(8,128)S(1)} %get-tuple-element.22), channel_id=1, source_target_pairs={{0,1},{1,0},{2,3},{3,2},{4,5},{5,4},{6,7},{7,6},{8,9},{9,8},{10,11... | collective-permute-start | bytes 3145736 | tf_op jit(solution)/shard_map/ppermute | solution.py:278
  45.1 17.7 %all-to-all-start.1 = ((f32[8,256,128]{2,1,0:T(8,128)}), f32[8,256,128]{2,1,0:T(8,128)S(1)}, u32[]{:S(2)}, u32[]{:S(2)}) async-start(f32[8,256,128]{2,1,0:T(8,128)} %bitcast.2), calls=%async_computation.1 | async-start | bytes 2097152 | tf_op jit(solution)/shard_map/all_to_all | solution.py:210
  50.0 9.6 %collective-permute-start.1 = (f32[32,672]{1,0:T(8,128)S(1)}, f32[32,672]{1,0:T(8,128)S(1)}, u32[]{:S(2)}, u32[]{:S(2)}) collective-permute-start(f32[32,672]{1,0:T(8,128)S(1)} %get-tuple-element.25), channel_id=1, source_target_pairs={{0,128},{128,256},{256,384},{384,0},{1,129},{129,257},{257,385},{3... | collective-permute-start | bytes 258056 | tf_op jit(solution)/shard_map/ppermute | solution.py:293
  53.4 8.3 %collective-permute-start.2 = (f32[32,672]{1,0:T(8,128)S(1)}, f32[32,672]{1,0:T(8,128)S(1)}, u32[]{:S(2)}, u32[]{:S(2)}) collective-permute-start(f32[32,672]{1,0:T(8,128)S(1)} %get-tuple-element.26), channel_id=1, source_target_pairs={{0,256},{128,384},{256,0},{384,128},{1,257},{129,385},{257,1},{385... | collective-permute-start | bytes 258056 | tf_op jit(solution)/shard_map/ppermute | solution.py:293
  57.1 5.7 %collective-permute-start.3 = (f32[32,672]{1,0:T(8,128)S(1)}, f32[32,672]{1,0:T(8,128)S(1)}, u32[]{:S(2)}, u32[]{:S(2)}) collective-permute-start(f32[32,672]{1,0:T(8,128)S(1)} %get-tuple-element.27), channel_id=1, source_target_pairs={{0,384},{128,0},{256,128},{384,256},{1,385},{129,1},{257,129},{385... | collective-permute-start | bytes 258056 | tf_op jit(solution)/shard_map/ppermute | solution.py:293
  127.2 7.5 %collective-permute-start.4 = (f32[2048,128]{1,0:T(8,128)S(1)}, f32[2048,128]{1,0:T(8,128)S(1)}, u32[]{:S(2)}, u32[]{:S(2)}) collective-permute-start(f32[2048,128]{1,0:T(8,128)S(1)} %bitcast.6), channel_id=1, source_target_pairs={{0,1},{1,0},{2,3},{3,2},{4,5},{5,4},{6,7},{7,6},{8,9},{9,8},{10,11... | collective-permute-start | bytes 3145736 | tf_op jit(solution)/shard_map/ppermute | solution.py:309

commit v10 on v8

--- a/solution.py
+++ b/solution.py
@@ -11,7 +11,7 @@
 LANES = 128
 FOLD = LANES // 2
 VMEM = pl.BlockSpec(memory_space=pltpu.VMEM)
-SMEM = pl.BlockSpec(memory_space=pltpu.SMEM)
+ANY = pl.BlockSpec(memory_space=pl.ANY)
 ROOM = pltpu.CompilerParams(vmem_limit_bytes=24 << 20)
 
 
@@ -109,7 +109,7 @@
 
 
 def gram_kernel(
-    layout, place_ref, dense_ref, keep_ref, send_ref, core_ref,
+    layout, dense_ref, keep_ref, send_ref, core_ref,
     field, basis, field_high, field_low, left_side, right_side, packed,
 ):
     blocks = dense_ref.shape[0]
@@ -151,59 +151,87 @@
 
     pack_gram(layout, field_product, packed, 0)
     pack_gram(layout, core_product, packed, 1)
-    mine = place_ref[1]
+    mine = lax.axis_index("c")
     keep_ref[...] = packed[mine]
     send_ref[...] = packed[1 - mine]
 
 
-def parts_kernel(place_ref, core_ref, after_ref, *out_refs):
+def parts_kernel(core_ref, after_ref, *out_refs):
     owned = out_refs[0].shape[0]
     for step, out_ref in enumerate(out_refs):
-        owner = lax.rem(place_ref[0] + step, len(out_refs))
+        owner = lax.rem(lax.axis_index("x") + step, len(out_refs))
         out_ref[...] = core_ref[pl.ds(pl.multiple_of(owner * owned, 8), owned), :]
 
 
-def rows_kernel(place_ref, *refs):
+def rows_kernel(*refs):
     came, (out_ref, ordered) = refs[:-2], refs[-2:]
     count = len(came)
     for step, ref in enumerate(came):
-        ordered[lax.rem(place_ref[0] + count - step, count)] = ref[...]
+        ordered[lax.rem(lax.axis_index("x") + count - step, count)] = ref[...]
     for owner in range(count):
         out_ref[:, owner, :] = ordered[owner]
 
 
-def unpack(layout, packed, half, out_ref, scale):
+def unpack_rows(layout, packed, half, block, out_ref, scale):
     full, left = layout.full, layout.left
-    for block in range(full):
-        columns = pl.ds(block * LANES, LANES)
-        for row in range(block):
-            there = pl.ds(row * LANES, LANES)
-            tile = packed[half, pl.ds(layout.above[block] + row * LANES, LANES), :] * scale
-            out_ref[there, columns] = tile
-            out_ref[columns, there] = tile.T
-        into, row = layout.fold[block]
-        upper = packed[into, pl.ds(row + half * FOLD, FOLD), :] * scale
-        lower = packed[into, pl.ds(row + 2 * FOLD, FOLD), :] * scale
-        if half == 0:
-            lower = pltpu.roll(lower, FOLD, 1)
-        turned = jnp.concatenate([upper, upper], axis=0).T[FOLD:]
-        out_ref[pl.ds(block * LANES, FOLD), columns] = upper
-        out_ref[pl.ds(block * LANES + FOLD, FOLD), columns] = jnp.where(lane_below(FOLD), turned, lower)
-        tile = packed[half, pl.ds(layout.strip + block * left, left), :] * scale
-        out_ref[pl.ds(full * LANES, left), columns] = tile
-        out_ref[columns, pl.ds(full * LANES, left)] = tile.T
-    corner = packed[half, pl.ds(layout.strip + full * left, left), :] * scale
-    out_ref[pl.ds(full * LANES, left), pl.ds(full * LANES, left)] = corner[:, 0:left]
-
-
-def unpack_kernel(layout, scale_one, scale_two, place_ref, own_ref, other_ref, one_ref, two_ref, packed, whole):
-    rows = one_ref.shape[0]
-    mine = place_ref[1]
+    last = pl.ds(full * LANES, left)
+    if block == full:
+        for column in range(full):
+            piece = packed[half, pl.ds(layout.strip + column * left, left), :]
+            out_ref[last, pl.ds(column * LANES, LANES)] = piece * scale
+        corner = packed[half, pl.ds(layout.strip + full * left, left), :] * scale
+        out_ref[last, last] = corner[:, 0:left]
+        return
+    rows = pl.ds(block * LANES, LANES)
+    for column in range(full):
+        columns = pl.ds(column * LANES, LANES)
+        if column > block:
+            out_ref[rows, columns] = packed[half, pl.ds(layout.above[column] + block * LANES, LANES), :] * scale
+        elif column < block:
+            tile = packed[half, pl.ds(layout.above[block] + column * LANES, LANES), :] * scale
+            out_ref[rows, columns] = tile.T
+        else:
+            into, row = layout.fold[block]
+            upper = packed[into, pl.ds(row + half * FOLD, FOLD), :] * scale
+            lower = packed[into, pl.ds(row + 2 * FOLD, FOLD), :] * scale
+            if half == 0:
+                lower = pltpu.roll(lower, FOLD, 1)
+            turned = jnp.concatenate([upper, upper], axis=0).T[FOLD:]
+            out_ref[pl.ds(block * LANES, FOLD), columns] = upper
+            out_ref[pl.ds(block * LANES + FOLD, FOLD), columns] = jnp.where(lane_below(FOLD), turned, lower)
+    piece = packed[half, pl.ds(layout.strip + block * left, left), :] * scale
+    out_ref[rows, last] = piece.T
+
+
+def unpack_kernel(
+    layout, scale_one, scale_two, own_ref, other_ref, one_ref, two_ref, packed, whole_one, whole_two, sent
+):
+    width = layout.width
+    mine = lax.axis_index("c")
     packed[mine] = own_ref[...]
     packed[1 - mine] = other_ref[...]
-    unpack(layout, packed, 0, whole, scale_one)
-    one_ref[...] = whole[pl.ds(pl.multiple_of(place_ref[0] * rows, 8), rows), :]
-    unpack(layout, packed, 1, two_ref, scale_two)
+    moves = []
+    for block in range(layout.full + 1):
+        unpack_rows(layout, packed, 1, block, whole_two, scale_two)
+        rows = pl.ds(block * LANES, min(LANES, width - block * LANES))
+        move = pltpu.make_async_copy(whole_two.at[rows, :], two_ref.at[rows, :], sent.at[block])
+        move.start()
+        moves.append(move)
+    place = lax.axis_index("x")
+    owned = one_ref.shape[0]
+    for owner in range(width // owned):
+
+        @pl.when(place == owner)
+        def _():
+            for block in range(owner * owned // LANES, ((owner + 1) * owned - 1) // LANES + 1):
+                unpack_rows(layout, packed, 0, block, whole_one, scale_one)
+
+    rows = pl.ds(pl.multiple_of(place * owned, 8), owned)
+    move = pltpu.make_async_copy(whole_one.at[rows, :], one_ref, sent.at[layout.full + 1])
+    move.start()
+    moves.append(move)
+    for move in moves:
+        move.wait()
 
 
 def exchange(parts, axes, groups=None):
@@ -240,7 +268,6 @@
     layout = Layout(first, 8 * near_count * far_count)
     dense = dense_rows(rows_here, second)[-1]
     swap = [(i, sizes["c"] - 1 - i) for i in range(sizes["c"])]
-    place = jnp.stack([lax.axis_index("x"), lax.axis_index("c")]).astype(jnp.int32)
     f32, bf16 = jnp.float32, jnp.bfloat16
 
     blocks = pl.pallas_call(
@@ -251,13 +278,12 @@
         compiler_params=ROOM,
         name="dense_blocks",
     )(tensor, basis)
-    blocks, place = lax.optimization_barrier((blocks, place))
     blocks = exchange(blocks, "x")
     half_shape = jax.ShapeDtypeStruct((layout.rows, LANES), f32)
     keep, send, core = pl.pallas_call(
         functools.partial(gram_kernel, layout),
         out_shape=(half_shape, half_shape, jax.ShapeDtypeStruct((rank, second), f32)),
-        in_specs=[SMEM, VMEM],
+        in_specs=[VMEM],
         out_specs=(VMEM, VMEM, VMEM),
         scratch_shapes=[
             pltpu.VMEM((first, second), f32),
@@ -271,7 +297,7 @@
         compiler_params=ROOM,
         cost_estimate=cost(5 * first * first * second, 12 * first * second),
         name="local_grams",
-    )(place, blocks)
+    )(blocks)
 
     came = lax.ppermute(send, "c", swap)
     sums = keep + came
@@ -279,12 +305,12 @@
     core_parts = pl.pallas_call(
         parts_kernel,
         out_shape=[jax.ShapeDtypeStruct((owned, second), f32)] * gx,
-        in_specs=[SMEM, VMEM, pl.BlockSpec(memory_space=pl.ANY)],
+        in_specs=[VMEM, ANY],
         out_specs=[VMEM] * gx,
         compiler_params=ROOM,
         cost_estimate=cost(rank * second, 8 * rank * second),
         name="core_parts",
-    )(place, core, came)
+    )(core, came)
     came_core = [core_parts[0]]
     for step in range(1, gx):
         shift = [(i, (i + step) % gx) for i in range(gx)]
@@ -295,13 +321,13 @@
     core_out = pl.pallas_call(
         rows_kernel,
         out_shape=jax.ShapeDtypeStruct((owned, gx, second), f32),
-        in_specs=[SMEM] + [VMEM] * gx,
+        in_specs=[VMEM] * gx,
         out_specs=VMEM,
         scratch_shapes=[pltpu.VMEM((gx, owned, second), f32)],
         compiler_params=ROOM,
         cost_estimate=cost(rank * second, 8 * rank * second),
         name="core_rows",
-    )(place, *came_core)
+    )(*came_core)
     part = exchange(copies(jnp.sum(part, axis=0), far_count), axes, far).reshape(-1, LANES)
     own = exchange(copies(part, near_count), axes, near).reshape(-1, LANES)
     other = lax.ppermute(own, "c", swap)
@@ -312,12 +338,17 @@
             jax.ShapeDtypeStruct((rows_here, first), f32),
             jax.ShapeDtypeStruct((second, second), f32),
         ),
-        in_specs=[SMEM, VMEM, VMEM],
-        out_specs=(VMEM, VMEM),
-        scratch_shapes=[pltpu.VMEM((2, layout.rows, LANES), f32), pltpu.VMEM((first, first), f32)],
+        in_specs=[VMEM, VMEM],
+        out_specs=(ANY, ANY),
+        scratch_shapes=[
+            pltpu.VMEM((2, layout.rows, LANES), f32),
+            pltpu.VMEM((first, first), f32),
+            pltpu.VMEM((second, second), f32),
+            pltpu.SemaphoreType.DMA((layout.full + 2,)),
+        ],
         compiler_params=ROOM,
         name="mirror",
-    )(place, own, other)
+    )(own, other)
     return gram_one, core_out, gram_two
 
 

time: 132 us -> 130 us (0.985)
  Pallas kernels: 8.76 us -> 6.25 us
  transfers between devices with their start and end apart: 6 -> 6, of which waited for: 6 -> 5; matrix products, arithmetic and copies ran while one was open for 0% -> 0% of each run, Pallas kernels for 1% -> 1%
where the time goes in v10:
time: 130 us
  blocking collectives  80.3 us (62%)
  starting transfers between devices  26.1 us (20%)
  waiting for transfers between devices  12.9 us (10%)
  Pallas kernels  6.25 us (5%)
  local copies, waits for them, and re-layouts  2.54 us (2%)
    all_to_all x4, blocking collectives, exchange(): lax.all_to_all(parts, axes, 0, 0, axis_index_groups=groups, tiled=True)  80.3 us
    ppermute x3, starting transfers between devices, local(): came_core.append(lax.ppermute(core_parts[step], 'x', shift))  8.51 us
    ppermute x1, starting transfers between devices, local(): came = lax.ppermute(send, 'c', swap)  7.62 us
    all_to_all x1, starting transfers between devices, exchange(): lax.all_to_all(parts, axes, 0, 0, axis_index_groups=groups, tiled=True)  6.82 us
    all_to_all x1, waiting for transfers between devices, exchange(): lax.all_to_all(parts, axes, 0, 0, axis_index_groups=groups, tiled=True)  5.59 us
    ppermute x3, waiting for transfers between devices, local(): came_core.append(lax.ppermute(core_parts[step], 'x', shift))  3.65 us
    pallas_call x1, Pallas kernels, local(): pl.pallas_call(functools.partial(gram_kernel, layout), out_shape=(half_sh...  3.42 us
    ppermute x1, starting transfers between devices, local(): other = lax.ppermute(own, 'c', swap)  3.12 us
  transfers between devices with their start and end apart: 6, of which 5 were waited for; matrix products, arithmetic and copies ran while one was open for 0% of the time, Pallas kernels for 1%

profile of v10, /device:TPU:1, one launch (start us, length us, event | category | flops | bytes accessed | tf_op | source)
XLA Modules:
  0.0 129.9 jit_solution(13738734258804933796)
XLA Ops:
  0.6 0.0 copy-start
  0.6 1.6 %copy-done = f32[4,168,672]{2,1,0:T(8,128)S(1)} copy-done((f32[4,168,672]{2,1,0:T(8,128)S(1)}, f32[4,168,672]{2,1,0:T(8,128)}, u32[]{:S(2)}) %copy-start) | copy-done | bytes 1806360
  2.2 0.0 copy-start.1
  2.2 0.9 copy-done.1
  3.1 0.2 dense_blocks.1
  3.3 26.9 %all_to_all.25.dense_ref = f32[4,1056,128]{2,1,0:T(8,128)S(1)} all-to-all(f32[4,1056,128]{2,1,0:T(8,128)S(1)} %dense_blocks.1), channel_id=1, replica_groups=mesh['x'=4,'y'=8,'zh'=4,'zl'=2,'c'=2] {'x'}, dimensions={0} | all-to-all | bytes 4325376 | tf_op jit(solution)/shard_map/all_to_all | solution.py:238
  30.2 3.4 %local_grams.1 = (f32[2048,128]{1,0:T(8,128)S(1)}, f32[2048,128]{1,0:T(8,128)S(1)}, f32[128,672]{1,0:T(8,128)S(1)}) custom-call(f32[4,1056,128]{2,1,0:T(8,128)S(1)} %all_to_all.25.dense_ref), custom_call_target="tpu_custom_call" | custom-call | flops 1517322240 | bytes 5419008 | tf_op jit(solution)/shard_map/local_grams/pallas_call | solution.py:283
  33.6 7.6 %collective-permute-start = (f32[2048,128]{1,0:T(8,128)S(1)}, f32[2048,128]{1,0:T(8,128)S(1)}, u32[]{:S(2)}, u32[]{:S(2)}) collective-permute-start(f32[2048,128]{1,0:T(8,128)S(1)} %get-tuple-element.18), channel_id=1, source_target_pairs={{0,1},{1,0},{2,3},{3,2},{4,5},{5,4},{6,7},{7,6},{8,9},{9,8},{10,11... | collective-permute-start | bytes 3145736 | tf_op jit(solution)/shard_map/ppermute | solution.py:302
  41.2 2.3 %collective-permute-done.after_ref = f32[2048,128]{1,0:T(8,128)S(1)} collective-permute-done((f32[2048,128]{1,0:T(8,128)S(1)}, f32[2048,128]{1,0:T(8,128)S(1)}, u32[]{:S(2)}, u32[]{:S(2)}) %collective-permute-start) | collective-permute-done | bytes 1048608 | tf_op jit(solution)/shard_map/ppermute | solution.py:302
  43.5 1.1 add.3
  44.6 6.8 %all-to-all-start.1 = ((f32[8,256,128]{2,1,0:T(8,128)}), f32[8,256,128]{2,1,0:T(8,128)S(1)}, u32[]{:S(2)}, u32[]{:S(2)}) async-start(f32[8,256,128]{2,1,0:T(8,128)} %bitcast), calls=%async_computation.1 | async-start | bytes 2097152 | tf_op jit(solution)/shard_map/all_to_all | solution.py:238
  51.4 2.2 %collective-permute-start.1 = (f32[32,672]{1,0:T(8,128)S(1)}, f32[32,672]{1,0:T(8,128)S(1)}, u32[]{:S(2)}, u32[]{:S(2)}) collective-permute-start(f32[32,672]{1,0:T(8,128)S(1)} %get-tuple-element.21), channel_id=1, source_target_pairs={{0,128},{128,256},{256,384},{384,0},{1,129},{129,257},{257,385},{3... | collective-permute-start | bytes 258056 | tf_op jit(solution)/shard_map/ppermute | solution.py:317
  53.6 3.7 %collective-permute-start.2 = (f32[32,672]{1,0:T(8,128)S(1)}, f32[32,672]{1,0:T(8,128)S(1)}, u32[]{:S(2)}, u32[]{:S(2)}) collective-permute-start(f32[32,672]{1,0:T(8,128)S(1)} %get-tuple-element.22), channel_id=1, source_target_pairs={{0,256},{128,384},{256,0},{384,128},{1,257},{129,385},{257,1},{385... | collective-permute-start | bytes 258056 | tf_op jit(solution)/shard_map/ppermute | solution.py:317
  57.3 2.6 %collective-permute-start.3 = (f32[32,672]{1,0:T(8,128)S(1)}, f32[32,672]{1,0:T(8,128)S(1)}, u32[]{:S(2)}, u32[]{:S(2)}) collective-permute-start(f32[32,672]{1,0:T(8,128)S(1)} %get-tuple-element.23), channel_id=1, source_target_pairs={{0,384},{128,0},{256,128},{384,256},{1,385},{129,1},{257,129},{385... | collective-permute-start | bytes 258056 | tf_op jit(solution)/shard_map/ppermute | solution.py:317
  60.0 1.9 %collective-permute-done.1.refs_1_ = f32[32,672]{1,0:T(8,128)S(1)} collective-permute-done((f32[32,672]{1,0:T(8,128)S(1)}, f32[32,672]{1,0:T(8,128)S(1)}, u32[]{:S(2)}, u32[]{:S(2)}) %collective-permute-start.1) | collective-permute-done | bytes 86048 | tf_op jit(solution)/shard_map/ppermute | solution.py:317
  61.9 1.7 %collective-permute-done.2.refs_2_ = f32[32,672]{1,0:T(8,128)S(1)} collective-permute-done((f32[32,672]{1,0:T(8,128)S(1)}, f32[32,672]{1,0:T(8,128)S(1)}, u32[]{:S(2)}, u32[]{:S(2)}) %collective-permute-start.2) | collective-permute-done | bytes 86048 | tf_op jit(solution)/shard_map/ppermute | solution.py:317
  63.6 0.0 collective-permute-done.3.refs_3_
  63.6 5.6 %all-to-all-done.1 = f32[8,256,128]{2,1,0:T(8,128)S(1)} async-done(((f32[8,256,128]{2,1,0:T(8,128)}), f32[8,256,128]{2,1,0:T(8,128)S(1)}, u32[]{:S(2)}, u32[]{:S(2)}) %all-to-all-start.1) | async-done | bytes 1048608 | tf_op jit(solution)/shard_map/all_to_all | solution.py:238
  69.2 0.1 reduce_sum.18
  69.3 20.2 %all_to_all.26 = f32[32,8,128]{2,1,0:T(8,128)S(1)} all-to-all(f32[32,8,128]{2,1,0:T(8,128)S(1)} %bitcast.6), channel_id=1, replica_groups={{0,4,8,12,16,20,24,28,32,36,40,44,48,52,56,60,64,68,72,76,80,84,88,92,9..., dimensions={0} | all-to-all | bytes 262144 | tf_op jit(solution)/shard_map/all_to_all | solution.py:238
  89.6 12.9 %all_to_all.27 = f32[32,8,128]{2,1,0:T(8,128)S(1)} all-to-all(f32[32,8,128]{2,1,0:T(8,128)S(1)} %broadcast_in_dim.6), channel_id=1, replica_groups={{0,4,8,12,16,20,24,28,32,36,40,44,48,52,56,60,64,68,72,76,80,84,88,92,9..., dimensions={0} | all-to-all | bytes 262144 | tf_op jit(solution)/shard_map/all_to_all | solution.py:238
  102.5 0.1 broadcast_in_dim.15
  102.6 20.2 %all_to_all.28 = f32[8,256,128]{2,1,0:T(8,128)S(1)} all-to-all(f32[8,256,128]{2,1,0:T(8,128)S(1)} %broadcast_in_dim.15), channel_id=1, replica_groups={{0,2,128,130,256,258,384,386},{4,6,132,134,260,262,388,390},{8,10,136,1..., dimensions={0} | all-to-all | bytes 2097152 | tf_op jit(solution)/shard_map/all_to_all | solution.py:238
  122.8 3.1 %collective-permute-start.4 = (f32[2048,128]{1,0:T(8,128)S(1)}, f32[2048,128]{1,0:T(8,128)S(1)}, u32[]{:S(2)}, u32[]{:S(2)}) collective-permute-start(f32[2048,128]{1,0:T(8,128)S(1)} %bitcast.4), channel_id=1, source_target_pairs={{0,1},{1,0},{2,3},{3,2},{4,5},{5,4},{6,7},{7,6},{8,9},{9,8},{10,11... | collective-permute-start | bytes 3145736 | tf_op jit(solution)/shard_map/ppermute | solution.py:333
  125.9 0.9 core_rows.1
  126.8 1.4 %collective-permute-done.4.other_ref = f32[2048,128]{1,0:T(8,128)S(1)} collective-permute-done((f32[2048,128]{1,0:T(8,128)S(1)}, f32[2048,128]{1,0:T(8,128)S(1)}, u32[]{:S(2)}, u32[]{:S(2)}) %collective-permute-start.4) | collective-permute-done | bytes 1048608 | tf_op jit(solution)/shard_map/ppermute | solution.py:333
  128.2 1.8 %mirror.1 = (f32[168,672]{1,0:T(8,128)}, f32[672,672]{1,0:T(8,128)}) custom-call(f32[2048,128]{1,0:T(8,128)S(1)} %bitcast.5, f32[2048,128]{1,0:T(8,128)S(1)} %collective-permute-done.4.other_ref), custom_call_target="tpu_custom_call" | custom-call | tf_op jit(solution)/shard_map/mirror/pallas_call | solution.py:335
  (3 shorter events, 0.1 us)
Async XLA Ops:
  0.6 1.6 %copy-start = (f32[4,168,672]{2,1,0:T(8,128)S(1)}, f32[4,168,672]{2,1,0:T(8,128)}, u32[]{:S(2)}) copy-start(f32[4,168,672]{2,1,0:T(8,128)} %field_ref.1) | copy-start | bytes 5419012
  2.2 0.9 copy-start.1
  33.6 9.9 %collective-permute-start = (f32[2048,128]{1,0:T(8,128)S(1)}, f32[2048,128]{1,0:T(8,128)S(1)}, u32[]{:S(2)}, u32[]{:S(2)}) collective-permute-start(f32[2048,128]{1,0:T(8,128)S(1)} %get-tuple-element.18), channel_id=1, source_target_pairs={{0,1},{1,0},{2,3},{3,2},{4,5},{5,4},{6,7},{7,6},{8,9},{9,8},{10,11... | collective-permute-start | bytes 3145736 | tf_op jit(solution)/shard_map/ppermute | solution.py:302
  44.6 24.6 %all-to-all-start.1 = ((f32[8,256,128]{2,1,0:T(8,128)}), f32[8,256,128]{2,1,0:T(8,128)S(1)}, u32[]{:S(2)}, u32[]{:S(2)}) async-start(f32[8,256,128]{2,1,0:T(8,128)} %bitcast), calls=%async_computation.1 | async-start | bytes 2097152 | tf_op jit(solution)/shard_map/all_to_all | solution.py:238
  51.4 10.5 %collective-permute-start.1 = (f32[32,672]{1,0:T(8,128)S(1)}, f32[32,672]{1,0:T(8,128)S(1)}, u32[]{:S(2)}, u32[]{:S(2)}) collective-permute-start(f32[32,672]{1,0:T(8,128)S(1)} %get-tuple-element.21), channel_id=1, source_target_pairs={{0,128},{128,256},{256,384},{384,0},{1,129},{129,257},{257,385},{3... | collective-permute-start | bytes 258056 | tf_op jit(solution)/shard_map/ppermute | solution.py:317
  53.6 10.0 %collective-permute-start.2 = (f32[32,672]{1,0:T(8,128)S(1)}, f32[32,672]{1,0:T(8,128)S(1)}, u32[]{:S(2)}, u32[]{:S(2)}) collective-permute-start(f32[32,672]{1,0:T(8,128)S(1)} %get-tuple-element.22), channel_id=1, source_target_pairs={{0,256},{128,384},{256,0},{384,128},{1,257},{129,385},{257,1},{385... | collective-permute-start | bytes 258056 | tf_op jit(solution)/shard_map/ppermute | solution.py:317
  57.3 6.3 %collective-permute-start.3 = (f32[32,672]{1,0:T(8,128)S(1)}, f32[32,672]{1,0:T(8,128)S(1)}, u32[]{:S(2)}, u32[]{:S(2)}) collective-permute-start(f32[32,672]{1,0:T(8,128)S(1)} %get-tuple-element.23), channel_id=1, source_target_pairs={{0,384},{128,0},{256,128},{384,256},{1,385},{129,1},{257,129},{385... | collective-permute-start | bytes 258056 | tf_op jit(solution)/shard_map/ppermute | solution.py:317
  122.8 5.4 %collective-permute-start.4 = (f32[2048,128]{1,0:T(8,128)S(1)}, f32[2048,128]{1,0:T(8,128)S(1)}, u32[]{:S(2)}, u32[]{:S(2)}) collective-permute-start(f32[2048,128]{1,0:T(8,128)S(1)} %bitcast.4), channel_id=1, source_target_pairs={{0,1},{1,0},{2,3},{3,2},{4,5},{5,4},{6,7},{7,6},{8,9},{9,8},{10,11... | collective-permute-start | bytes 3145736 | tf_op jit(solution)/shard_map/ppermute | solution.py:333

commit v11 on v10

--- a/solution.py
+++ b/solution.py
@@ -156,6 +156,20 @@
     send_ref[...] = packed[1 - mine]
 
 
+def sum_kernel(keep_ref, came_ref, out_ref, sums, sent):
+    count = sent.shape[0]
+    some = sums.shape[0] // count
+    moves = []
+    for step in range(count):
+        rows = pl.ds(step * some, some)
+        sums[rows, :] = keep_ref[rows, :] + came_ref[rows, :]
+        move = pltpu.make_async_copy(sums.at[rows, :], out_ref.at[rows, :], sent.at[step])
+        move.start()
+        moves.append(move)
+    for move in moves:
+        move.wait()
+
+
 def parts_kernel(core_ref, after_ref, *out_refs):
     owned = out_refs[0].shape[0]
     for step, out_ref in enumerate(out_refs):
@@ -204,12 +218,19 @@
 
 
 def unpack_kernel(
-    layout, scale_one, scale_two, own_ref, other_ref, one_ref, two_ref, packed, whole_one, whole_two, sent
+    layout, orders, scale_one, scale_two, own_ref, other_ref, one_ref, two_ref, packed, came, whole_one, whole_two, sent
 ):
     width = layout.width
     mine = lax.axis_index("c")
     packed[mine] = own_ref[...]
     packed[1 - mine] = other_ref[...]
+    for half in range(2):
+        chunk = layout.rows // len(orders[half])
+        if orders[half] == sorted(orders[half]):
+            continue
+        came[...] = packed[half]
+        for place, source in enumerate(orders[half]):
+            packed[half, pl.ds(place * chunk, chunk), :] = came[pl.ds(source * chunk, chunk), :]
     moves = []
     for block in range(layout.full + 1):
         unpack_rows(layout, packed, 1, block, whole_two, scale_two)
@@ -249,11 +270,19 @@
 def both_groups(sizes):
     shape = tuple(sizes.values())
     index = np.arange(np.prod(shape)).reshape(shape)
-    near = [index[:, b, d, :, 0] for b, d in np.ndindex(shape[1], shape[2])]
-    near += [index[a, :, d, e, 1] for a, d, e in np.ndindex(shape[0], shape[2], shape[3])]
-    far = [index[a, :, :, e, 0] for a, e in np.ndindex(shape[0], shape[3])]
-    far += [index[:, b, :, :, 1] for b in range(shape[1])]
-    return [[group.reshape(-1).tolist() for group in groups] for groups in (near, far)]
+
+    def short(core):
+        return [index[:, b, d, :, core] for b, d in np.ndindex(shape[1], shape[2])]
+
+    def rest(core):
+        return [index[a, :, :, e, core] for a, e in np.ndindex(shape[0], shape[3])]
+
+    near = short(0) + [index[a, :, d, e, 1] for a, d, e in np.ndindex(shape[0], shape[2], shape[3])]
+    far = rest(0) + [index[:, b, :, :, 1] for b in range(shape[1])]
+    groups = [near, far, short(0) + short(1), rest(0) + rest(1)]
+    chunks = np.arange(np.prod(shape[:4])).reshape(shape[0], shape[3], shape[1], shape[2])
+    orders = [sorted(chunks.reshape(-1).tolist()), chunks.transpose(2, 0, 3, 1).reshape(-1).tolist()]
+    return [[group.reshape(-1).tolist() for group in part] for part in groups], orders
 
 
 def local(sizes, tensor, basis):
@@ -262,7 +291,7 @@
     first = rows_here * gx
     rank = basis.shape[1]
     axes = tuple(sizes)
-    near, far = both_groups(sizes)
+    (near, far, back_near, back_far), orders = both_groups(sizes)
     near_count, far_count = len(near[0]), len(far[0])
     slices_all = slices_here * near_count * far_count // gx * sizes["c"]
     layout = Layout(first, 8 * near_count * far_count)
@@ -300,7 +329,15 @@
     )(blocks)
 
     came = lax.ppermute(send, "c", swap)
-    sums = keep + came
+    sums = pl.pallas_call(
+        sum_kernel,
+        out_shape=half_shape,
+        in_specs=[VMEM, VMEM],
+        out_specs=ANY,
+        scratch_shapes=[pltpu.VMEM((layout.rows, LANES), f32), pltpu.SemaphoreType.DMA((8,))],
+        compiler_params=ROOM,
+        name="sum_of_cores",
+    )(keep, came)
     owned = rank // gx
     core_parts = pl.pallas_call(
         parts_kernel,
@@ -328,12 +365,12 @@
         cost_estimate=cost(rank * second, 8 * rank * second),
         name="core_rows",
     )(*came_core)
-    part = exchange(copies(jnp.sum(part, axis=0), far_count), axes, far).reshape(-1, LANES)
-    own = exchange(copies(part, near_count), axes, near).reshape(-1, LANES)
+    part = exchange(copies(jnp.sum(part, axis=0), far_count), axes, back_far).reshape(-1, LANES)
+    own = exchange(copies(part, near_count), axes, back_near).reshape(-1, LANES)
     other = lax.ppermute(own, "c", swap)
 
     gram_one, gram_two = pl.pallas_call(
-        functools.partial(unpack_kernel, layout, 1.0 / (slices_all * second), 1.0 / (slices_all * rank)),
+        functools.partial(unpack_kernel, layout, orders, 1.0 / (slices_all * second), 1.0 / (slices_all * rank)),
         out_shape=(
             jax.ShapeDtypeStruct((rows_here, first), f32),
             jax.ShapeDtypeStruct((second, second), f32),
@@ -342,6 +379,7 @@
         out_specs=(ANY, ANY),
         scratch_shapes=[
             pltpu.VMEM((2, layout.rows, LANES), f32),
+            pltpu.VMEM((layout.rows, LANES), f32),
             pltpu.VMEM((first, first), f32),
             pltpu.VMEM((second, second), f32),
             pltpu.SemaphoreType.DMA((layout.full + 2,)),

time: 130 us -> 131 us (level)
  starting transfers between devices: 26.1 us -> 31.7 us
  blocking collectives: 80.3 us -> 74.7 us
    all_to_all x4, blocking collectives: 80.3 us -> 74.7 us  [exchange(): lax.all_to_all(parts, axes, 0, 0, axis_index_groups=groups, tiled=True)]
    ppermute x1, starting transfers between devices: 3.12 us -> 8.74 us  [local(): other = lax.ppermute(own, 'c', swap)]
    pallas_call x1 -> x2, Pallas kernels: 1.76 us -> 2.92 us  [the longest x1 1.88 us: local(): pl.pallas_call(functools.partial(unpack_kernel, layout, orders, 1.0 / (sl...]
where the time goes in v11:
time: 131 us; the launch traced here: 130 us
  blocking collectives  74.7 us (57%)
  starting transfers between devices  31.7 us (24%)
  waiting for transfers between devices  12.9 us (10%)
  Pallas kernels  7.41 us (6%)
  local copies, waits for them, and re-layouts  2.54 us (2%)
    all_to_all x4, blocking collectives, exchange(): lax.all_to_all(parts, axes, 0, 0, axis_index_groups=groups, tiled=True)  74.7 us
    ppermute x1, starting transfers between devices, local(): other = lax.ppermute(own, 'c', swap)  8.74 us
    ppermute x3, starting transfers between devices, local(): came_core.append(lax.ppermute(core_parts[step], 'x', shift))  8.51 us
    ppermute x1, starting transfers between devices, local(): came = lax.ppermute(send, 'c', swap)  7.62 us
    all_to_all x1, starting transfers between devices, exchange(): lax.all_to_all(parts, axes, 0, 0, axis_index_groups=groups, tiled=True)  6.83 us
    all_to_all x1, waiting for transfers between devices, exchange(): lax.all_to_all(parts, axes, 0, 0, axis_index_groups=groups, tiled=True)  5.59 us
    ppermute x3, waiting for transfers between devices, local(): came_core.append(lax.ppermute(core_parts[step], 'x', shift))  3.65 us
    pallas_call x1, Pallas kernels, local(): pl.pallas_call(functools.partial(gram_kernel, layout), out_shape=(half_sh...  3.42 us
  transfers between devices with their start and end apart: 6, of which 5 were waited for; matrix products, arithmetic and copies ran while one was open for 0% of the time, Pallas kernels for 1%

profile of v11, /device:TPU:1, one launch (start us, length us, event | category | flops | bytes accessed | tf_op | source)
XLA Modules:
  0.0 130.0 jit_solution(15072181956958296700)
XLA Ops:
  0.6 0.0 copy-start
  0.6 1.6 %copy-done = f32[4,168,672]{2,1,0:T(8,128)S(1)} copy-done((f32[4,168,672]{2,1,0:T(8,128)S(1)}, f32[4,168,672]{2,1,0:T(8,128)}, u32[]{:S(2)}) %copy-start) | copy-done | bytes 1806360
  2.2 0.0 copy-start.1
  2.2 0.9 copy-done.1
  3.1 0.2 dense_blocks.1
  3.3 26.9 %all_to_all.25.dense_ref = f32[4,1056,128]{2,1,0:T(8,128)S(1)} all-to-all(f32[4,1056,128]{2,1,0:T(8,128)S(1)} %dense_blocks.1), channel_id=1, replica_groups=mesh['x'=4,'y'=8,'zh'=4,'zl'=2,'c'=2] {'x'}, dimensions={0} | all-to-all | bytes 4325376 | tf_op jit(solution)/shard_map/all_to_all | solution.py:259
  30.2 3.4 %local_grams.1 = (f32[2048,128]{1,0:T(8,128)S(1)}, f32[2048,128]{1,0:T(8,128)S(1)}, f32[128,672]{1,0:T(8,128)S(1)}) custom-call(f32[4,1056,128]{2,1,0:T(8,128)S(1)} %all_to_all.25.dense_ref), custom_call_target="tpu_custom_call" | custom-call | flops 1517322240 | bytes 5419008 | tf_op jit(solution)/shard_map/local_grams/pallas_call | solution.py:312
  33.6 7.6 %collective-permute-start = (f32[2048,128]{1,0:T(8,128)S(1)}, f32[2048,128]{1,0:T(8,128)S(1)}, u32[]{:S(2)}, u32[]{:S(2)}) collective-permute-start(f32[2048,128]{1,0:T(8,128)S(1)} %get-tuple-element.18), channel_id=1, source_target_pairs={{0,1},{1,0},{2,3},{3,2},{4,5},{5,4},{6,7},{7,6},{8,9},{9,8},{10,11... | collective-permute-start | bytes 3145736 | tf_op jit(solution)/shard_map/ppermute | solution.py:331
  41.2 2.3 %collective-permute-done.came_ref.after_ref = f32[2048,128]{1,0:T(8,128)S(1)} collective-permute-done((f32[2048,128]{1,0:T(8,128)S(1)}, f32[2048,128]{1,0:T(8,128)S(1)}, u32[]{:S(2)}, u32[]{:S(2)}) %collective-permute-start) | collective-permute-done | bytes 1048608 | tf_op jit(solution)/shard_map/ppermute | solution.py:331
  43.5 1.0 sum_of_cores.1
  44.6 6.8 %all-to-all-start.1 = ((f32[8,256,128]{2,1,0:T(8,128)}), f32[8,256,128]{2,1,0:T(8,128)S(1)}, u32[]{:S(2)}, u32[]{:S(2)}) async-start(f32[8,256,128]{2,1,0:T(8,128)} %bitcast), calls=%async_computation.1 | async-start | bytes 2097152 | tf_op jit(solution)/shard_map/all_to_all | solution.py:259
  51.4 2.2 %collective-permute-start.1 = (f32[32,672]{1,0:T(8,128)S(1)}, f32[32,672]{1,0:T(8,128)S(1)}, u32[]{:S(2)}, u32[]{:S(2)}) collective-permute-start(f32[32,672]{1,0:T(8,128)S(1)} %get-tuple-element.21), channel_id=1, source_target_pairs={{0,128},{128,256},{256,384},{384,0},{1,129},{129,257},{257,385},{3... | collective-permute-start | bytes 258056 | tf_op jit(solution)/shard_map/ppermute | solution.py:354
  53.6 3.7 %collective-permute-start.2 = (f32[32,672]{1,0:T(8,128)S(1)}, f32[32,672]{1,0:T(8,128)S(1)}, u32[]{:S(2)}, u32[]{:S(2)}) collective-permute-start(f32[32,672]{1,0:T(8,128)S(1)} %get-tuple-element.22), channel_id=1, source_target_pairs={{0,256},{128,384},{256,0},{384,128},{1,257},{129,385},{257,1},{385... | collective-permute-start | bytes 258056 | tf_op jit(solution)/shard_map/ppermute | solution.py:354
  57.3 2.6 %collective-permute-start.3 = (f32[32,672]{1,0:T(8,128)S(1)}, f32[32,672]{1,0:T(8,128)S(1)}, u32[]{:S(2)}, u32[]{:S(2)}) collective-permute-start(f32[32,672]{1,0:T(8,128)S(1)} %get-tuple-element.23), channel_id=1, source_target_pairs={{0,384},{128,0},{256,128},{384,256},{1,385},{129,1},{257,129},{385... | collective-permute-start | bytes 258056 | tf_op jit(solution)/shard_map/ppermute | solution.py:354
  60.0 1.9 %collective-permute-done.1.refs_1_ = f32[32,672]{1,0:T(8,128)S(1)} collective-permute-done((f32[32,672]{1,0:T(8,128)S(1)}, f32[32,672]{1,0:T(8,128)S(1)}, u32[]{:S(2)}, u32[]{:S(2)}) %collective-permute-start.1) | collective-permute-done | bytes 86048 | tf_op jit(solution)/shard_map/ppermute | solution.py:354
  61.9 1.7 %collective-permute-done.2.refs_2_ = f32[32,672]{1,0:T(8,128)S(1)} collective-permute-done((f32[32,672]{1,0:T(8,128)S(1)}, f32[32,672]{1,0:T(8,128)S(1)}, u32[]{:S(2)}, u32[]{:S(2)}) %collective-permute-start.2) | collective-permute-done | bytes 86048 | tf_op jit(solution)/shard_map/ppermute | solution.py:354
  63.6 0.0 collective-permute-done.3.refs_3_
  63.6 5.6 %all-to-all-done.1 = f32[8,256,128]{2,1,0:T(8,128)S(1)} async-done(((f32[8,256,128]{2,1,0:T(8,128)}), f32[8,256,128]{2,1,0:T(8,128)S(1)}, u32[]{:S(2)}, u32[]{:S(2)}) %all-to-all-start.1) | async-done | bytes 1048608 | tf_op jit(solution)/shard_map/all_to_all | solution.py:259
  69.2 0.1 reduce_sum.18
  69.3 20.2 %all_to_all.26 = f32[32,8,128]{2,1,0:T(8,128)S(1)} all-to-all(f32[32,8,128]{2,1,0:T(8,128)S(1)} %bitcast.6), channel_id=1, replica_groups={{0,4,8,12,16,20,24,28,32,36,40,44,48,52,56,60,64,68,72,76,80,84,88,92,9..., dimensions={0} | all-to-all | bytes 262144 | tf_op jit(solution)/shard_map/all_to_all | solution.py:259
  89.6 14.5 %all_to_all.27 = f32[32,8,128]{2,1,0:T(8,128)S(1)} all-to-all(f32[32,8,128]{2,1,0:T(8,128)S(1)} %broadcast_in_dim.6), channel_id=1, replica_groups={{0,4,8,12,16,20,24,28,32,36,40,44,48,52,56,60,64,68,72,76,80,84,88,92,9..., dimensions={0} | all-to-all | bytes 262144 | tf_op jit(solution)/shard_map/all_to_all | solution.py:259
  104.1 0.1 broadcast_in_dim.15
  104.2 13.0 %all_to_all.28 = f32[8,256,128]{2,1,0:T(8,128)S(1)} all-to-all(f32[8,256,128]{2,1,0:T(8,128)S(1)} %broadcast_in_dim.15), channel_id=1, replica_groups={{0,2,128,130,256,258,384,386},{4,6,132,134,260,262,388,390},{8,10,136,1..., dimensions={0} | all-to-all | bytes 2097152 | tf_op jit(solution)/shard_map/all_to_all | solution.py:259
  117.1 8.7 %collective-permute-start.4 = (f32[2048,128]{1,0:T(8,128)S(1)}, f32[2048,128]{1,0:T(8,128)S(1)}, u32[]{:S(2)}, u32[]{:S(2)}) collective-permute-start(f32[2048,128]{1,0:T(8,128)S(1)} %bitcast.4), channel_id=1, source_target_pairs={{0,1},{1,0},{2,3},{3,2},{4,5},{5,4},{6,7},{7,6},{8,9},{9,8},{10,11... | collective-permute-start | bytes 3145736 | tf_op jit(solution)/shard_map/ppermute | solution.py:370
  125.9 0.9 core_rows.1
  126.7 1.4 %collective-permute-done.4.other_ref = f32[2048,128]{1,0:T(8,128)S(1)} collective-permute-done((f32[2048,128]{1,0:T(8,128)S(1)}, f32[2048,128]{1,0:T(8,128)S(1)}, u32[]{:S(2)}, u32[]{:S(2)}) %collective-permute-start.4) | collective-permute-done | bytes 1048608 | tf_op jit(solution)/shard_map/ppermute | solution.py:370
  128.1 1.9 %mirror.1 = (f32[168,672]{1,0:T(8,128)}, f32[672,672]{1,0:T(8,128)}) custom-call(f32[2048,128]{1,0:T(8,128)S(1)} %bitcast.5, f32[2048,128]{1,0:T(8,128)S(1)} %collective-permute-done.4.other_ref), custom_call_target="tpu_custom_call" | custom-call | tf_op jit(solution)/shard_map/mirror/pallas_call | solution.py:372
  (3 shorter events, 0.1 us)
Async XLA Ops:
  0.6 1.6 %copy-start = (f32[4,168,672]{2,1,0:T(8,128)S(1)}, f32[4,168,672]{2,1,0:T(8,128)}, u32[]{:S(2)}) copy-start(f32[4,168,672]{2,1,0:T(8,128)} %field_ref.1) | copy-start | bytes 5419012
  2.2 0.9 copy-start.1
  33.6 9.9 %collective-permute-start = (f32[2048,128]{1,0:T(8,128)S(1)}, f32[2048,128]{1,0:T(8,128)S(1)}, u32[]{:S(2)}, u32[]{:S(2)}) collective-permute-start(f32[2048,128]{1,0:T(8,128)S(1)} %get-tuple-element.18), channel_id=1, source_target_pairs={{0,1},{1,0},{2,3},{3,2},{4,5},{5,4},{6,7},{7,6},{8,9},{9,8},{10,11... | collective-permute-start | bytes 3145736 | tf_op jit(solution)/shard_map/ppermute | solution.py:331
  44.6 24.6 %all-to-all-start.1 = ((f32[8,256,128]{2,1,0:T(8,128)}), f32[8,256,128]{2,1,0:T(8,128)S(1)}, u32[]{:S(2)}, u32[]{:S(2)}) async-start(f32[8,256,128]{2,1,0:T(8,128)} %bitcast), calls=%async_computation.1 | async-start | bytes 2097152 | tf_op jit(solution)/shard_map/all_to_all | solution.py:259
  51.4 10.5 %collective-permute-start.1 = (f32[32,672]{1,0:T(8,128)S(1)}, f32[32,672]{1,0:T(8,128)S(1)}, u32[]{:S(2)}, u32[]{:S(2)}) collective-permute-start(f32[32,672]{1,0:T(8,128)S(1)} %get-tuple-element.21), channel_id=1, source_target_pairs={{0,128},{128,256},{256,384},{384,0},{1,129},{129,257},{257,385},{3... | collective-permute-start | bytes 258056 | tf_op jit(solution)/shard_map/ppermute | solution.py:354
  53.6 10.0 %collective-permute-start.2 = (f32[32,672]{1,0:T(8,128)S(1)}, f32[32,672]{1,0:T(8,128)S(1)}, u32[]{:S(2)}, u32[]{:S(2)}) collective-permute-start(f32[32,672]{1,0:T(8,128)S(1)} %get-tuple-element.22), channel_id=1, source_target_pairs={{0,256},{128,384},{256,0},{384,128},{1,257},{129,385},{257,1},{385... | collective-permute-start | bytes 258056 | tf_op jit(solution)/shard_map/ppermute | solution.py:354
  57.3 6.3 %collective-permute-start.3 = (f32[32,672]{1,0:T(8,128)S(1)}, f32[32,672]{1,0:T(8,128)S(1)}, u32[]{:S(2)}, u32[]{:S(2)}) collective-permute-start(f32[32,672]{1,0:T(8,128)S(1)} %get-tuple-element.23), channel_id=1, source_target_pairs={{0,384},{128,0},{256,128},{384,256},{1,385},{129,1},{257,129},{385... | collective-permute-start | bytes 258056 | tf_op jit(solution)/shard_map/ppermute | solution.py:354
  117.1 11.0 %collective-permute-start.4 = (f32[2048,128]{1,0:T(8,128)S(1)}, f32[2048,128]{1,0:T(8,128)S(1)}, u32[]{:S(2)}, u32[]{:S(2)}) collective-permute-start(f32[2048,128]{1,0:T(8,128)S(1)} %bitcast.4), channel_id=1, source_target_pairs={{0,1},{1,0},{2,3},{3,2},{4,5},{5,4},{6,7},{7,6},{8,9},{9,8},{10,11... | collective-permute-start | bytes 3145736 | tf_op jit(solution)/shard_map/ppermute | solution.py:370

commit v12 on v11

--- a/solution.py
+++ b/solution.py
@@ -170,10 +170,10 @@
         move.wait()
 
 
-def parts_kernel(core_ref, after_ref, *out_refs):
+def parts_kernel(steps, owners, core_ref, after_ref, *out_refs):
     owned = out_refs[0].shape[0]
-    for step, out_ref in enumerate(out_refs):
-        owner = lax.rem(lax.axis_index("x") + step, len(out_refs))
+    for step, out_ref in zip(steps, out_refs):
+        owner = lax.rem(lax.axis_index("x") + step, owners)
         out_ref[...] = core_ref[pl.ds(pl.multiple_of(owner * owned, 8), owned), :]
 
 
@@ -339,22 +339,31 @@
         name="sum_of_cores",
     )(keep, came)
     owned = rank // gx
-    core_parts = pl.pallas_call(
-        parts_kernel,
-        out_shape=[jax.ShapeDtypeStruct((owned, second), f32)] * gx,
-        in_specs=[VMEM, ANY],
-        out_specs=[VMEM] * gx,
-        compiler_params=ROOM,
-        cost_estimate=cost(rank * second, 8 * rank * second),
-        name="core_parts",
-    )(core, came)
-    came_core = [core_parts[0]]
-    for step in range(1, gx):
-        shift = [(i, (i + step) % gx) for i in range(gx)]
-        came_core.append(lax.ppermute(core_parts[step], "x", shift))
+    def parts(steps, after):
+        return pl.pallas_call(
+            functools.partial(parts_kernel, steps, gx),
+            out_shape=[jax.ShapeDtypeStruct((owned, second), f32)] * len(steps),
+            in_specs=[VMEM, ANY],
+            out_specs=[VMEM] * len(steps),
+            compiler_params=ROOM,
+            cost_estimate=cost(rank * second, 8 * rank * second),
+            name="core_parts",
+        )(core, after)
+
+    def along_x(block, step):
+        return lax.ppermute(block, "x", [(i, (i + step) % gx) for i in range(gx)])
+
+    early = [step for step in range(gx) if 2 * step != gx]
+    late = gx // 2
+    blocks_early = parts(early, came)
+    came_core = [along_x(block, step) if step else block for step, block in zip(early, blocks_early)]
     part = exchange(sums.reshape(near_count, -1, LANES), axes, near)
     part, *came_core = lax.optimization_barrier((part, *came_core))
-    part = exchange(jnp.sum(part, axis=0).reshape(far_count, -1, LANES), axes, far)
+    part = jnp.sum(part, axis=0)
+    came_late = along_x(parts([late], part)[0], late)
+    part = exchange(part.reshape(far_count, -1, LANES), axes, far)
+    part, came_late = lax.optimization_barrier((part, came_late))
+    came_core = came_core[:late] + [came_late] + came_core[late:]
     core_out = pl.pallas_call(
         rows_kernel,
         out_shape=jax.ShapeDtypeStruct((owned, gx, second), f32),

time: 131 us -> 134 us (1.023)
  blocking collectives: 74.7 us -> 60.4 us
  starting transfers between devices: 31.7 us -> 42.2 us
  waiting for transfers between devices: 12.9 us -> 19.5 us
    all_to_all x4 -> x3, blocking collectives: 74.7 us -> 60.4 us  [exchange(): lax.all_to_all(parts, axes, 0, 0, axis_index_groups=groups, tiled=True)]
    all_to_all x1 -> x2, starting transfers between devices: 6.83 us -> 17.9 us  [exchange(): lax.all_to_all(parts, axes, 0, 0, axis_index_groups=groups, tiled=True)]
    all_to_all x1 -> x2, waiting for transfers between devices: 5.59 us -> 9.42 us  [exchange(): lax.all_to_all(parts, axes, 0, 0, axis_index_groups=groups, tiled=True)]
    ppermute x1, starting transfers between devices: 8.74 us -> 5.56 us  [local(): other = lax.ppermute(own, 'c', swap)]
    ppermute x3, waiting for transfers between devices: 3.65 us -> 6.37 us  [along_x(): return lax.ppermute(block, 'x', [(i, (i + step) % gx) for i in range(gx)])]
    ppermute x3, starting transfers between devices: 8.51 us -> 11.1 us  [along_x(): return lax.ppermute(block, 'x', [(i, (i + step) % gx) for i in range(gx)])]
  transfers between devices with their start and end apart: 6 -> 7, of which waited for: 5 -> 6; matrix products, arithmetic and copies ran while one was open for 0% -> 0% of each run, Pallas kernels for 1% -> 1%
where the time goes in v12:
time: 134 us; the launch traced here: 133 us
  blocking collectives  60.4 us (45%)
  starting transfers between devices  42.2 us (31%)
  waiting for transfers between devices  19.5 us (15%)
  Pallas kernels  7.43 us (6%)
  local copies, waits for them, and re-layouts  2.54 us (2%)
    all_to_all x3, blocking collectives, exchange(): lax.all_to_all(parts, axes, 0, 0, axis_index_groups=groups, tiled=True)  60.4 us
    all_to_all x2, starting transfers between devices, exchange(): lax.all_to_all(parts, axes, 0, 0, axis_index_groups=groups, tiled=True)  17.9 us
    ppermute x3, starting transfers between devices, along_x(): return lax.ppermute(block, 'x', [(i, (i + step) % gx) for i in range(gx)])  11.1 us
    all_to_all x2, waiting for transfers between devices, exchange(): lax.all_to_all(parts, axes, 0, 0, axis_index_groups=groups, tiled=True)  9.42 us
    ppermute x1, starting transfers between devices, local(): came = lax.ppermute(send, 'c', swap)  7.62 us
    ppermute x3, waiting for transfers between devices, along_x(): return lax.ppermute(block, 'x', [(i, (i + step) % gx) for i in range(gx)])  6.37 us
    ppermute x1, starting transfers between devices, local(): other = lax.ppermute(own, 'c', swap)  5.56 us
    pallas_call x1, Pallas kernels, local(): pl.pallas_call(functools.partial(gram_kernel, layout), out_shape=(half_sh...  3.42 us
  transfers between devices with their start and end apart: 7, of which 6 were waited for; matrix products, arithmetic and copies ran while one was open for 0% of the time, Pallas kernels for 1%

profile of v12, /device:TPU:1, one launch (start us, length us, event | category | flops | bytes accessed | tf_op | source)
XLA Modules:
  0.0 133.5 jit_solution(11170588145740585732)
XLA Ops:
  0.6 0.0 copy-start
  0.6 1.6 %copy-done = f32[4,168,672]{2,1,0:T(8,128)S(1)} copy-done((f32[4,168,672]{2,1,0:T(8,128)S(1)}, f32[4,168,672]{2,1,0:T(8,128)}, u32[]{:S(2)}) %copy-start) | copy-done | bytes 1806360
  2.2 0.0 copy-start.1
  2.2 0.9 copy-done.1
  3.1 0.2 dense_blocks.1
  3.3 26.9 %all_to_all.25.dense_ref = f32[4,1056,128]{2,1,0:T(8,128)S(1)} all-to-all(f32[4,1056,128]{2,1,0:T(8,128)S(1)} %dense_blocks.1), channel_id=1, replica_groups=mesh['x'=4,'y'=8,'zh'=4,'zl'=2,'c'=2] {'x'}, dimensions={0} | all-to-all | bytes 4325376 | tf_op jit(solution)/shard_map/all_to_all | solution.py:259
  30.2 3.4 %local_grams.1 = (f32[2048,128]{1,0:T(8,128)S(1)}, f32[2048,128]{1,0:T(8,128)S(1)}, f32[128,672]{1,0:T(8,128)S(1)}) custom-call(f32[4,1056,128]{2,1,0:T(8,128)S(1)} %all_to_all.25.dense_ref), custom_call_target="tpu_custom_call" | custom-call | flops 1517322240 | bytes 5419008 | tf_op jit(solution)/shard_map/local_grams/pallas_call | solution.py:312
  33.6 7.6 %collective-permute-start = (f32[2048,128]{1,0:T(8,128)S(1)}, f32[2048,128]{1,0:T(8,128)S(1)}, u32[]{:S(2)}, u32[]{:S(2)}) collective-permute-start(f32[2048,128]{1,0:T(8,128)S(1)} %get-tuple-element.18), channel_id=1, source_target_pairs={{0,1},{1,0},{2,3},{3,2},{4,5},{5,4},{6,7},{7,6},{8,9},{9,8},{10,11... | collective-permute-start | bytes 3145736 | tf_op jit(solution)/shard_map/ppermute | solution.py:331
  41.2 2.3 %collective-permute-done.came_ref.after_ref = f32[2048,128]{1,0:T(8,128)S(1)} collective-permute-done((f32[2048,128]{1,0:T(8,128)S(1)}, f32[2048,128]{1,0:T(8,128)S(1)}, u32[]{:S(2)}, u32[]{:S(2)}) %collective-permute-start) | collective-permute-done | bytes 1048608 | tf_op jit(solution)/shard_map/ppermute | solution.py:331
  43.5 1.0 sum_of_cores.1
  44.6 6.8 %all-to-all-start.1 = ((f32[8,256,128]{2,1,0:T(8,128)}), f32[8,256,128]{2,1,0:T(8,128)S(1)}, u32[]{:S(2)}, u32[]{:S(2)}) async-start(f32[8,256,128]{2,1,0:T(8,128)} %bitcast), calls=%async_computation.1 | async-start | bytes 2097152 | tf_op jit(solution)/shard_map/all_to_all | solution.py:259
  51.4 2.2 %collective-permute-start.1 = (f32[32,672]{1,0:T(8,128)S(1)}, f32[32,672]{1,0:T(8,128)S(1)}, u32[]{:S(2)}, u32[]{:S(2)}) collective-permute-start(f32[32,672]{1,0:T(8,128)S(1)} %get-tuple-element.21), channel_id=1, source_target_pairs={{0,128},{128,256},{256,384},{384,0},{1,129},{129,257},{257,385},{3... | collective-permute-start | bytes 258056 | tf_op jit(solution)/shard_map/ppermute | solution.py:354
  53.6 4.3 %collective-permute-start.2 = (f32[32,672]{1,0:T(8,128)S(1)}, f32[32,672]{1,0:T(8,128)S(1)}, u32[]{:S(2)}, u32[]{:S(2)}) collective-permute-start(f32[32,672]{1,0:T(8,128)S(1)} %get-tuple-element.22), channel_id=1, source_target_pairs={{0,384},{128,0},{256,128},{384,256},{1,385},{129,1},{257,129},{385... | collective-permute-start | bytes 258056 | tf_op jit(solution)/shard_map/ppermute | solution.py:354
  57.9 3.8 %collective-permute-done.1.refs_1_ = f32[32,672]{1,0:T(8,128)S(1)} collective-permute-done((f32[32,672]{1,0:T(8,128)S(1)}, f32[32,672]{1,0:T(8,128)S(1)}, u32[]{:S(2)}, u32[]{:S(2)}) %collective-permute-start.1) | collective-permute-done | bytes 86048 | tf_op jit(solution)/shard_map/ppermute | solution.py:354
  61.7 0.0 collective-permute-done.2.refs_3_
  61.7 7.5 %all-to-all-done.1 = f32[8,256,128]{2,1,0:T(8,128)S(1)} async-done(((f32[8,256,128]{2,1,0:T(8,128)}), f32[8,256,128]{2,1,0:T(8,128)S(1)}, u32[]{:S(2)}, u32[]{:S(2)}) %all-to-all-start.1) | async-done | bytes 1048608 | tf_op jit(solution)/shard_map/all_to_all | solution.py:259
  69.2 0.7 reduce_sum.18.after_ref
  69.9 11.0 %all-to-all-start.2 = ((f32[32,8,128]{2,1,0:T(8,128)}), f32[32,8,128]{2,1,0:T(8,128)S(1)}, u32[]{:S(2)}, u32[]{:S(2)}) async-start(f32[32,8,128]{2,1,0:T(8,128)} %bitcast.1), calls=%async_computation.2 | async-start | bytes 262144 | tf_op jit(solution)/shard_map/all_to_all | solution.py:259
  81.0 4.7 %collective-permute-start.3 = (f32[32,672]{1,0:T(8,128)S(1)}, f32[32,672]{1,0:T(8,128)S(1)}, u32[]{:S(2)}, u32[]{:S(2)}) collective-permute-start(f32[32,672]{1,0:T(8,128)S(1)} %core_parts.3), channel_id=1, source_target_pairs={{0,256},{128,384},{256,0},{384,128},{1,257},{129,385},{257,1},{385... | collective-permute-start | bytes 258056 | tf_op jit(solution)/shard_map/ppermute | solution.py:354
  85.6 2.6 %collective-permute-done.3.refs_2_ = f32[32,672]{1,0:T(8,128)S(1)} collective-permute-done((f32[32,672]{1,0:T(8,128)S(1)}, f32[32,672]{1,0:T(8,128)S(1)}, u32[]{:S(2)}, u32[]{:S(2)}) %collective-permute-start.3) | collective-permute-done | bytes 86048 | tf_op jit(solution)/shard_map/ppermute | solution.py:354
  88.2 1.9 %all-to-all-done.2 = f32[32,8,128]{2,1,0:T(8,128)S(1)} async-done(((f32[32,8,128]{2,1,0:T(8,128)}), f32[32,8,128]{2,1,0:T(8,128)S(1)}, u32[]{:S(2)}, u32[]{:S(2)}) %all-to-all-start.2) | async-done | bytes 131104 | tf_op jit(solution)/shard_map/all_to_all | solution.py:259
  90.2 15.9 %all_to_all.26 = f32[32,8,128]{2,1,0:T(8,128)S(1)} all-to-all(f32[32,8,128]{2,1,0:T(8,128)S(1)} %broadcast_in_dim.6), channel_id=1, replica_groups={{0,4,8,12,16,20,24,28,32,36,40,44,48,52,56,60,64,68,72,76,80,84,88,92,9..., dimensions={0} | all-to-all | bytes 262144 | tf_op jit(solution)/shard_map/all_to_all | solution.py:259
  106.1 0.1 broadcast_in_dim.15
  106.1 17.6 %all_to_all.27 = f32[8,256,128]{2,1,0:T(8,128)S(1)} all-to-all(f32[8,256,128]{2,1,0:T(8,128)S(1)} %broadcast_in_dim.15), channel_id=1, replica_groups={{0,2,128,130,256,258,384,386},{4,6,132,134,260,262,388,390},{8,10,136,1..., dimensions={0} | all-to-all | bytes 2097152 | tf_op jit(solution)/shard_map/all_to_all | solution.py:259
  123.8 5.6 %collective-permute-start.4 = (f32[2048,128]{1,0:T(8,128)S(1)}, f32[2048,128]{1,0:T(8,128)S(1)}, u32[]{:S(2)}, u32[]{:S(2)}) collective-permute-start(f32[2048,128]{1,0:T(8,128)S(1)} %bitcast.4), channel_id=1, source_target_pairs={{0,1},{1,0},{2,3},{3,2},{4,5},{5,4},{6,7},{7,6},{8,9},{9,8},{10,11... | collective-permute-start | bytes 3145736 | tf_op jit(solution)/shard_map/ppermute | solution.py:379
  129.3 0.9 core_rows.1
  130.2 1.4 %collective-permute-done.4.other_ref = f32[2048,128]{1,0:T(8,128)S(1)} collective-permute-done((f32[2048,128]{1,0:T(8,128)S(1)}, f32[2048,128]{1,0:T(8,128)S(1)}, u32[]{:S(2)}, u32[]{:S(2)}) %collective-permute-start.4) | collective-permute-done | bytes 1048608 | tf_op jit(solution)/shard_map/ppermute | solution.py:379
  131.6 1.9 %mirror.1 = (f32[168,672]{1,0:T(8,128)}, f32[672,672]{1,0:T(8,128)}) custom-call(f32[2048,128]{1,0:T(8,128)S(1)} %bitcast.5, f32[2048,128]{1,0:T(8,128)S(1)} %collective-permute-done.4.other_ref), custom_call_target="tpu_custom_call" | custom-call | tf_op jit(solution)/shard_map/mirror/pallas_call | solution.py:381
  (4 shorter events, 0.1 us)
Async XLA Ops:
  0.6 1.6 %copy-start = (f32[4,168,672]{2,1,0:T(8,128)S(1)}, f32[4,168,672]{2,1,0:T(8,128)}, u32[]{:S(2)}) copy-start(f32[4,168,672]{2,1,0:T(8,128)} %field_ref.1) | copy-start | bytes 5419012
  2.2 0.9 copy-start.1
  33.6 9.9 %collective-permute-start = (f32[2048,128]{1,0:T(8,128)S(1)}, f32[2048,128]{1,0:T(8,128)S(1)}, u32[]{:S(2)}, u32[]{:S(2)}) collective-permute-start(f32[2048,128]{1,0:T(8,128)S(1)} %get-tuple-element.18), channel_id=1, source_target_pairs={{0,1},{1,0},{2,3},{3,2},{4,5},{5,4},{6,7},{7,6},{8,9},{9,8},{10,11... | collective-permute-start | bytes 3145736 | tf_op jit(solution)/shard_map/ppermute | solution.py:331
  44.6 24.6 %all-to-all-start.1 = ((f32[8,256,128]{2,1,0:T(8,128)}), f32[8,256,128]{2,1,0:T(8,128)S(1)}, u32[]{:S(2)}, u32[]{:S(2)}) async-start(f32[8,256,128]{2,1,0:T(8,128)} %bitcast), calls=%async_computation.1 | async-start | bytes 2097152 | tf_op jit(solution)/shard_map/all_to_all | solution.py:259
  51.4 10.3 %collective-permute-start.1 = (f32[32,672]{1,0:T(8,128)S(1)}, f32[32,672]{1,0:T(8,128)S(1)}, u32[]{:S(2)}, u32[]{:S(2)}) collective-permute-start(f32[32,672]{1,0:T(8,128)S(1)} %get-tuple-element.21), channel_id=1, source_target_pairs={{0,128},{128,256},{256,384},{384,0},{1,129},{129,257},{257,385},{3... | collective-permute-start | bytes 258056 | tf_op jit(solution)/shard_map/ppermute | solution.py:354
  53.6 8.1 %collective-permute-start.2 = (f32[32,672]{1,0:T(8,128)S(1)}, f32[32,672]{1,0:T(8,128)S(1)}, u32[]{:S(2)}, u32[]{:S(2)}) collective-permute-start(f32[32,672]{1,0:T(8,128)S(1)} %get-tuple-element.22), channel_id=1, source_target_pairs={{0,384},{128,0},{256,128},{384,256},{1,385},{129,1},{257,129},{385... | collective-permute-start | bytes 258056 | tf_op jit(solution)/shard_map/ppermute | solution.py:354
  69.9 20.2 %all-to-all-start.2 = ((f32[32,8,128]{2,1,0:T(8,128)}), f32[32,8,128]{2,1,0:T(8,128)S(1)}, u32[]{:S(2)}, u32[]{:S(2)}) async-start(f32[32,8,128]{2,1,0:T(8,128)} %bitcast.1), calls=%async_computation.2 | async-start | bytes 262144 | tf_op jit(solution)/shard_map/all_to_all | solution.py:259
  81.0 7.2 %collective-permute-start.3 = (f32[32,672]{1,0:T(8,128)S(1)}, f32[32,672]{1,0:T(8,128)S(1)}, u32[]{:S(2)}, u32[]{:S(2)}) collective-permute-start(f32[32,672]{1,0:T(8,128)S(1)} %core_parts.3), channel_id=1, source_target_pairs={{0,256},{128,384},{256,0},{384,128},{1,257},{129,385},{257,1},{385... | collective-permute-start | bytes 258056 | tf_op jit(solution)/shard_map/ppermute | solution.py:354
  123.8 7.8 %collective-permute-start.4 = (f32[2048,128]{1,0:T(8,128)S(1)}, f32[2048,128]{1,0:T(8,128)S(1)}, u32[]{:S(2)}, u32[]{:S(2)}) collective-permute-start(f32[2048,128]{1,0:T(8,128)S(1)} %bitcast.4), channel_id=1, source_target_pairs={{0,1},{1,0},{2,3},{3,2},{4,5},{5,4},{6,7},{7,6},{8,9},{9,8},{10,11... | collective-permute-start | bytes 3145736 | tf_op jit(solution)/shard_map/ppermute | solution.py:379

commit v13 on v11

--- a/solution.py
+++ b/solution.py
@@ -277,11 +277,13 @@
     def rest(core):
         return [index[a, :, :, e, core] for a, e in np.ndindex(shape[0], shape[3])]
 
-    near = short(0) + [index[a, :, d, e, 1] for a, d, e in np.ndindex(shape[0], shape[2], shape[3])]
-    far = rest(0) + [index[:, b, :, :, 1] for b in range(shape[1])]
+    near = [index[a, b, :, :, 0] for a, b in np.ndindex(shape[0], shape[1])]
+    near += [index[a, :, d, e, 1] for a, d, e in np.ndindex(shape[0], shape[2], shape[3])]
+    far = [index[:, :, d, e, 0] for d, e in np.ndindex(shape[2], shape[3])]
+    far += [index[:, b, :, :, 1] for b in range(shape[1])]
     groups = [near, far, short(0) + short(1), rest(0) + rest(1)]
     chunks = np.arange(np.prod(shape[:4])).reshape(shape[0], shape[3], shape[1], shape[2])
-    orders = [sorted(chunks.reshape(-1).tolist()), chunks.transpose(2, 0, 3, 1).reshape(-1).tolist()]
+    orders = [chunks.transpose(order).reshape(-1).tolist() for order in ((3, 1, 0, 2), (2, 0, 3, 1))]
     return [[group.reshape(-1).tolist() for group in part] for part in groups], orders
 
 

time: 131 us -> 131 us (level)
  blocking collectives: 74.7 us -> 77 us
  starting transfers between devices: 31.7 us -> 29.5 us
    all_to_all x4, blocking collectives: 74.7 us -> 77 us  [exchange(): lax.all_to_all(parts, axes, 0, 0, axis_index_groups=groups, tiled=True)]
    ppermute x1, starting transfers between devices: 8.74 us -> 6.53 us  [local(): other = lax.ppermute(own, 'c', swap)]
where the time goes in v13:
time: 131 us; the launch traced here: 130 us
  blocking collectives  77 us (59%)
  starting transfers between devices  29.5 us (23%)
  waiting for transfers between devices  12.9 us (10%)
  Pallas kernels  7.5 us (6%)
  local copies, waits for them, and re-layouts  2.54 us (2%)
    all_to_all x4, blocking collectives, exchange(): lax.all_to_all(parts, axes, 0, 0, axis_index_groups=groups, tiled=True)  77 us
    ppermute x3, starting transfers between devices, local(): came_core.append(lax.ppermute(core_parts[step], 'x', shift))  8.51 us
    ppermute x1, starting transfers between devices, local(): came = lax.ppermute(send, 'c', swap)  7.62 us
    all_to_all x1, starting transfers between devices, exchange(): lax.all_to_all(parts, axes, 0, 0, axis_index_groups=groups, tiled=True)  6.83 us
    ppermute x1, starting transfers between devices, local(): other = lax.ppermute(own, 'c', swap)  6.53 us
    all_to_all x1, waiting for transfers between devices, exchange(): lax.all_to_all(parts, axes, 0, 0, axis_index_groups=groups, tiled=True)  6.22 us
    pallas_call x1, Pallas kernels, local(): pl.pallas_call(functools.partial(gram_kernel, layout), out_shape=(half_sh...  3.42 us
    ppermute x3, waiting for transfers between devices, local(): came_core.append(lax.ppermute(core_parts[step], 'x', shift))  3.02 us
  transfers between devices with their start and end apart: 6, of which 5 were waited for; matrix products, arithmetic and copies ran while one was open for 0% of the time, Pallas kernels for 1%

profile of v13, /device:TPU:1, one launch (start us, length us, event | category | flops | bytes accessed | tf_op | source)
XLA Modules:
  0.0 130.3 jit_solution(4062046031560606718)
XLA Ops:
  0.6 0.0 copy-start
  0.6 1.6 %copy-done = f32[4,168,672]{2,1,0:T(8,128)S(1)} copy-done((f32[4,168,672]{2,1,0:T(8,128)S(1)}, f32[4,168,672]{2,1,0:T(8,128)}, u32[]{:S(2)}) %copy-start) | copy-done | bytes 1806360
  2.2 0.0 copy-start.1
  2.2 0.9 copy-done.1
  3.1 0.2 dense_blocks.1
  3.3 26.9 %all_to_all.25.dense_ref = f32[4,1056,128]{2,1,0:T(8,128)S(1)} all-to-all(f32[4,1056,128]{2,1,0:T(8,128)S(1)} %dense_blocks.1), channel_id=1, replica_groups=mesh['x'=4,'y'=8,'zh'=4,'zl'=2,'c'=2] {'x'}, dimensions={0} | all-to-all | bytes 4325376 | tf_op jit(solution)/shard_map/all_to_all | solution.py:259
  30.2 3.4 %local_grams.1 = (f32[2048,128]{1,0:T(8,128)S(1)}, f32[2048,128]{1,0:T(8,128)S(1)}, f32[128,672]{1,0:T(8,128)S(1)}) custom-call(f32[4,1056,128]{2,1,0:T(8,128)S(1)} %all_to_all.25.dense_ref), custom_call_target="tpu_custom_call" | custom-call | flops 1517322240 | bytes 5419008 | tf_op jit(solution)/shard_map/local_grams/pallas_call | solution.py:314
  33.6 7.6 %collective-permute-start = (f32[2048,128]{1,0:T(8,128)S(1)}, f32[2048,128]{1,0:T(8,128)S(1)}, u32[]{:S(2)}, u32[]{:S(2)}) collective-permute-start(f32[2048,128]{1,0:T(8,128)S(1)} %get-tuple-element.18), channel_id=1, source_target_pairs={{0,1},{1,0},{2,3},{3,2},{4,5},{5,4},{6,7},{7,6},{8,9},{9,8},{10,11... | collective-permute-start | bytes 3145736 | tf_op jit(solution)/shard_map/ppermute | solution.py:333
  41.2 2.3 %collective-permute-done.came_ref.after_ref = f32[2048,128]{1,0:T(8,128)S(1)} collective-permute-done((f32[2048,128]{1,0:T(8,128)S(1)}, f32[2048,128]{1,0:T(8,128)S(1)}, u32[]{:S(2)}, u32[]{:S(2)}) %collective-permute-start) | collective-permute-done | bytes 1048608 | tf_op jit(solution)/shard_map/ppermute | solution.py:333
  43.5 1.0 sum_of_cores.1
  44.6 6.8 %all-to-all-start.1 = ((f32[8,256,128]{2,1,0:T(8,128)}), f32[8,256,128]{2,1,0:T(8,128)S(1)}, u32[]{:S(2)}, u32[]{:S(2)}) async-start(f32[8,256,128]{2,1,0:T(8,128)} %bitcast), calls=%async_computation.1 | async-start | bytes 2097152 | tf_op jit(solution)/shard_map/all_to_all | solution.py:259
  51.4 2.2 %collective-permute-start.1 = (f32[32,672]{1,0:T(8,128)S(1)}, f32[32,672]{1,0:T(8,128)S(1)}, u32[]{:S(2)}, u32[]{:S(2)}) collective-permute-start(f32[32,672]{1,0:T(8,128)S(1)} %get-tuple-element.21), channel_id=1, source_target_pairs={{0,128},{128,256},{256,384},{384,0},{1,129},{129,257},{257,385},{3... | collective-permute-start | bytes 258056 | tf_op jit(solution)/shard_map/ppermute | solution.py:356
  53.6 3.7 %collective-permute-start.2 = (f32[32,672]{1,0:T(8,128)S(1)}, f32[32,672]{1,0:T(8,128)S(1)}, u32[]{:S(2)}, u32[]{:S(2)}) collective-permute-start(f32[32,672]{1,0:T(8,128)S(1)} %get-tuple-element.22), channel_id=1, source_target_pairs={{0,256},{128,384},{256,0},{384,128},{1,257},{129,385},{257,1},{385... | collective-permute-start | bytes 258056 | tf_op jit(solution)/shard_map/ppermute | solution.py:356
  57.3 2.6 %collective-permute-start.3 = (f32[32,672]{1,0:T(8,128)S(1)}, f32[32,672]{1,0:T(8,128)S(1)}, u32[]{:S(2)}, u32[]{:S(2)}) collective-permute-start(f32[32,672]{1,0:T(8,128)S(1)} %get-tuple-element.23), channel_id=1, source_target_pairs={{0,384},{128,0},{256,128},{384,256},{1,385},{129,1},{257,129},{385... | collective-permute-start | bytes 258056 | tf_op jit(solution)/shard_map/ppermute | solution.py:356
  60.0 0.0 collective-permute-done.1.refs_1_
  60.0 0.5 collective-permute-done.2.refs_2_
  60.5 2.5 %collective-permute-done.3.refs_3_ = f32[32,672]{1,0:T(8,128)S(1)} collective-permute-done((f32[32,672]{1,0:T(8,128)S(1)}, f32[32,672]{1,0:T(8,128)S(1)}, u32[]{:S(2)}, u32[]{:S(2)}) %collective-permute-start.3) | collective-permute-done | bytes 86048 | tf_op jit(solution)/shard_map/ppermute | solution.py:356
  63.0 6.2 %all-to-all-done.1 = f32[8,256,128]{2,1,0:T(8,128)S(1)} async-done(((f32[8,256,128]{2,1,0:T(8,128)}), f32[8,256,128]{2,1,0:T(8,128)S(1)}, u32[]{:S(2)}, u32[]{:S(2)}) %all-to-all-start.1) | async-done | bytes 1048608 | tf_op jit(solution)/shard_map/all_to_all | solution.py:259
  69.2 0.1 reduce_sum.18
  69.3 20.0 %all_to_all.26 = f32[32,8,128]{2,1,0:T(8,128)S(1)} all-to-all(f32[32,8,128]{2,1,0:T(8,128)S(1)} %bitcast.6), channel_id=1, replica_groups={{0,16,32,48,64,80,96,112,128,144,160,176,192,208,224,240,256,272,288,30..., dimensions={0} | all-to-all | bytes 262144 | tf_op jit(solution)/shard_map/all_to_all | solution.py:259
  89.3 15.3 %all_to_all.27 = f32[32,8,128]{2,1,0:T(8,128)S(1)} all-to-all(f32[32,8,128]{2,1,0:T(8,128)S(1)} %broadcast_in_dim.6), channel_id=1, replica_groups={{0,4,8,12,16,20,24,28,32,36,40,44,48,52,56,60,64,68,72,76,80,84,88,92,9..., dimensions={0} | all-to-all | bytes 262144 | tf_op jit(solution)/shard_map/all_to_all | solution.py:259
  104.6 0.1 broadcast_in_dim.15
  104.7 14.8 %all_to_all.28 = f32[8,256,128]{2,1,0:T(8,128)S(1)} all-to-all(f32[8,256,128]{2,1,0:T(8,128)S(1)} %broadcast_in_dim.15), channel_id=1, replica_groups={{0,2,128,130,256,258,384,386},{4,6,132,134,260,262,388,390},{8,10,136,1..., dimensions={0} | all-to-all | bytes 2097152 | tf_op jit(solution)/shard_map/all_to_all | solution.py:259
  119.5 6.5 %collective-permute-start.4 = (f32[2048,128]{1,0:T(8,128)S(1)}, f32[2048,128]{1,0:T(8,128)S(1)}, u32[]{:S(2)}, u32[]{:S(2)}) collective-permute-start(f32[2048,128]{1,0:T(8,128)S(1)} %bitcast.4), channel_id=1, source_target_pairs={{0,1},{1,0},{2,3},{3,2},{4,5},{5,4},{6,7},{7,6},{8,9},{9,8},{10,11... | collective-permute-start | bytes 3145736 | tf_op jit(solution)/shard_map/ppermute | solution.py:372
  126.0 0.9 core_rows.1
  126.9 1.4 %collective-permute-done.4.other_ref = f32[2048,128]{1,0:T(8,128)S(1)} collective-permute-done((f32[2048,128]{1,0:T(8,128)S(1)}, f32[2048,128]{1,0:T(8,128)S(1)}, u32[]{:S(2)}, u32[]{:S(2)}) %collective-permute-start.4) | collective-permute-done | bytes 1048608 | tf_op jit(solution)/shard_map/ppermute | solution.py:372
  128.3 2.0 %mirror.1 = (f32[168,672]{1,0:T(8,128)}, f32[672,672]{1,0:T(8,128)}) custom-call(f32[2048,128]{1,0:T(8,128)S(1)} %bitcast.5, f32[2048,128]{1,0:T(8,128)S(1)} %collective-permute-done.4.other_ref), custom_call_target="tpu_custom_call" | custom-call | tf_op jit(solution)/shard_map/mirror/pallas_call | solution.py:374
  (3 shorter events, 0.1 us)
Async XLA Ops:
  0.6 1.6 %copy-start = (f32[4,168,672]{2,1,0:T(8,128)S(1)}, f32[4,168,672]{2,1,0:T(8,128)}, u32[]{:S(2)}) copy-start(f32[4,168,672]{2,1,0:T(8,128)} %field_ref.1) | copy-start | bytes 5419012
  2.2 0.9 copy-start.1
  33.6 9.9 %collective-permute-start = (f32[2048,128]{1,0:T(8,128)S(1)}, f32[2048,128]{1,0:T(8,128)S(1)}, u32[]{:S(2)}, u32[]{:S(2)}) collective-permute-start(f32[2048,128]{1,0:T(8,128)S(1)} %get-tuple-element.18), channel_id=1, source_target_pairs={{0,1},{1,0},{2,3},{3,2},{4,5},{5,4},{6,7},{7,6},{8,9},{9,8},{10,11... | collective-permute-start | bytes 3145736 | tf_op jit(solution)/shard_map/ppermute | solution.py:333
  44.6 24.6 %all-to-all-start.1 = ((f32[8,256,128]{2,1,0:T(8,128)}), f32[8,256,128]{2,1,0:T(8,128)S(1)}, u32[]{:S(2)}, u32[]{:S(2)}) async-start(f32[8,256,128]{2,1,0:T(8,128)} %bitcast), calls=%async_computation.1 | async-start | bytes 2097152 | tf_op jit(solution)/shard_map/all_to_all | solution.py:259
  51.4 8.5 %collective-permute-start.1 = (f32[32,672]{1,0:T(8,128)S(1)}, f32[32,672]{1,0:T(8,128)S(1)}, u32[]{:S(2)}, u32[]{:S(2)}) collective-permute-start(f32[32,672]{1,0:T(8,128)S(1)} %get-tuple-element.21), channel_id=1, source_target_pairs={{0,128},{128,256},{256,384},{384,0},{1,129},{129,257},{257,385},{3... | collective-permute-start | bytes 258056 | tf_op jit(solution)/shard_map/ppermute | solution.py:356
  53.6 6.9 %collective-permute-start.2 = (f32[32,672]{1,0:T(8,128)S(1)}, f32[32,672]{1,0:T(8,128)S(1)}, u32[]{:S(2)}, u32[]{:S(2)}) collective-permute-start(f32[32,672]{1,0:T(8,128)S(1)} %get-tuple-element.22), channel_id=1, source_target_pairs={{0,256},{128,384},{256,0},{384,128},{1,257},{129,385},{257,1},{385... | collective-permute-start | bytes 258056 | tf_op jit(solution)/shard_map/ppermute | solution.py:356
  57.3 5.7 %collective-permute-start.3 = (f32[32,672]{1,0:T(8,128)S(1)}, f32[32,672]{1,0:T(8,128)S(1)}, u32[]{:S(2)}, u32[]{:S(2)}) collective-permute-start(f32[32,672]{1,0:T(8,128)S(1)} %get-tuple-element.23), channel_id=1, source_target_pairs={{0,384},{128,0},{256,128},{384,256},{1,385},{129,1},{257,129},{385... | collective-permute-start | bytes 258056 | tf_op jit(solution)/shard_map/ppermute | solution.py:356
  119.5 8.8 %collective-permute-start.4 = (f32[2048,128]{1,0:T(8,128)S(1)}, f32[2048,128]{1,0:T(8,128)S(1)}, u32[]{:S(2)}, u32[]{:S(2)}) collective-permute-start(f32[2048,128]{1,0:T(8,128)S(1)} %bitcast.4), channel_id=1, source_target_pairs={{0,1},{1,0},{2,3},{3,2},{4,5},{5,4},{6,7},{7,6},{8,9},{9,8},{10,11... | collective-permute-start | bytes 3145736 | tf_op jit(solution)/shard_map/ppermute | solution.py:372

commit v14 on v11

--- a/solution.py
+++ b/solution.py
@@ -348,12 +348,14 @@
         cost_estimate=cost(rank * second, 8 * rank * second),
         name="core_parts",
     )(core, came)
-    came_core = [core_parts[0]]
-    for step in range(1, gx):
+    came_core = [core_parts[0]] * gx
+    for step in sorted(range(1, gx), key=lambda step: min(step, gx - step)):
         shift = [(i, (i + step) % gx) for i in range(gx)]
-        came_core.append(lax.ppermute(core_parts[step], "x", shift))
+        came_core[step] = lax.ppermute(core_parts[step], "x", shift)
     part = exchange(sums.reshape(near_count, -1, LANES), axes, near)
-    part, *came_core = lax.optimization_barrier((part, *came_core))
+    order = sorted(range(gx), key=lambda step: -min(step, gx - step))
+    part, *tied = lax.optimization_barrier((part, *[came_core[step] for step in order]))
+    came_core = [tied[order.index(step)] for step in range(gx)]
     part = exchange(jnp.sum(part, axis=0).reshape(far_count, -1, LANES), axes, far)
     core_out = pl.pallas_call(
         rows_kernel,

time: 131 us -> 131 us (level)
  no operation moved by 1% of the time
where the time goes in v14:
time: 131 us
  blocking collectives  74.9 us (57%)
  starting transfers between devices  32.7 us (25%)
  waiting for transfers between devices  12.3 us (9%)
  Pallas kernels  7.41 us (6%)
  local copies, waits for them, and re-layouts  2.54 us (2%)
    all_to_all x4, blocking collectives, exchange(): lax.all_to_all(parts, axes, 0, 0, axis_index_groups=groups, tiled=True)  74.9 us
    ppermute x1, starting transfers between devices, local(): other = lax.ppermute(own, 'c', swap)  9.12 us
    ppermute x3, starting transfers between devices, local(): came_core[step] = lax.ppermute(core_parts[step], 'x', shift)  9.12 us
    ppermute x1, starting transfers between devices, local(): came = lax.ppermute(send, 'c', swap)  7.62 us
    all_to_all x1, starting transfers between devices, exchange(): lax.all_to_all(parts, axes, 0, 0, axis_index_groups=groups, tiled=True)  6.83 us
    all_to_all x1, waiting for transfers between devices, exchange(): lax.all_to_all(parts, axes, 0, 0, axis_index_groups=groups, tiled=True)  5.39 us
    pallas_call x1, Pallas kernels, local(): pl.pallas_call(functools.partial(gram_kernel, layout), out_shape=(half_sh...  3.42 us
    ppermute x3, waiting for transfers between devices, local(): came_core[step] = lax.ppermute(core_parts[step], 'x', shift)  3.25 us
  transfers between devices with their start and end apart: 6, of which 5 were waited for; matrix products, arithmetic and copies ran while one was open for 0% of the time, Pallas kernels for 1%

profile of v14, /device:TPU:1, one launch (start us, length us, event | category | flops | bytes accessed | tf_op | source)
XLA Modules:
  0.0 130.6 jit_solution(650421742939247615)
XLA Ops:
  0.6 0.0 copy-start
  0.6 1.6 %copy-done = f32[4,168,672]{2,1,0:T(8,128)S(1)} copy-done((f32[4,168,672]{2,1,0:T(8,128)S(1)}, f32[4,168,672]{2,1,0:T(8,128)}, u32[]{:S(2)}) %copy-start) | copy-done | bytes 1806360
  2.2 0.0 copy-start.1
  2.2 0.9 copy-done.1
  3.1 0.2 dense_blocks.1
  3.3 26.9 %all_to_all.25.dense_ref = f32[4,1056,128]{2,1,0:T(8,128)S(1)} all-to-all(f32[4,1056,128]{2,1,0:T(8,128)S(1)} %dense_blocks.1), channel_id=1, replica_groups=mesh['x'=4,'y'=8,'zh'=4,'zl'=2,'c'=2] {'x'}, dimensions={0} | all-to-all | bytes 4325376 | tf_op jit(solution)/shard_map/all_to_all | solution.py:259
  30.2 3.4 %local_grams.1 = (f32[2048,128]{1,0:T(8,128)S(1)}, f32[2048,128]{1,0:T(8,128)S(1)}, f32[128,672]{1,0:T(8,128)S(1)}) custom-call(f32[4,1056,128]{2,1,0:T(8,128)S(1)} %all_to_all.25.dense_ref), custom_call_target="tpu_custom_call" | custom-call | flops 1517322240 | bytes 5419008 | tf_op jit(solution)/shard_map/local_grams/pallas_call | solution.py:312
  33.6 7.6 %collective-permute-start = (f32[2048,128]{1,0:T(8,128)S(1)}, f32[2048,128]{1,0:T(8,128)S(1)}, u32[]{:S(2)}, u32[]{:S(2)}) collective-permute-start(f32[2048,128]{1,0:T(8,128)S(1)} %get-tuple-element.18), channel_id=1, source_target_pairs={{0,1},{1,0},{2,3},{3,2},{4,5},{5,4},{6,7},{7,6},{8,9},{9,8},{10,11... | collective-permute-start | bytes 3145736 | tf_op jit(solution)/shard_map/ppermute | solution.py:331
  41.2 2.3 %collective-permute-done.came_ref.after_ref = f32[2048,128]{1,0:T(8,128)S(1)} collective-permute-done((f32[2048,128]{1,0:T(8,128)S(1)}, f32[2048,128]{1,0:T(8,128)S(1)}, u32[]{:S(2)}, u32[]{:S(2)}) %collective-permute-start) | collective-permute-done | bytes 1048608 | tf_op jit(solution)/shard_map/ppermute | solution.py:331
  43.5 1.0 sum_of_cores.1
  44.6 6.8 %all-to-all-start.1 = ((f32[8,256,128]{2,1,0:T(8,128)}), f32[8,256,128]{2,1,0:T(8,128)S(1)}, u32[]{:S(2)}, u32[]{:S(2)}) async-start(f32[8,256,128]{2,1,0:T(8,128)} %bitcast), calls=%async_computation.1 | async-start | bytes 2097152 | tf_op jit(solution)/shard_map/all_to_all | solution.py:259
  51.4 2.6 %collective-permute-start.1 = (f32[32,672]{1,0:T(8,128)S(1)}, f32[32,672]{1,0:T(8,128)S(1)}, u32[]{:S(2)}, u32[]{:S(2)}) collective-permute-start(f32[32,672]{1,0:T(8,128)S(1)} %get-tuple-element.20), channel_id=1, source_target_pairs={{0,256},{128,384},{256,0},{384,128},{1,257},{129,385},{257,1},{385... | collective-permute-start | bytes 258056 | tf_op jit(solution)/shard_map/ppermute | solution.py:354
  54.0 2.7 %collective-permute-start.2 = (f32[32,672]{1,0:T(8,128)S(1)}, f32[32,672]{1,0:T(8,128)S(1)}, u32[]{:S(2)}, u32[]{:S(2)}) collective-permute-start(f32[32,672]{1,0:T(8,128)S(1)} %get-tuple-element.21), channel_id=1, source_target_pairs={{0,128},{128,256},{256,384},{384,0},{1,129},{129,257},{257,385},{3... | collective-permute-start | bytes 258056 | tf_op jit(solution)/shard_map/ppermute | solution.py:354
  56.7 3.8 %collective-permute-start.3 = (f32[32,672]{1,0:T(8,128)S(1)}, f32[32,672]{1,0:T(8,128)S(1)}, u32[]{:S(2)}, u32[]{:S(2)}) collective-permute-start(f32[32,672]{1,0:T(8,128)S(1)} %get-tuple-element.22), channel_id=1, source_target_pairs={{0,384},{128,0},{256,128},{384,256},{1,385},{129,1},{257,129},{385... | collective-permute-start | bytes 258056 | tf_op jit(solution)/shard_map/ppermute | solution.py:354
  60.6 0.9 collective-permute-done.1.refs_2_
  61.5 2.4 %collective-permute-done.2.refs_1_ = f32[32,672]{1,0:T(8,128)S(1)} collective-permute-done((f32[32,672]{1,0:T(8,128)S(1)}, f32[32,672]{1,0:T(8,128)S(1)}, u32[]{:S(2)}, u32[]{:S(2)}) %collective-permute-start.2) | collective-permute-done | bytes 86048 | tf_op jit(solution)/shard_map/ppermute | solution.py:354
  63.8 0.0 collective-permute-done.3.refs_3_
  63.8 5.4 %all-to-all-done.1 = f32[8,256,128]{2,1,0:T(8,128)S(1)} async-done(((f32[8,256,128]{2,1,0:T(8,128)}), f32[8,256,128]{2,1,0:T(8,128)S(1)}, u32[]{:S(2)}, u32[]{:S(2)}) %all-to-all-start.1) | async-done | bytes 1048608 | tf_op jit(solution)/shard_map/all_to_all | solution.py:259
  69.2 0.1 reduce_sum.18
  69.3 20.3 %all_to_all.26 = f32[32,8,128]{2,1,0:T(8,128)S(1)} all-to-all(f32[32,8,128]{2,1,0:T(8,128)S(1)} %bitcast.6), channel_id=1, replica_groups={{0,4,8,12,16,20,24,28,32,36,40,44,48,52,56,60,64,68,72,76,80,84,88,92,9..., dimensions={0} | all-to-all | bytes 262144 | tf_op jit(solution)/shard_map/all_to_all | solution.py:259
  89.6 14.8 %all_to_all.27 = f32[32,8,128]{2,1,0:T(8,128)S(1)} all-to-all(f32[32,8,128]{2,1,0:T(8,128)S(1)} %broadcast_in_dim.6), channel_id=1, replica_groups={{0,4,8,12,16,20,24,28,32,36,40,44,48,52,56,60,64,68,72,76,80,84,88,92,9..., dimensions={0} | all-to-all | bytes 262144 | tf_op jit(solution)/shard_map/all_to_all | solution.py:259
  104.4 0.1 broadcast_in_dim.15
  104.5 12.9 %all_to_all.28 = f32[8,256,128]{2,1,0:T(8,128)S(1)} all-to-all(f32[8,256,128]{2,1,0:T(8,128)S(1)} %broadcast_in_dim.15), channel_id=1, replica_groups={{0,2,128,130,256,258,384,386},{4,6,132,134,260,262,388,390},{8,10,136,1..., dimensions={0} | all-to-all | bytes 2097152 | tf_op jit(solution)/shard_map/all_to_all | solution.py:259
  117.3 9.1 %collective-permute-start.4 = (f32[2048,128]{1,0:T(8,128)S(1)}, f32[2048,128]{1,0:T(8,128)S(1)}, u32[]{:S(2)}, u32[]{:S(2)}) collective-permute-start(f32[2048,128]{1,0:T(8,128)S(1)} %bitcast.4), channel_id=1, source_target_pairs={{0,1},{1,0},{2,3},{3,2},{4,5},{5,4},{6,7},{7,6},{8,9},{9,8},{10,11... | collective-permute-start | bytes 3145736 | tf_op jit(solution)/shard_map/ppermute | solution.py:372
  126.5 0.9 core_rows.1
  127.3 1.4 %collective-permute-done.4.other_ref = f32[2048,128]{1,0:T(8,128)S(1)} collective-permute-done((f32[2048,128]{1,0:T(8,128)S(1)}, f32[2048,128]{1,0:T(8,128)S(1)}, u32[]{:S(2)}, u32[]{:S(2)}) %collective-permute-start.4) | collective-permute-done | bytes 1048608 | tf_op jit(solution)/shard_map/ppermute | solution.py:372
  128.7 1.9 %mirror.1 = (f32[168,672]{1,0:T(8,128)}, f32[672,672]{1,0:T(8,128)}) custom-call(f32[2048,128]{1,0:T(8,128)S(1)} %bitcast.5, f32[2048,128]{1,0:T(8,128)S(1)} %collective-permute-done.4.other_ref), custom_call_target="tpu_custom_call" | custom-call | tf_op jit(solution)/shard_map/mirror/pallas_call | solution.py:374
  (3 shorter events, 0.1 us)
Async XLA Ops:
  0.6 1.6 %copy-start = (f32[4,168,672]{2,1,0:T(8,128)S(1)}, f32[4,168,672]{2,1,0:T(8,128)}, u32[]{:S(2)}) copy-start(f32[4,168,672]{2,1,0:T(8,128)} %field_ref.1) | copy-start | bytes 5419012
  2.2 0.9 copy-start.1
  33.6 9.9 %collective-permute-start = (f32[2048,128]{1,0:T(8,128)S(1)}, f32[2048,128]{1,0:T(8,128)S(1)}, u32[]{:S(2)}, u32[]{:S(2)}) collective-permute-start(f32[2048,128]{1,0:T(8,128)S(1)} %get-tuple-element.18), channel_id=1, source_target_pairs={{0,1},{1,0},{2,3},{3,2},{4,5},{5,4},{6,7},{7,6},{8,9},{9,8},{10,11... | collective-permute-start | bytes 3145736 | tf_op jit(solution)/shard_map/ppermute | solution.py:331
  44.6 24.6 %all-to-all-start.1 = ((f32[8,256,128]{2,1,0:T(8,128)}), f32[8,256,128]{2,1,0:T(8,128)S(1)}, u32[]{:S(2)}, u32[]{:S(2)}) async-start(f32[8,256,128]{2,1,0:T(8,128)} %bitcast), calls=%async_computation.1 | async-start | bytes 2097152 | tf_op jit(solution)/shard_map/all_to_all | solution.py:259
  51.4 10.0 %collective-permute-start.1 = (f32[32,672]{1,0:T(8,128)S(1)}, f32[32,672]{1,0:T(8,128)S(1)}, u32[]{:S(2)}, u32[]{:S(2)}) collective-permute-start(f32[32,672]{1,0:T(8,128)S(1)} %get-tuple-element.20), channel_id=1, source_target_pairs={{0,256},{128,384},{256,0},{384,128},{1,257},{129,385},{257,1},{385... | collective-permute-start | bytes 258056 | tf_op jit(solution)/shard_map/ppermute | solution.py:354
  54.0 9.8 %collective-permute-start.2 = (f32[32,672]{1,0:T(8,128)S(1)}, f32[32,672]{1,0:T(8,128)S(1)}, u32[]{:S(2)}, u32[]{:S(2)}) collective-permute-start(f32[32,672]{1,0:T(8,128)S(1)} %get-tuple-element.21), channel_id=1, source_target_pairs={{0,128},{128,256},{256,384},{384,0},{1,129},{129,257},{257,385},{3... | collective-permute-start | bytes 258056 | tf_op jit(solution)/shard_map/ppermute | solution.py:354
  56.7 7.1 %collective-permute-start.3 = (f32[32,672]{1,0:T(8,128)S(1)}, f32[32,672]{1,0:T(8,128)S(1)}, u32[]{:S(2)}, u32[]{:S(2)}) collective-permute-start(f32[32,672]{1,0:T(8,128)S(1)} %get-tuple-element.22), channel_id=1, source_target_pairs={{0,384},{128,0},{256,128},{384,256},{1,385},{129,1},{257,129},{385... | collective-permute-start | bytes 258056 | tf_op jit(solution)/shard_map/ppermute | solution.py:354
  117.3 11.4 %collective-permute-start.4 = (f32[2048,128]{1,0:T(8,128)S(1)}, f32[2048,128]{1,0:T(8,128)S(1)}, u32[]{:S(2)}, u32[]{:S(2)}) collective-permute-start(f32[2048,128]{1,0:T(8,128)S(1)} %bitcast.4), channel_id=1, source_target_pairs={{0,1},{1,0},{2,3},{3,2},{4,5},{5,4},{6,7},{7,6},{8,9},{9,8},{10,11... | collective-permute-start | bytes 3145736 | tf_op jit(solution)/shard_map/ppermute | solution.py:372
